TPU v7x, 32 devices: a whole 2x2x4 slice. The times are simulated.
32 devices in a mesh: seq: 8 (over z, x), fsdp: 4 (over y, core).
Axes of the slice: x: 2, y: 2, z: 4, core: 2. Of those that a mesh axis runs over, the one named last changes fastest.
Arguments:
- tokens: bfloat16 [4, 2048, 1024], P('fsdp', 'seq'), may hold values from -6 to 6
- cotangent: bfloat16 [4, 2048, 1024], P('fsdp', 'seq'), may hold values from -6 to 6
- offsets: int32 [4, 16], P('fsdp'), may hold values from 0 to 2047, as said below
- gain_in: bfloat16 [1024], P('fsdp'), may hold values from 0.5 to 1.5
- w_query: bfloat16 [1024, 1024], P('fsdp'), may hold values from -0.1875 to 0.1875
- w_key: bfloat16 [1024, 2048], P('fsdp'), may hold values from -0.1875 to 0.1875
- w_value: bfloat16 [1024, 2048], P('fsdp'), may hold values from -0.1875 to 0.1875
- w_beta: bfloat16 [1024, 16], P('fsdp'), may hold values from -0.1875 to 0.1875
- w_decay: bfloat16 [1024, 8], P('fsdp'), may hold values from -0.1875 to 0.1875
- w_outgate: bfloat16 [1024, 1024], P('fsdp'), may hold values from -0.1875 to 0.1875
- conv_query: bfloat16 [4, 1024], P(None, 'fsdp'), may hold values from -3 to 3
- conv_key: bfloat16 [4, 2048], P(None, 'fsdp'), may hold values from -3 to 3
- conv_value: bfloat16 [4, 2048], P(None, 'fsdp'), may hold values from -3 to 3
- decay_scale: float32 [8], replicated, may hold values from 0.001953125 to 0.0078125
- gain_head: bfloat16 [128], P('fsdp'), may hold values from 0.5 to 1.5
- w_out: bfloat16 [1024, 1024], P('fsdp'), may hold values from -0.375 to 0.375
- gain_ffn: bfloat16 [1024], P('fsdp'), may hold values from 0.5 to 1.5
- w_gate: bfloat16 [1024, 2816], P('fsdp'), may hold values from -0.1875 to 0.1875
- w_up: bfloat16 [1024, 2816], P('fsdp'), may hold values from -0.1875 to 0.1875
- w_down: bfloat16 [2816, 1024], P('fsdp'), may hold values from -0.109375 to 0.109375
Outputs:
- layer_out: bfloat16 [4, 2048, 1024], P('fsdp', 'seq')
- input_grad: bfloat16 [4, 2048, 1024], P('fsdp', 'seq')
- grad_gain_in: float32 [1024], P('fsdp')
- grad_query: float32 [1024, 1024], P('fsdp')
- grad_key: float32 [1024, 2048], P('fsdp')
- grad_value: float32 [1024, 2048], P('fsdp')
- grad_beta: float32 [1024, 16], P('fsdp')
- grad_decay: float32 [1024, 8], P('fsdp')
- grad_outgate: float32 [1024, 1024], P('fsdp')
- grad_conv_query: float32 [4, 1024], P(None, 'fsdp')
- grad_conv_key: float32 [4, 2048], P(None, 'fsdp')
- grad_conv_value: float32 [4, 2048], P(None, 'fsdp')
- grad_decay_scale: float32 [8], replicated
- grad_gain_head: float32 [128], P('fsdp')
- grad_out: float32 [1024, 1024], P('fsdp')
- grad_gain_ffn: float32 [1024], P('fsdp')
- grad_gate: float32 [1024, 2816], P('fsdp')
- grad_up: float32 [1024, 2816], P('fsdp')
- grad_down: float32 [2816, 1024], P('fsdp')
Inputs may be any that keep to these rules, and one draw needn't show every extreme that they name: offsets[s, 0] is 0 and each row rises strictly; offsets[s, j] for 1 <= j <= 7 lie below 128, the later ones at 1920 or beyond.
All inputs are finite; a program needn't handle non-finite values.
Results may differ from a plain program's by a relative error of at most 0.035.
Values may be sent and summed in bfloat16 or wider, within the bound.
No kernel may reach another device: no remote copies, remote signals or barrier semaphores. Data moves between devices by JAX's collectives and lax.ppermute only.
A program may use at most 320 MiB of HBM per device.

v0:
```python
import jax
import jax.numpy as jnp
from jax import lax
from jax.sharding import PartitionSpec as P

SPAN = 64


EPSILON = 1e-06
EXACT = lax.Precision.HIGHEST


def passed_along(value, axis, by):
    count = lax.axis_size(axis)
    pairs = [(i, i + by) for i in range(count) if 0 <= i + by < count]
    return lax.ppermute(value, axis, pairs)


def prefix(value, axis, join, neutral):
    place = lax.axis_index(axis)
    gathered = jax.tree.map(
        lambda a, kind: lax.all_gather(a.astype(kind), axis), value, (jnp.bfloat16, jnp.bfloat16)
    )
    state = jax.tree.map(lambda a, e: jnp.zeros_like(a) + jnp.asarray(e, a.dtype), value, neutral)

    def one(hop, state):
        return join(
            state,
            jax.tree.map(
                lambda a, own: lax.dynamic_index_in_dim(a, hop, 0, False).astype(own.dtype),
                gathered,
                value,
            ),
        )

    return lax.fori_loop(0, place, one, state)


def prefix_2(value, axis, combine, identity):
    count, position = (lax.axis_size(axis), lax.axis_index(axis))
    everything = jax.tree.map(
        lambda part, kind: lax.all_gather(part.astype(kind), axis),
        value,
        jax.tree.map(lambda a: jnp.bfloat16 if a.dtype == jnp.float32 else a.dtype, value),
    )
    start = jax.tree.map(
        lambda part, zero: jnp.broadcast_to(jnp.asarray(zero, part.dtype), part.shape),
        value,
        identity,
    )

    def hop(k, before):
        at = count - 1 - k
        reached = at > position
        new = combine(
            before, jax.tree.map(lambda part, own: part[at].astype(own.dtype), everything, value)
        )
        return jax.tree.map(lambda a, b: jnp.where(reached, a, b), new, before)

    return lax.fori_loop(0, count, hop, start)


def rms_scale(values, gain_vec):
    return (
        values * lax.rsqrt(jnp.mean(values * values, axis=-1, keepdims=True) + EPSILON) * gain_vec
    )


def unit_rows(values):
    return values * lax.rsqrt(jnp.sum(values * values, axis=-1, keepdims=True) + EPSILON)


def doc_marks(doc_offsets, position, tap_count):
    doc_count = doc_offsets.shape[0]
    seg_ids = jnp.sum((doc_offsets[None, 1:] <= position[:, None]).astype(jnp.int32), axis=1)
    member = seg_ids[:, None] == jnp.arange(doc_count, dtype=jnp.int32)[None, :]
    doc_begin = jnp.sum(jnp.where(member, doc_offsets[None, :], 0), axis=1)
    starts = (position == doc_begin).astype(jnp.float32)
    lag_ids = jnp.arange(tap_count, dtype=jnp.int32)
    tap_valid = (position[:, None] - lag_ids[None, :] >= doc_begin[:, None]).astype(jnp.float32)
    return (starts, tap_valid)


def causal_conv(inputs, edge_rows, weights, tap_valid):
    tap_count = weights.shape[0]
    length = inputs.shape[0]
    padded = jnp.concatenate([edge_rows, inputs], axis=0)
    result = jnp.zeros_like(inputs)
    for lag_step in range(tap_count):
        begin_row = tap_count - 1 - lag_step
        result = (
            result
            + weights[lag_step][None, :]
            * padded[begin_row : begin_row + length]
            * tap_valid[:, lag_step : lag_step + 1]
        )
    return result


def mixer_inputs(
    pre_query,
    pre_key,
    pre_value,
    edge_query,
    edge_key,
    edge_value,
    conv_query,
    conv_key,
    conv_value,
    pre_beta,
    pre_decay,
    rate_scale,
    tap_valid,
):
    tokens_here = pre_query.shape[0]
    head_count = rate_scale.shape[0]
    model_width = pre_query.shape[1]
    head_dim = model_width // head_count
    step_count = pre_key.shape[1] // model_width
    queries = unit_rows(
        jax.nn.silu(causal_conv(pre_query, edge_query, conv_query, tap_valid)).reshape(
            tokens_here, head_count, head_dim
        )
    )
    key_rows = unit_rows(
        jax.nn.silu(causal_conv(pre_key, edge_key, conv_key, tap_valid)).reshape(
            tokens_here, step_count, head_count, head_dim
        )
    )
    value_rows = jax.nn.silu(causal_conv(pre_value, edge_value, conv_value, tap_valid)).reshape(
        tokens_here, step_count, head_count, head_dim
    )
    beta_rows = jax.nn.sigmoid(pre_beta).reshape(tokens_here, step_count, head_count)
    log_decay = -rate_scale[None, :] * jax.nn.softplus(pre_decay)
    return (queries, key_rows, value_rows, beta_rows, log_decay)


def delta_block(carry_state, block_data):
    queries, key_rows, value_rows, beta_rows, log_decay, starts = block_data
    block_len, step_count, head_count, key_dim = key_rows.shape
    value_dim = value_rows.shape[-1]
    row_count = block_len * step_count
    head_keys = jnp.transpose(key_rows, (2, 0, 1, 3)).reshape(head_count, row_count, key_dim)
    head_values = jnp.transpose(value_rows, (2, 0, 1, 3)).reshape(head_count, row_count, value_dim)
    head_beta = jnp.transpose(beta_rows, (2, 0, 1)).reshape(head_count, row_count)
    step_log = jnp.concatenate(
        [log_decay[:, None, :], jnp.zeros((block_len, step_count - 1, head_count), jnp.float32)],
        axis=1,
    )
    log_total = jnp.cumsum(
        jnp.transpose(step_log, (2, 0, 1)).reshape(head_count, row_count), axis=1
    )
    row_starts = jnp.concatenate(
        [starts[:, None], jnp.zeros((block_len, step_count - 1), jnp.float32)], axis=1
    ).reshape(row_count)
    resets = jnp.cumsum(row_starts)
    row_order = jnp.arange(row_count)
    same_doc = resets[:, None] == resets[None, :]
    lower_mask = ((row_order[:, None] >= row_order[None, :]) & same_doc)[None]
    strict = ((row_order[:, None] > row_order[None, :]) & same_doc)[None]
    spread = log_total[:, :, None] - log_total[:, None, :]
    decay_mask = jnp.where(lower_mask, jnp.exp(jnp.where(lower_mask, spread, 0.0)), 0.0)
    key_inner = jnp.einsum("hrd,hjd->hrj", head_keys, head_keys, precision=EXACT)
    system = jnp.eye(row_count, dtype=jnp.float32)[None] + jnp.where(
        strict, head_beta[:, :, None] * decay_mask * key_inner, 0.0
    )
    carry_in = jnp.exp(log_total) * (resets == 0.0).astype(jnp.float32)[None, :]
    recall = jnp.einsum("hrd,hdw->hrw", head_keys, carry_state, precision=EXACT)
    target = head_beta[:, :, None] * (head_values - carry_in[:, :, None] * recall)
    update = jax.scipy.linalg.solve_triangular(system, target, lower=True, unit_diagonal=True)
    head_query = jnp.transpose(queries, (1, 0, 2))
    scores = (
        jnp.einsum("hcd,hjd->hcj", head_query, head_keys, precision=EXACT)
        * decay_mask[:, step_count - 1 :: step_count, :]
    )
    outputs = jnp.einsum("hcj,hjw->hcw", scores, update, precision=EXACT)
    outputs = outputs + carry_in[:, step_count - 1 :: step_count, None] * jnp.einsum(
        "hcd,hdw->hcw", head_query, carry_state, precision=EXACT
    )
    new_state = carry_in[:, -1, None, None] * carry_state + jnp.einsum(
        "hrd,hrw->hdw", head_keys * decay_mask[:, -1, :, None], update, precision=EXACT
    )
    return (new_state, jnp.transpose(outputs, (1, 0, 2)))


def delta_scan(queries, key_rows, value_rows, beta_rows, log_decay, starts, carry_state):
    tokens_here = queries.shape[0]
    block_total = tokens_here // SPAN

    def block_split(values):
        return values.reshape((block_total, SPAN) + values.shape[1:])

    last_state, outputs = lax.scan(
        jax.checkpoint(delta_block),
        carry_state,
        (
            block_split(queries),
            block_split(key_rows),
            block_split(value_rows),
            block_split(beta_rows),
            block_split(log_decay),
            block_split(starts),
        ),
    )
    return (outputs.reshape((tokens_here,) + outputs.shape[2:]), last_state)


def gated_out(mixed_heads, gate_pre, gain_vec):
    tokens_here, head_count, head_dim = mixed_heads.shape
    gated_rows = rms_scale(mixed_heads, gain_vec) * jax.nn.silu(
        gate_pre.reshape(tokens_here, head_count, head_dim)
    )
    return gated_rows.reshape(tokens_here, head_count * head_dim)


def dot_plain(left, right):
    return jnp.dot(left, right, preferred_element_type=jnp.float32)


def dot_left(left, right):
    return lax.dot_general(
        left, right, (((0,), (0,)), ((), ())), preferred_element_type=jnp.float32
    )


def dot_right(left, right):
    return lax.dot_general(
        left, right, (((1,), (1,)), ((), ())), preferred_element_type=jnp.float32
    )


def compose(earlier, later):
    first_map, first_add = earlier
    second_map, second_add = later
    joined_map = jnp.einsum("hij,hjk->hik", second_map, first_map, precision=EXACT)
    joined_add = jnp.einsum("hij,hjk->hik", second_map, first_add, precision=EXACT) + second_add
    return (joined_map, joined_add)


def per_device(
    tokens,
    cotangent,
    offsets,
    gain_in,
    w_query,
    w_key,
    w_value,
    w_beta,
    w_decay,
    w_outgate,
    conv_query,
    conv_key,
    conv_value,
    decay_scale,
    gain_head,
    w_out,
    gain_ffn,
    w_gate,
    w_up,
    w_down,
):
    rows_here = tokens.shape[1]
    head_count = decay_scale.shape[0]
    tap_count = conv_query.shape[0]
    inputs = tokens[0].astype(jnp.float32)
    position = lax.axis_index("seq") * rows_here + jnp.arange(rows_here, dtype=jnp.int32)
    starts, tap_valid = doc_marks(offsets[0], position, tap_count)
    (
        full_gain_in,
        full_query,
        full_key,
        full_value,
        full_beta,
        full_decay,
        full_outgate,
        full_conv_q,
        full_conv_k,
        full_conv_v,
        full_gain_head,
        full_out,
    ) = (
        lax.all_gather(gain_in, "fsdp", axis=0, tiled=True),
        lax.all_gather(w_query, "fsdp", axis=0, tiled=True),
        lax.all_gather(w_key, "fsdp", axis=0, tiled=True),
        lax.all_gather(w_value, "fsdp", axis=0, tiled=True),
        lax.all_gather(w_beta, "fsdp", axis=0, tiled=True),
        lax.all_gather(w_decay, "fsdp", axis=0, tiled=True),
        lax.all_gather(w_outgate, "fsdp", axis=0, tiled=True),
        lax.all_gather(conv_query, "fsdp", axis=1, tiled=True),
        lax.all_gather(conv_key, "fsdp", axis=1, tiled=True),
        lax.all_gather(conv_value, "fsdp", axis=1, tiled=True),
        lax.all_gather(gain_head, "fsdp", axis=0, tiled=True),
        lax.all_gather(w_out, "fsdp", axis=0, tiled=True),
    )
    model_width = full_query.shape[0]
    head_dim = model_width // head_count
    normed_in, pull_in = jax.vjp(rms_scale, inputs, full_gain_in.astype(jnp.float32))
    normed_low = normed_in.astype(jnp.bfloat16)
    proj_query = dot_plain(normed_low, full_query).astype(jnp.bfloat16)
    proj_key = dot_plain(normed_low, full_key).astype(jnp.bfloat16)
    proj_value = dot_plain(normed_low, full_value).astype(jnp.bfloat16)
    proj_beta = dot_plain(normed_low, full_beta)
    proj_decay = dot_plain(normed_low, full_decay)
    proj_gate = dot_plain(normed_low, full_outgate)
    edge_start = rows_here - (tap_count - 1)
    edge_query, edge_key, edge_value = passed_along(
        (proj_query[edge_start:], proj_key[edge_start:], proj_value[edge_start:]), "seq", 1
    )

    def front_piece(
        pre_query,
        pre_key,
        pre_value,
        prior_query,
        prior_key,
        prior_value,
        taps_query,
        taps_key,
        taps_value,
        pre_beta,
        pre_decay,
        rate_scale,
    ):
        return mixer_inputs(
            pre_query,
            pre_key,
            pre_value,
            prior_query,
            prior_key,
            prior_value,
            taps_query,
            taps_key,
            taps_value,
            pre_beta,
            pre_decay,
            rate_scale,
            tap_valid,
        )

    front_values, pull_front = jax.vjp(
        front_piece,
        proj_query.astype(jnp.float32),
        proj_key.astype(jnp.float32),
        proj_value.astype(jnp.float32),
        edge_query.astype(jnp.float32),
        edge_key.astype(jnp.float32),
        edge_value.astype(jnp.float32),
        full_conv_q.astype(jnp.float32),
        full_conv_k.astype(jnp.float32),
        full_conv_v.astype(jnp.float32),
        proj_beta,
        proj_decay,
        decay_scale,
    )
    queries, key_rows, value_rows, beta_rows, log_decay = front_values
    eye_block = jnp.broadcast_to(
        jnp.eye(head_dim, dtype=jnp.float32), (head_count, head_dim, head_dim)
    )
    zero_block = jnp.zeros((head_count, head_dim, head_dim), jnp.float32)

    def summary(queries_in, keys_in, values_in, beta_in, decay_in):
        padded_values = jnp.concatenate(
            [values_in, jnp.zeros(values_in.shape[:-1] + (head_dim,), jnp.float32)], axis=-1
        )
        start_state = jnp.concatenate([zero_block, eye_block], axis=-1)
        return delta_scan(
            queries_in, keys_in, padded_values, beta_in, decay_in, starts, start_state
        )

    (aug_out, aug_state), pull_scan = jax.vjp(
        summary, queries, key_rows, value_rows, beta_rows, log_decay
    )
    reach_rows = aug_out[..., head_dim:]
    local_add = aug_state[..., :head_dim]
    local_map = aug_state[..., head_dim:]
    prior_map, state_in = prefix((local_map, local_add), "seq", compose, (eye_block, zero_block))
    mixed_heads, unused_state = delta_scan(
        queries, key_rows, value_rows, beta_rows, log_decay, starts, state_in
    )
    gated_rows, pull_gate = jax.vjp(
        gated_out, mixed_heads, proj_gate, full_gain_head.astype(jnp.float32)
    )
    gated_low = gated_rows.astype(jnp.bfloat16)
    mixer_res = inputs + dot_plain(gated_low, full_out)
    full_gain_ffn, full_gate, full_up, full_down = (
        lax.all_gather(gain_ffn, "fsdp", axis=0, tiled=True),
        lax.all_gather(w_gate, "fsdp", axis=0, tiled=True),
        lax.all_gather(w_up, "fsdp", axis=0, tiled=True),
        lax.all_gather(w_down, "fsdp", axis=0, tiled=True),
    )
    normed_mid, pull_mid = jax.vjp(rms_scale, mixer_res, full_gain_ffn.astype(jnp.float32))
    mid_low = normed_mid.astype(jnp.bfloat16)
    gate_pre = dot_plain(mid_low, full_gate)
    up_pre = dot_plain(mid_low, full_up)
    gate_act = jax.nn.silu(gate_pre)
    hidden = (gate_act * up_pre).astype(jnp.bfloat16)
    layer_out = (mixer_res + dot_plain(hidden, full_down)).astype(jnp.bfloat16)
    grad_low = cotangent[0]
    grad_down = dot_left(hidden, grad_low)
    grad_hidden = dot_right(grad_low, full_down)
    sigmoid_gate = jax.nn.sigmoid(gate_pre)
    grad_gate_pre = (
        grad_hidden * up_pre * sigmoid_gate * (1.0 + gate_pre * (1.0 - sigmoid_gate))
    ).astype(jnp.bfloat16)
    grad_up_pre = (grad_hidden * gate_act).astype(jnp.bfloat16)
    grad_gate = dot_left(mid_low, grad_gate_pre)
    grad_up = dot_left(mid_low, grad_up_pre)
    grad_mid = dot_right(grad_gate_pre, full_gate) + dot_right(grad_up_pre, full_up)
    mid_back, grad_gain_ffn = pull_mid(grad_mid)
    grad_res = grad_low.astype(jnp.float32) + mid_back
    res_low = grad_res.astype(jnp.bfloat16)
    grad_out = dot_left(gated_low, res_low)
    grad_gated = dot_right(res_low, full_out)
    grad_mixed, grad_pre_gate, grad_gain_head = pull_gate(grad_gated)
    gate_in_low = grad_pre_gate.astype(jnp.bfloat16)
    grad_reach = jnp.einsum("thw,hdw->thd", grad_mixed, state_in, precision=EXACT)
    grad_state_in = jnp.einsum("thd,thw->hdw", reach_rows, grad_mixed, precision=EXACT)
    map_back = jnp.swapaxes(local_map, 1, 2)
    unused_map, grad_state_out = prefix_2(
        (map_back, grad_state_in), "seq", compose, (eye_block, zero_block)
    )
    grad_map = jnp.einsum("hdw,hew->hde", grad_state_out, state_in, precision=EXACT)
    grad_aug_state = jnp.concatenate([grad_state_out, grad_map], axis=-1)
    grad_aug_out = jnp.concatenate([grad_mixed, grad_reach], axis=-1)
    grad_queries, grad_keys, grad_values, grad_beta_rows, grad_log = pull_scan(
        (grad_aug_out, grad_aug_state)
    )
    (
        grad_pre_q,
        grad_pre_k,
        grad_pre_v,
        grad_edge_q,
        grad_edge_k,
        grad_edge_v,
        grad_conv_q,
        grad_conv_k,
        grad_conv_v,
        grad_pre_beta,
        grad_pre_decay,
        grad_rate,
    ) = pull_front((grad_queries, grad_keys, grad_values, grad_beta_rows, grad_log))
    back_query, back_key, back_value = (
        passed_along(grad_edge_q.astype(jnp.bfloat16), "seq", -1).astype(grad_edge_q.dtype),
        passed_along(grad_edge_k.astype(jnp.bfloat16), "seq", -1).astype(grad_edge_k.dtype),
        passed_along(grad_edge_v.astype(jnp.bfloat16), "seq", -1).astype(grad_edge_v.dtype),
    )
    tail_pad = ((edge_start, 0), (0, 0))
    query_low = (grad_pre_q + jnp.pad(back_query, tail_pad)).astype(jnp.bfloat16)
    key_low = (grad_pre_k + jnp.pad(back_key, tail_pad)).astype(jnp.bfloat16)
    value_low = (grad_pre_v + jnp.pad(back_value, tail_pad)).astype(jnp.bfloat16)
    beta_low = grad_pre_beta.astype(jnp.bfloat16)
    decay_low = grad_pre_decay.astype(jnp.bfloat16)
    grad_query = dot_left(normed_low, query_low)
    grad_key = dot_left(normed_low, key_low)
    grad_value = dot_left(normed_low, value_low)
    grad_beta = dot_left(normed_low, beta_low)
    grad_decay = dot_left(normed_low, decay_low)
    grad_outgate = dot_left(normed_low, gate_in_low)
    grad_norm_in = (
        dot_right(query_low, full_query)
        + dot_right(key_low, full_key)
        + dot_right(value_low, full_value)
    )
    grad_norm_in = (
        grad_norm_in
        + dot_right(beta_low, full_beta)
        + dot_right(decay_low, full_decay)
        + dot_right(gate_in_low, full_outgate)
    )
    in_back, grad_gain_in = pull_in(grad_norm_in)
    input_grad = (grad_res + in_back).astype(jnp.bfloat16)
    rate_sum = lax.psum(grad_rate, ("seq", "fsdp"))
    all_parts = (
        lax.psum_scatter(
            grad_gain_in.astype(jnp.bfloat16), "fsdp", scatter_dimension=0, tiled=True
        ).astype(jnp.float32),
        lax.psum_scatter(
            grad_query.astype(jnp.bfloat16), "fsdp", scatter_dimension=0, tiled=True
        ).astype(jnp.float32),
        lax.psum_scatter(
            grad_key.astype(jnp.bfloat16), "fsdp", scatter_dimension=0, tiled=True
        ).astype(jnp.float32),
        lax.psum_scatter(
            grad_value.astype(jnp.bfloat16), "fsdp", scatter_dimension=0, tiled=True
        ).astype(jnp.float32),
        lax.psum_scatter(
            grad_beta.astype(jnp.bfloat16), "fsdp", scatter_dimension=0, tiled=True
        ).astype(jnp.float32),
        lax.psum_scatter(
            grad_decay.astype(jnp.bfloat16), "fsdp", scatter_dimension=0, tiled=True
        ).astype(jnp.float32),
        lax.psum_scatter(
            grad_outgate.astype(jnp.bfloat16), "fsdp", scatter_dimension=0, tiled=True
        ).astype(jnp.float32),
        lax.psum_scatter(
            grad_conv_q.astype(jnp.bfloat16), "fsdp", scatter_dimension=1, tiled=True
        ).astype(jnp.float32),
        lax.psum_scatter(
            grad_conv_k.astype(jnp.bfloat16), "fsdp", scatter_dimension=1, tiled=True
        ).astype(jnp.float32),
        lax.psum_scatter(
            grad_conv_v.astype(jnp.bfloat16), "fsdp", scatter_dimension=1, tiled=True
        ).astype(jnp.float32),
        lax.psum_scatter(
            grad_gain_head.astype(jnp.bfloat16), "fsdp", scatter_dimension=0, tiled=True
        ).astype(jnp.float32),
        lax.psum_scatter(
            grad_out.astype(jnp.bfloat16), "fsdp", scatter_dimension=0, tiled=True
        ).astype(jnp.float32),
        lax.psum_scatter(
            grad_gain_ffn.astype(jnp.bfloat16), "fsdp", scatter_dimension=0, tiled=True
        ).astype(jnp.float32),
        lax.psum_scatter(
            grad_gate.astype(jnp.bfloat16), "fsdp", scatter_dimension=0, tiled=True
        ).astype(jnp.float32),
        lax.psum_scatter(
            grad_up.astype(jnp.bfloat16), "fsdp", scatter_dimension=0, tiled=True
        ).astype(jnp.float32),
        lax.psum_scatter(
            grad_down.astype(jnp.bfloat16), "fsdp", scatter_dimension=0, tiled=True
        ).astype(jnp.float32),
    )
    shard_list = (
        lax.psum(all_parts[0].astype(jnp.bfloat16), "seq").astype(jnp.float32),
        lax.psum(all_parts[1].astype(jnp.bfloat16), "seq").astype(jnp.float32),
        lax.psum(all_parts[2].astype(jnp.bfloat16), "seq").astype(jnp.float32),
        lax.psum(all_parts[3].astype(jnp.bfloat16), "seq").astype(jnp.float32),
        lax.psum(all_parts[4].astype(jnp.bfloat16), "seq").astype(jnp.float32),
        lax.psum(all_parts[5].astype(jnp.bfloat16), "seq").astype(jnp.float32),
        lax.psum(all_parts[6].astype(jnp.bfloat16), "seq").astype(jnp.float32),
        lax.psum(all_parts[7].astype(jnp.bfloat16), "seq").astype(jnp.float32),
        lax.psum(all_parts[8].astype(jnp.bfloat16), "seq").astype(jnp.float32),
        lax.psum(all_parts[9].astype(jnp.bfloat16), "seq").astype(jnp.float32),
        lax.psum(all_parts[10].astype(jnp.bfloat16), "seq").astype(jnp.float32),
        lax.psum(all_parts[11].astype(jnp.bfloat16), "seq").astype(jnp.float32),
        lax.psum(all_parts[12].astype(jnp.bfloat16), "seq").astype(jnp.float32),
        lax.psum(all_parts[13].astype(jnp.bfloat16), "seq").astype(jnp.float32),
        lax.psum(all_parts[14].astype(jnp.bfloat16), "seq").astype(jnp.float32),
        lax.psum(all_parts[15].astype(jnp.bfloat16), "seq").astype(jnp.float32),
    )
    return (
        layer_out[None],
        input_grad[None],
        shard_list[0],
        shard_list[1],
        shard_list[2],
        shard_list[3],
        shard_list[4],
        shard_list[5],
        shard_list[6],
        shard_list[7],
        shard_list[8],
        shard_list[9],
        rate_sum,
        shard_list[10],
        shard_list[11],
        shard_list[12],
        shard_list[13],
        shard_list[14],
        shard_list[15],
    )


def solution(mesh):
    return jax.shard_map(
        per_device,
        mesh=mesh,
        in_specs=(
            P("fsdp", "seq", None),
            P("fsdp", "seq", None),
            P("fsdp", None),
            P("fsdp"),
            P("fsdp", None),
            P("fsdp", None),
            P("fsdp", None),
            P("fsdp", None),
            P("fsdp", None),
            P("fsdp", None),
            P(None, "fsdp"),
            P(None, "fsdp"),
            P(None, "fsdp"),
            P(),
            P("fsdp"),
            P("fsdp", None),
            P("fsdp"),
            P("fsdp", None),
            P("fsdp", None),
            P("fsdp", None),
        ),
        out_specs=(
            P("fsdp", "seq", None),
            P("fsdp", "seq", None),
            P("fsdp"),
            P("fsdp", None),
            P("fsdp", None),
            P("fsdp", None),
            P("fsdp", None),
            P("fsdp", None),
            P("fsdp", None),
            P(None, "fsdp"),
            P(None, "fsdp"),
            P(None, "fsdp"),
            P(),
            P("fsdp"),
            P("fsdp", None),
            P("fsdp"),
            P("fsdp", None),
            P("fsdp", None),
            P("fsdp", None),
        ),
        check_vma=False,
    )
```

profile of v0, /device:TPU:0, one launch (start us, length us, event | category | flops | bytes accessed | tf_op | source)
XLA Modules:
  0.0 2535.1 jit_solution(3326190909456093647)
XLA Ops:
  11.3 6.0 all-gather.4
  17.4 5.5 all_gather.74
  22.9 5.2 all_gather.79
  28.2 5.2 all_gather.77
  33.5 5.2 all_gather.73
  38.7 5.2 all_gather.76
  58.0 13.3 all-gather.19.cloned.1.call-done
  80.4 26.9 %all-gather.21.cloned.1.call-done = bf16[1024,2048]{1,0:T(8,128)(2,1)} async-done(((bf16[256,2048]{1,0:T(8,128)(2,1)}), bf16[1024,2048]{1,0:T(8,128)(2,1)}) %all-gather.21.cloned.1.call-update) | async-done | bytes 4194320 | tf_op jit(solution)/shard_map/all_gather | solution.py:285
  122.2 6.9 multiply_bitcast_fusion
  138.6 400.6 %while.84 = (s32[]{:T(128)}, f32[8,128,256]{2,1,0:T(8,128)S(1)}, f32[4,64,8,256]{3,2,1,0:T(8,128)}, f32[4,8,128,256]{3,2,1,0:T(8,128)}, f32[4,64,8]{1,2,0:T(8,12...) while((s32[]{:T(128)}, f32[8,128,256]{2,1,0:T(8,128)S(1)}, ...), condition=%wide.region_8.10_spmd.clone, body=%wide.region_5.9_spmd.clone.sunk | while | flops 1916256512 | bytes 28534812 | solution.py:193
  143.4 78.6 %custom-call.32 = f32[8,1,128,128]{2,3,1,0:T(8,128)S(1)} custom-call(f32[8,1,128,128]{3,2,1,0:T(8,128)S(1)} %fusion.497), custom_call_target="InvertDiagBlocksLowerTriangular" | custom-call | tf_op jit(solution)/shard_map/jvp()/while/body/eval_jaxpr/jit(_solve_triangular)/vmap()/triangular_solve/custom-call.1 | solution.py:170
  243.5 78.6 %custom-call.32 = f32[8,1,128,128]{2,3,1,0:T(8,128)S(1)} custom-call(f32[8,1,128,128]{3,2,1,0:T(8,128)S(1)} %fusion.497), custom_call_target="InvertDiagBlocksLowerTriangular" | custom-call | tf_op jit(solution)/shard_map/jvp()/while/body/eval_jaxpr/jit(_solve_triangular)/vmap()/triangular_solve/custom-call.1 | solution.py:170
  343.5 78.6 %custom-call.32 = f32[8,1,128,128]{2,3,1,0:T(8,128)S(1)} custom-call(f32[8,1,128,128]{3,2,1,0:T(8,128)S(1)} %fusion.497), custom_call_target="InvertDiagBlocksLowerTriangular" | custom-call | tf_op jit(solution)/shard_map/jvp()/while/body/eval_jaxpr/jit(_solve_triangular)/vmap()/triangular_solve/custom-call.1 | solution.py:170
  443.6 78.6 %custom-call.32 = f32[8,1,128,128]{2,3,1,0:T(8,128)S(1)} custom-call(f32[8,1,128,128]{3,2,1,0:T(8,128)S(1)} %fusion.497), custom_call_target="InvertDiagBlocksLowerTriangular" | custom-call | tf_op jit(solution)/shard_map/jvp()/while/body/eval_jaxpr/jit(_solve_triangular)/vmap()/triangular_solve/custom-call.1 | solution.py:170
  545.3 5.9 all-reduce.39
  562.4 26.3 %all-gather.35.cloned.1.call-done = bf16[64,128,128]{2,1,0:T(8,128)(2,1)} async-done(((bf16[8,128,128]{2,1,0:T(8,128)(2,1)}), bf16[64,128,128]{2,1,0:T(8,128)(2,1)}) %all-gather.35.cloned.1.call-update) | async-done | bytes 2097168 | tf_op jit(solution)/shard_map/all_gather | solution.py:22
  588.7 50.4 %all-gather.37.cloned.1.call-done = bf16[64,128,128]{2,1,0:T(8,128)(2,1)} async-done(((bf16[8,128,128]{2,1,0:T(8,128)(2,1)}), bf16[64,128,128]{2,1,0:T(8,128)(2,1)}) %all-gather.37.cloned.1.call-update) | async-done | bytes 2097168 | tf_op jit(solution)/shard_map/all_gather | solution.py:22
  639.1 378.8 %while.82 = (s32[]{:T(128)}, f32[8,128,128]{2,1,0:T(8,128)S(1)}, f32[4,64,8,128]{3,1,2,0:T(8,128)}, f32[4,64,8]{1,2,0:T(8,128)S(1)}, f32[4,64]{1,0:T(4,128)S(1)}...) while((s32[]{:T(128)}, f32[8,128,128]{2,1,0:T(8,128)S(1)}, ...), condition=%wide.region_14.16_spmd, body=%wide.region_11.15_spmd.sunk | while | flops 1110163712 | bytes 15164921 | solution.py:193
  644.4 79.4 %custom-call.30 = f32[8,1,128,128]{2,3,1,0:T(8,128)S(1)} custom-call(f32[8,1,128,128]{3,2,1,0:T(8,128)} %fusion.428), custom_call_target="InvertDiagBlocksLowerTriangular" | custom-call | tf_op jit(solution)/shard_map/while/body/eval_jaxpr/checkpoint/jit(_solve_triangular)/vmap()/triangular_solve | solution.py:170
  739.0 79.4 %custom-call.30 = f32[8,1,128,128]{2,3,1,0:T(8,128)S(1)} custom-call(f32[8,1,128,128]{3,2,1,0:T(8,128)} %fusion.428), custom_call_target="InvertDiagBlocksLowerTriangular" | custom-call | tf_op jit(solution)/shard_map/while/body/eval_jaxpr/checkpoint/jit(_solve_triangular)/vmap()/triangular_solve | solution.py:170
  833.6 79.4 %custom-call.30 = f32[8,1,128,128]{2,3,1,0:T(8,128)S(1)} custom-call(f32[8,1,128,128]{3,2,1,0:T(8,128)} %fusion.428), custom_call_target="InvertDiagBlocksLowerTriangular" | custom-call | tf_op jit(solution)/shard_map/while/body/eval_jaxpr/checkpoint/jit(_solve_triangular)/vmap()/triangular_solve | solution.py:170
  928.3 79.4 %custom-call.30 = f32[8,1,128,128]{2,3,1,0:T(8,128)S(1)} custom-call(f32[8,1,128,128]{3,2,1,0:T(8,128)} %fusion.428), custom_call_target="InvertDiagBlocksLowerTriangular" | custom-call | tf_op jit(solution)/shard_map/while/body/eval_jaxpr/checkpoint/jit(_solve_triangular)/vmap()/triangular_solve | solution.py:170
  1030.5 6.0 fusion.215
  1036.5 5.9 fusion.216
  1042.4 9.3 multiply_convert_fusion
  1051.8 5.4 fusion.217
  1081.8 46.0 %all-gather.41.cloned.1.call-done = bf16[64,128,128]{2,1,0:T(8,128)(2,1)} async-done(((bf16[8,128,128]{2,1,0:T(8,128)(2,1)}), bf16[64,128,128]{2,1,0:T(8,128)(2,1)}) %all-gather.41.cloned.1.call-update) | async-done | bytes 2097168 | tf_op jit(solution)/shard_map/all_gather | solution.py:42
  1127.8 12.8 while.85
  1148.8 664.4 %while.83 = (s32[]{:T(128)}, f32[8,128,256]{2,1,0:T(8,128)S(1)}, f32[4,64,8,128]{3,2,1,0:T(8,128)}, f32[4,64,2,8,128]{4,3,2,1,0:T(8,128)}, f32[4,64,2,8,256]{4,3...) while((s32[]{:T(128)}, f32[8,128,256]{2,1,0:T(8,128)S(1)}, ...), condition=%wide.region_33.35_spmd, body=%wide.region_21.34_spmd.sunk | while | flops 5347721728 | bytes 112223408 | solution.py:193
  1197.9 80.0 %custom-call.31 = f32[8,1,128,128]{2,3,1,0:T(8,128)} custom-call(f32[8,1,128,128]{3,2,1,0:T(8,128)} %get-tuple-element.1481), custom_call_target="InvertDiagBlocksLowerTriangular" | custom-call | tf_op jit(solution)/shard_map/transpose(jvp())/while/body/eval_jaxpr/checkpoint/jit(_solve_triangular)/vmap()/triangular_solve | solution.py:170
  1294.4 5.2 pad.366
  1357.3 80.0 %custom-call.31 = f32[8,1,128,128]{2,3,1,0:T(8,128)} custom-call(f32[8,1,128,128]{3,2,1,0:T(8,128)} %get-tuple-element.1481), custom_call_target="InvertDiagBlocksLowerTriangular" | custom-call | tf_op jit(solution)/shard_map/transpose(jvp())/while/body/eval_jaxpr/checkpoint/jit(_solve_triangular)/vmap()/triangular_solve | solution.py:170
  1516.6 80.0 %custom-call.31 = f32[8,1,128,128]{2,3,1,0:T(8,128)} custom-call(f32[8,1,128,128]{3,2,1,0:T(8,128)} %get-tuple-element.1481), custom_call_target="InvertDiagBlocksLowerTriangular" | custom-call | tf_op jit(solution)/shard_map/transpose(jvp())/while/body/eval_jaxpr/checkpoint/jit(_solve_triangular)/vmap()/triangular_solve | solution.py:170
  1613.2 5.2 pad.366
  1676.0 80.0 %custom-call.31 = f32[8,1,128,128]{2,3,1,0:T(8,128)} custom-call(f32[8,1,128,128]{3,2,1,0:T(8,128)} %get-tuple-element.1481), custom_call_target="InvertDiagBlocksLowerTriangular" | custom-call | tf_op jit(solution)/shard_map/transpose(jvp())/while/body/eval_jaxpr/checkpoint/jit(_solve_triangular)/vmap()/triangular_solve | solution.py:170
  1883.9 5.4 collective-permute-done.4
  1898.9 17.7 reduce-scatter.34.cloned.1.call-done
  1916.6 57.3 %reduce-scatter.36.cloned.1.call-done = bf16[256,2816]{1,0:T(8,128)(2,1)} async-done(((bf16[1024,2816]{1,0:T(8,128)(2,1)}), bf16[256,2816]{1,0:T(8,128)(2,1)}) %reduce-scatter.36.cloned.1.call-update) | async-done | bytes 1441808 | tf_op jit(solution)/shard_map/reduce_scatter | solution.py:516
  1973.9 57.5 %reduce-scatter.38.cloned.1.call-done = bf16[704,1024]{1,0:T(8,128)(2,1)} async-done(((bf16[2816,1024]{1,0:T(8,128)(2,1)}), bf16[704,1024]{1,0:T(8,128)(2,1)}) %reduce-scatter.38.cloned.1.call-update) | async-done | bytes 1441808 | tf_op jit(solution)/shard_map/reduce_scatter | solution.py:519
  2031.3 47.1 %reduce-scatter.24.cloned.1.call-done = bf16[256,2048]{1,0:T(8,128)(2,1)} async-done(((bf16[1024,2048]{1,0:T(8,128)(2,1)}), bf16[256,2048]{1,0:T(8,128)(2,1)}) %reduce-scatter.24.cloned.1.call-update) | async-done | bytes 1048592 | tf_op jit(solution)/shard_map/reduce_scatter | solution.py:483
  2078.4 47.1 %reduce-scatter.22.cloned.1.call-done = bf16[256,2048]{1,0:T(8,128)(2,1)} async-done(((bf16[1024,2048]{1,0:T(8,128)(2,1)}), bf16[256,2048]{1,0:T(8,128)(2,1)}) %reduce-scatter.22.cloned.1.call-update) | async-done | bytes 1048592 | tf_op jit(solution)/shard_map/reduce_scatter | solution.py:480
  2126.9 5.7 fusion.136
  2134.3 39.4 %psum.129 = f32[8]{0:T(128)} all-reduce(f32[8]{0:T(128)S(1)} %neg.67), channel_id=1, replica_groups=mesh['seq'=8,'fsdp'=4] {'seq','fsdp'}, use_global_device_ids=true, to_apply=%region_71.73 | all-reduce | flops 8 | bytes 64 | tf_op jit(solution)/shard_map/psum | solution.py:472
  2183.1 6.8 all-reduce.45
  2199.6 21.3 reduce-scatter.28.cloned.1.call-done
  2221.0 22.3 reduce-scatter.26.cloned.1.call-done
  2243.3 39.2 %all-reduce.43 = (bf16[256]{0:T(256)(128)(2,1)S(1)}, bf16[256,16]{0,1:T(8,128)(2,1)S(1)}, bf16[256,8]{0,1:T(8,128)(2,1)S(1)}, bf16[4,256]{1,0:T(4,128)(2,1)S(1)}...) all-reduce(bf16[256]{0:T(256)(128)(2,1)S(1)} %dynamic-slice.2, ...), channel_id=1, replica_groups=mesh['seq'=8,'fsdp'=4] {'seq'}, use_global_device_ids=true, to_apply=%region_39.41 | all-reduce | flops 11808 | bytes 47232 | tf_op jit(solution)/shard_map/psum | solution.py:524
  2287.1 227.5 %all-reduce.48.cloned.1.call-done = (bf16[256,1024]{1,0:T(8,128)(2,1)}, bf16[256,2048]{1,0:T(8,128)(2,1)}, bf16[256,2048]{1,0:T(8,128)(2,1)}, bf16[256,1024]{1,0...) async-done(((bf16[256,1024]{1,0:T(8,128)(2,1)}, bf16[256,2048]{1,0:T(8,128)(2,1)}, ...) | async-done | bytes 7995408 | tf_op jit(solution)/shard_map/psum | solution.py:525
  (1233 shorter events, 695.0 us)
Async XLA Ops:
  7.3 38.6 %all-gather.23.cloned.1.call-start = ((), (), s32[]{:S(2)}) async-start(), calls=%async_computation.15 | async-start | bytes 2621440 | tf_op jit(solution)/shard_map/all_gather | solution.py:283
  8.0 63.2 %all-gather.19.cloned.1.call-start = ((), (), s32[]{:S(2)}) async-start(), calls=%async_computation.13 | async-start | bytes 5242880 | tf_op jit(solution)/shard_map/all_gather | solution.py:284
  8.8 98.6 %all-gather.21.cloned.1.call-start = ((), (), s32[]{:S(2)}) async-start(), calls=%async_computation.14 | async-start | bytes 5242880 | tf_op jit(solution)/shard_map/all_gather | solution.py:285
  9.5 546.8 %all-gather.25.cloned.1.call-start = ((), (), s32[]{:S(2)}) async-start(), calls=%async_computation.16 | async-start | bytes 2621440 | tf_op jit(solution)/shard_map/all_gather | solution.py:288
  10.1 578.6 %all-gather.35.cloned.1.call-start = ((), (), s32[]{:S(2)}) async-start(), calls=%async_computation.31 | async-start | bytes 2359296 | tf_op jit(solution)/shard_map/all_gather | solution.py:22
  17.3 1061.5 %copy-start.99 = (f32[4,1,256]{2,1,0:T(1,128)}, f32[4,1,256]{2,1,0:T(1,128)S(1)}, u32[]{:S(2)}) copy-start(f32[4,1,256]{2,1,0:T(1,128)S(1)} %convert_element_type.445) | copy-start | bytes 12292
  17.3 104.8 %copy-start.101 = (f32[256,1]{0,1:T(1,128)}, f32[256,1]{0,1:T(1,128)S(1)}, u32[]{:S(2)}) copy-start(f32[256,1]{0,1:T(1,128)S(1)} %get-tuple-element.1153) | copy-start | bytes 3076
  17.3 104.8 %copy-start.103 = (f32[256,1]{0,1:T(1,128)}, f32[256,1]{0,1:T(1,128)S(1)}, u32[]{:S(2)}) copy-start(f32[256,1]{0,1:T(1,128)S(1)} %get-tuple-element.1154) | copy-start | bytes 3076
  17.3 104.8 %copy-start.105 = (f32[256,1]{0,1:T(1,128)}, f32[256,1]{0,1:T(1,128)S(1)}, u32[]{:S(2)}) copy-start(f32[256,1]{0,1:T(1,128)S(1)} %get-tuple-element.1155) | copy-start | bytes 3076
  17.3 104.8 %copy-start.107 = (f32[256,1]{0,1:T(1,128)}, f32[256,1]{0,1:T(1,128)S(1)}, u32[]{:S(2)}) copy-start(f32[256,1]{0,1:T(1,128)S(1)} %get-tuple-element.1156) | copy-start | bytes 3076
  22.9 93.1 %copy-start.109 = (f32[1,2048]{1,0:T(1,128)}, f32[1,2048]{1,0:T(1,128)S(1)}, u32[]{:S(2)}) copy-start(f32[1,2048]{1,0:T(1,128)S(1)} %get-tuple-element.1141) | copy-start | bytes 24580
  22.9 93.1 %copy-start.111 = (f32[1,2048]{1,0:T(1,128)}, f32[1,2048]{1,0:T(1,128)S(1)}, u32[]{:S(2)}) copy-start(f32[1,2048]{1,0:T(1,128)S(1)} %get-tuple-element.1142) | copy-start | bytes 24580
  22.9 93.1 %copy-start.113 = (f32[1,2048]{1,0:T(1,128)}, f32[1,2048]{1,0:T(1,128)S(1)}, u32[]{:S(2)}) copy-start(f32[1,2048]{1,0:T(1,128)S(1)} %get-tuple-element.1143) | copy-start | bytes 24580
  22.9 93.1 %copy-start.115 = (f32[1,2048]{1,0:T(1,128)}, f32[1,2048]{1,0:T(1,128)S(1)}, u32[]{:S(2)}) copy-start(f32[1,2048]{1,0:T(1,128)S(1)} %get-tuple-element.1144) | copy-start | bytes 24580
  33.4 88.7 %copy-start.117 = (f32[1,2048]{1,0:T(1,128)}, f32[1,2048]{1,0:T(1,128)S(1)}, u32[]{:S(2)}) copy-start(f32[1,2048]{1,0:T(1,128)S(1)} %get-tuple-element.1137) | copy-start | bytes 24580
  33.4 88.7 %copy-start.119 = (f32[1,2048]{1,0:T(1,128)}, f32[1,2048]{1,0:T(1,128)S(1)}, u32[]{:S(2)}) copy-start(f32[1,2048]{1,0:T(1,128)S(1)} %get-tuple-element.1138) | copy-start | bytes 24580
  33.4 88.7 %copy-start.121 = (f32[1,2048]{1,0:T(1,128)}, f32[1,2048]{1,0:T(1,128)S(1)}, u32[]{:S(2)}) copy-start(f32[1,2048]{1,0:T(1,128)S(1)} %get-tuple-element.1139) | copy-start | bytes 24580
  33.4 88.7 %copy-start.123 = (f32[1,2048]{1,0:T(1,128)}, f32[1,2048]{1,0:T(1,128)S(1)}, u32[]{:S(2)}) copy-start(f32[1,2048]{1,0:T(1,128)S(1)} %get-tuple-element.1140) | copy-start | bytes 24580
  44.8 62.6 %copy-start.10 = (bf16[256,1024]{1,0:T(8,128)(2,1)}, bf16[256,1024]{1,0:T(8,128)(2,1)S(1)}, u32[]{:S(2)}) copy-start(bf16[256,1024]{1,0:T(8,128)(2,1)S(1)} %fusion.140) | copy-start | bytes 1572868
  49.2 5.0 collective-permute-start.2
  77.0 38.9 %collective-permute-start = (bf16[3,2048]{1,0:T(4,128)(2,1)S(1)}, bf16[3,2048]{1,0:T(4,128)(2,1)S(1)}, u32[]{:S(2)}, u32[]{:S(2)}) collective-permute-start(bf16[3,2048]{1,0:T(4,128)(2,1)S(1)} %slice.240), channel_id=1, source_target_pairs={{0,4},{4,8},{8,12},{12,16},{16,20},{20,24},{24,28},{1,5},{5,9},{9,... | collective-permute-start | bytes 36872 | tf_op jit(solution)/shard_map/ppermute | solution.py:16
  112.3 9.7 collective-permute-start.1
  540.1 98.9 %all-gather.37.cloned.1.call-start = ((), (), s32[]{:S(2)}) async-start(), calls=%async_computation.32 | async-start | bytes 2359296 | tf_op jit(solution)/shard_map/all_gather | solution.py:22
  540.7 485.9 %all-gather.27.cloned.1.call-start = ((), (), s32[]{:S(2)}) async-start(), calls=%async_computation.17 | async-start | bytes 2621440 | tf_op jit(solution)/shard_map/all_gather | solution.py:293
  541.5 489.0 %all-gather.29.cloned.1.call-start = ((), (), s32[]{:S(2)}) async-start(), calls=%async_computation.18 | async-start | bytes 7208960 | tf_op jit(solution)/shard_map/all_gather | solution.py:387
  542.2 494.3 %all-gather.31.cloned.1.call-start = ((), (), s32[]{:S(2)}) async-start(), calls=%async_computation.19 | async-start | bytes 7208960 | tf_op jit(solution)/shard_map/all_gather | solution.py:388
  543.0 499.5 %all-gather.33.cloned.1.call-start = ((), (), s32[]{:S(2)}) async-start(), calls=%async_computation.20 | async-start | bytes 7208960 | tf_op jit(solution)/shard_map/all_gather | solution.py:389
  543.6 538.2 %all-gather.39.cloned.1.call-start = ((), (), s32[]{:S(2)}) async-start(), calls=%async_computation.33 | async-start | bytes 2359296 | tf_op jit(solution)/shard_map/all_gather | solution.py:42
  562.3 565.5 %all-gather.41.cloned.1.call-start = ((), (), s32[]{:S(2)}) async-start(), calls=%async_computation.34 | async-start | bytes 2359296 | tf_op jit(solution)/shard_map/all_gather | solution.py:42
  1022.8 39.7 %copy-start.29 = (f32[256,8,128]{0,2,1:T(8,128)}, f32[256,8,128]{0,2,1:T(8,128)S(1)}, u32[]{:S(2)}) copy-start(f32[256,8,128]{0,2,1:T(8,128)S(1)} %copy.420) | copy-start | bytes 3145732
  1069.1 829.7 %reduce-scatter.32.cloned.1.call-start = ((), (), s32[]{:S(2)}) async-start(), calls=%async_computation.27 | async-start | bytes 2621440 | tf_op jit(solution)/shard_map/reduce_scatter | solution.py:507
  1072.4 826.5 %reduce-scatter.30.cloned.1.call-start = ((), (), s32[]{:S(2)}) async-start(), calls=%async_computation.26 | async-start | bytes 2621440 | tf_op jit(solution)/shard_map/reduce_scatter | solution.py:492
  1081.7 817.1 %reduce-scatter.20.cloned.1.call-start = ((), (), s32[]{:S(2)}) async-start(), calls=%async_computation.21 | async-start | bytes 2621440 | tf_op jit(solution)/shard_map/reduce_scatter | solution.py:477
  1820.2 5.8 collective-permute-start.3
  1828.1 88.4 %reduce-scatter.34.cloned.1.call-start = ((), (), s32[]{:S(2)}) async-start(), calls=%async_computation.28 | async-start | bytes 7208960 | tf_op jit(solution)/shard_map/reduce_scatter | solution.py:513
  1832.4 141.5 %reduce-scatter.36.cloned.1.call-start = ((), (), s32[]{:S(2)}) async-start(), calls=%async_computation.29 | async-start | bytes 7208960 | tf_op jit(solution)/shard_map/reduce_scatter | solution.py:516
  1838.0 193.3 %reduce-scatter.38.cloned.1.call-start = ((), (), s32[]{:S(2)}) async-start(), calls=%async_computation.30 | async-start | bytes 7208960 | tf_op jit(solution)/shard_map/reduce_scatter | solution.py:519
  1843.7 234.7 %reduce-scatter.24.cloned.1.call-start = ((), (), s32[]{:S(2)}) async-start(), calls=%async_computation.23 | async-start | bytes 5242880 | tf_op jit(solution)/shard_map/reduce_scatter | solution.py:483
  1869.2 5.6 collective-permute-start.5
  1878.1 247.4 %reduce-scatter.22.cloned.1.call-start = ((), (), s32[]{:S(2)}) async-start(), calls=%async_computation.22 | async-start | bytes 5242880 | tf_op jit(solution)/shard_map/reduce_scatter | solution.py:480
  1882.6 6.7 collective-permute-start.4
  1892.6 299.4 %reduce-scatter.40.cloned.1.call-start = ((), (), s32[]{:S(2)}) async-start(), calls=%async_computation.35 | async-start | bytes 327680
  1894.6 298.3 %reduce-scatter.44.cloned.1.call-start = ((), (), s32[]{:S(2)}) async-start(), calls=%async_computation.37 | async-start | bytes 655360
  1895.8 302.9 %reduce-scatter.42.cloned.1.call-start = ((), (), s32[]{:S(2)}) async-start(), calls=%async_computation.36 | async-start | bytes 655360
  1897.3 323.7 %reduce-scatter.28.cloned.1.call-start = ((), (), s32[]{:S(2)}) async-start(), calls=%async_computation.25 | async-start | bytes 20480 | tf_op jit(solution)/shard_map/reduce_scatter | solution.py:489
  1897.9 345.4 %reduce-scatter.26.cloned.1.call-start = ((), (), s32[]{:S(2)}) async-start(), calls=%async_computation.24 | async-start | bytes 40960 | tf_op jit(solution)/shard_map/reduce_scatter | solution.py:486
  1898.7 615.9 %all-reduce.48.cloned.1.call-start = ((), (), s32[]{:S(2)}) async-start(), calls=%async_computation.38 | async-start | bytes 15990784 | tf_op jit(solution)/shard_map/psum | solution.py:525
  2132.5 41.2 %copy-start.87 = (bf16[1024,16]{0,1:T(8,128)(2,1)S(1)}, bf16[1024,16]{0,1:T(8,128)(2,1)}, u32[]{:S(2)}) copy-start(bf16[1024,16]{0,1:T(8,128)(2,1)} %copy-done.86) | copy-start | bytes 98308
  (189 other events, 890.1 us)
Sparse Core Ops, SparseCore 0:
  9.7 25.4 all-gather.22
  36.7 34.5 all-gather.18
  72.8 34.4 all-gather.20
  108.8 22.5 all-gather.24
  540.2 48.3 all-gather.34
  591.2 47.7 all-gather.36
  640.6 21.1 all-gather.26
  663.3 43.5 all-gather.28
  708.5 43.9 all-gather.30
  753.8 43.5 all-gather.32
  799.6 50.3 all-gather.38
  1069.2 58.5 all-gather.40
  1130.3 29.9 reduce-scatter.31
  1162.9 31.3 reduce-scatter.29
  1828.2 30.8 reduce-scatter.19
  1861.7 54.8 reduce-scatter.33
  1918.9 54.8 reduce-scatter.35
  1976.4 54.8 reduce-scatter.37
  2033.8 44.4 reduce-scatter.23
  2080.9 44.5 reduce-scatter.21
  2128.5 19.9 reduce-scatter.39
  2151.8 22.1 reduce-scatter.43
  2177.0 21.5 reduce-scatter.41
  2201.6 19.3 reduce-scatter.27
  2223.9 19.3 reduce-scatter.25
  2249.4 265.1 all-reduce.47
where the time goes:
time: 2550 us; the launch traced here: 2540 us
  other arithmetic  1060 us (42%)
  waiting for transfers between devices  686 us (27%)
  matrix products  344 us (13%)
  local copies, waits for them, and re-layouts  250 us (10%)
  blocking collectives  129 us (5%)
  loops' own time  30.3 us (1%)
    another operation x32, other arithmetic, delta_block(): jax.scipy.linalg.solve_triangular(system, target, lower=True, unit_diagon...  961 us
    psum x1, waiting for transfers between devices, per_device(): lax.psum(all_parts[1].astype(jnp.bfloat16), 'seq').astype(jnp.float32)  227 us
    all_gather x2, waiting for transfers between devices, prefix(): lax.all_gather(a.astype(kind), axis)  76.7 us
    reduce_scatter x1, waiting for transfers between devices, per_device(): lax.psum_scatter(grad_down.astype(jnp.bfloat16), 'fsdp', scatter_dimensio...  57.5 us
    reduce_scatter x1, waiting for transfers between devices, per_device(): lax.psum_scatter(grad_up.astype(jnp.bfloat16), 'fsdp', scatter_dimension=...  57.3 us
  transfers between devices with their start and end apart: 32, of which 18 were waited for; matrix products, arithmetic and copies ran while one was open for 64% of the time, Pallas kernels for 0%

commit v1 on v0

v1 whole, which is shorter than its diff:
```python
import functools

import jax
import jax.numpy as jnp
from jax import lax
from jax.experimental import pallas as pl
from jax.experimental.pallas import tpu as pltpu
from jax.sharding import PartitionSpec as P

SPAN = 64
ROWS = 128
HEAD = 128
EPSILON = 1e-06
LOW = jnp.bfloat16
WIDE = jnp.float32
VMEM_LIMIT = 56 * 1024 * 1024


def contract(left, right, left_dim, right_dim):
    return lax.dot_general(
        left, right, (((left_dim,), (right_dim,)), ((), ())), preferred_element_type=WIDE
    )


def halves(value):
    high = value.astype(LOW)
    return high, (value - high.astype(WIDE)).astype(LOW)


def mm(left, right, left_dim=1, right_dim=0):
    return contract(left.astype(LOW), right.astype(LOW), left_dim, right_dim)


def mm3(left, right, left_dim=1, right_dim=0):
    lh, ll = halves(left)
    rh, rl = halves(right)
    return (
        contract(lh, rh, left_dim, right_dim)
        + contract(lh, rl, left_dim, right_dim)
        + contract(ll, rh, left_dim, right_dim)
    )


def stack(*parts):
    return jnp.concatenate(parts, axis=0)


def row_maps():
    row = lax.broadcasted_iota(jnp.int32, (ROWS, ROWS), 0)
    col = lax.broadcasted_iota(jnp.int32, (ROWS, ROWS), 1)
    tok, step = row & (SPAN - 1), row >> 6
    tok_c, step_c = col & (SPAN - 1), col >> 6
    return tok, step, tok_c, step_c


def span_tokens(offs_ref, doc_count, first):
    place = first + lax.broadcasted_iota(jnp.int32, (SPAN, 1), 0)
    begin = jnp.zeros((SPAN, 1), jnp.int32)
    for j in range(doc_count):
        start = offs_ref[0, j]
        begin = jnp.where(place >= start, start, begin)
    return place - begin


def softplus(value):
    return jnp.maximum(value, 0.0) + jnp.log1p(jnp.exp(-jnp.abs(value)))


def decay_sums(small, rate):
    logs = -rate * softplus(small)
    tok = lax.broadcasted_iota(jnp.int32, (SPAN, SPAN), 0)
    tok_c = lax.broadcasted_iota(jnp.int32, (SPAN, SPAN), 1)
    lower = jnp.where(tok >= tok_c, 1.0, 0.0).astype(LOW)
    tok_w = lax.broadcasted_iota(jnp.int32, (SPAN, ROWS), 0)
    tok_wc = lax.broadcasted_iota(jnp.int32, (SPAN, ROWS), 1) & (SPAN - 1)
    upper = jnp.where(tok_w <= tok_wc, 1.0, 0.0).astype(LOW)
    high, rest = halves(logs)
    cols = contract(lower, high, 1, 0) + contract(lower, rest, 1, 0)
    rows = contract(high, upper, 0, 0) + contract(rest, upper, 0, 0)
    return cols[:, 2:3], rows[2:3, :]


def unit(values):
    scale = lax.rsqrt(jnp.sum(values * values, axis=1, keepdims=True) + EPSILON)
    return values * scale, scale


def span_factors(small, rate, pos):
    sig = jax.nn.sigmoid(small)
    cum, cum_row = decay_sums(small, rate)
    beta = stack(sig[:, 0:1], sig[:, 1:2])
    cum2, pos2 = stack(cum, cum), stack(pos, pos)
    tok, step, tok_c, step_c = row_maps()
    before = tok > tok_c
    here = tok == tok_c
    reach = (before | (here & (step >= step_c))) & (tok - tok_c <= pos2)
    decay = jnp.where(reach, jnp.exp(jnp.where(reach, cum2 - cum_row, 0.0)), 0.0)
    strict = before | (here & (step > step_c))
    tok1 = tok[:, 0:1]
    carry = jnp.where(pos2 > tok1, jnp.exp(cum2), 0.0)
    end, end_pos = cum[SPAN - 1 : SPAN], pos[SPAN - 1 : SPAN]
    leave = jnp.where(SPAN - 1 - tok1 <= end_pos, jnp.exp(end - cum2), 0.0)
    carry_all = jnp.where(end_pos >= SPAN, jnp.exp(end), 0.0)
    return beta, decay, strict, carry, leave, carry_all, tok ^ tok_c


def unit_lower_inverse(strict_part, apart):
    row = lax.broadcasted_iota(jnp.int32, (ROWS, ROWS), 0)
    col = lax.broadcasted_iota(jnp.int32, (ROWS, ROWS), 1)
    inverse = jnp.where(row == col, 1.0, 0.0) - jnp.where(apart == 0, strict_part, 0.0)
    for level in range(6):
        block = jnp.where((apart >> level) == 1, strict_part, 0.0)
        inverse = inverse - mm(mm(inverse, block), inverse)
    return inverse


def forward_kernel(
    span_count, doc_count, group,
    offs_ref, rate_ref, pre_ref, gs_ref, edge_ref, taps_ref, gain_ref, state_ref,
    gated_ref, mixed_ref, conv_ref, t_ref, u_ref, sc_ref, qh_ref, a_ref, s_ref, end_ref,
    w_scr, u0_scr, b_scr, o0_scr,
):
    base = offs_ref[0, doc_count]
    rate = rate_ref[0, 0]

    def local(c):
        lo = pl.multiple_of(c * SPAN, SPAN)
        here = pre_ref[pl.ds(lo, SPAN), :].astype(WIDE)
        prior_at = pl.multiple_of(jnp.maximum(lo - 16, 0), 16)
        prior = pre_ref[pl.ds(prior_at, 16), :].astype(WIDE)
        prior = jnp.where(c == 0, edge_ref[...].astype(WIDE), prior)
        rows = stack(prior, here)
        pos = span_tokens(offs_ref, doc_count, base + lo)
        conv = taps_ref[0:1, :] * here
        for lag in range(1, 4):
            shifted = rows[16 - lag : 16 - lag + SPAN]
            conv = conv + jnp.where(pos >= lag, taps_ref[lag : lag + 1, :] * shifted, 0.0)
        conv_ref[pl.ds(lo, SPAN), :] = conv
        act = conv * jax.nn.sigmoid(conv)
        query, _ = unit(act[:, 0:128])
        key0, _ = unit(act[:, 128:256])
        key1, _ = unit(act[:, 256:384])
        keys = stack(key0, key1)
        values = stack(act[:, 384:512], act[:, 512:640])
        small = gs_ref[pl.ds(lo, SPAN), 128:256]
        beta, decay, strict, carry, leave, carry_all, apart = span_factors(small, rate, pos)
        inner = mm(keys, keys, 1, 1)
        inverse = unit_lower_inverse(jnp.where(strict, beta * decay * inner, 0.0), apart)
        t_ref[c] = inverse.astype(LOW)
        both = mm(inverse, jnp.concatenate([(beta * carry) * keys, beta * values], axis=1))
        weight, fresh = both[:, :HEAD], both[:, HEAD:]
        w_scr[c] = weight.astype(LOW)
        u0_scr[c] = fresh
        leaving = (keys * leave).astype(LOW)
        row = lax.broadcasted_iota(jnp.int32, (HEAD, HEAD), 0)
        col = lax.broadcasted_iota(jnp.int32, (HEAD, HEAD), 1)
        a_ref[c] = jnp.where(row == col, carry_all, 0.0) - mm(leaving, weight, 0, 0)
        b_scr[c] = mm(fresh, leaving, 0, 0)
        scores = mm(query, keys, 1, 1) * decay[SPAN:, :]
        sc_ref[c] = scores.astype(LOW)
        mixed_both = mm(scores, both)
        qh_ref[c] = (carry[SPAN:] * query - mixed_both[:, :HEAD]).astype(LOW)
        o0_scr[c] = mixed_both[:, HEAD:]

    def locals_step(i, none):
        for u in range(group):
            local(i * group + u)
        return none

    lax.fori_loop(0, span_count // group, locals_step, 0)

    def chain(c, state):
        s_ref[c] = state
        u_ref[c] = (u0_scr[c] - mm(w_scr[c], state, 1, 1)).astype(LOW)
        mixed = o0_scr[c] + mm(qh_ref[c], state, 1, 1)
        lo = pl.multiple_of(c * SPAN, SPAN)
        mixed_ref[pl.ds(lo, SPAN), :] = mixed
        gate = gs_ref[pl.ds(lo, SPAN), 0:128]
        scale = lax.rsqrt(jnp.mean(mixed * mixed, axis=1, keepdims=True) + EPSILON)
        gated_ref[pl.ds(lo, SPAN), :] = (
            mixed * scale * gain_ref[...] * (gate * jax.nn.sigmoid(gate))
        ).astype(LOW)
        return mm3(state, a_ref[c], 1, 1) + b_scr[c]

    def chain_step(i, state):
        for u in range(group):
            state = chain(i * group + u, state)
        return state

    end_ref[...] = lax.fori_loop(0, span_count // group, chain_step, state_ref[...])


def backward_kernel(
    span_count, doc_count, group,
    offs_ref, rate_ref, pre_ref, gs_ref, edge_ref, taps_ref, gain_ref,
    mixed_ref, conv_ref, t_ref, u_ref, sc_ref, qh_ref, a_ref, s_ref, dgated_ref, dend_ref,
    dy_ref, dtaps_ref, dgain_ref, drate_ref, dedge_ref, dbegin_ref,
    do_scr, f_scr, ds_scr, next_scr,
):
    base = offs_ref[0, doc_count]
    rate = rate_ref[0, 0]
    dgain_ref[...] = jnp.zeros_like(dgain_ref)
    dtaps_ref[...] = jnp.zeros_like(dtaps_ref)
    drate_ref[...] = jnp.zeros_like(drate_ref)
    next_scr[...] = jnp.zeros_like(next_scr)

    def gate_back(c):
        lo = pl.multiple_of(c * SPAN, SPAN)
        mixed = mixed_ref[pl.ds(lo, SPAN), :]
        gate = gs_ref[pl.ds(lo, SPAN), 0:128]
        scale = lax.rsqrt(jnp.mean(mixed * mixed, axis=1, keepdims=True) + EPSILON)
        normed = mixed * scale
        sig = jax.nn.sigmoid(gate)
        grad = dgated_ref[pl.ds(lo, SPAN), :].astype(WIDE)
        by_gain = grad * normed
        dy_ref[pl.ds(lo, SPAN), 640:768] = (
            by_gain * gain_ref[...] * (sig * (1.0 + gate * (1.0 - sig)))
        ).astype(LOW)
        dgain_ref[...] += jnp.sum(by_gain * (gate * sig), axis=0, keepdims=True)
        dn = grad * (gate * sig) * gain_ref[...]
        dmixed = scale * (dn - normed * jnp.mean(dn * normed, axis=1, keepdims=True))
        do_low = dmixed.astype(LOW)
        do_scr[c] = do_low
        f_scr[c] = contract(do_low, qh_ref[c], 0, 0)

    def gate_step(i, none):
        for u in range(group):
            gate_back(i * group + u)
        return none

    lax.fori_loop(0, span_count // group, gate_step, 0)

    def chain_step(i, grad):
        for u in range(group):
            c = span_count - 1 - (i * group + u)
            ds_scr[c] = grad
            grad = mm3(grad, a_ref[c]) + f_scr[c]
        return grad

    dbegin_ref[...] = lax.fori_loop(0, span_count // group, chain_step, dend_ref[...])

    def local(c):
        lo = pl.multiple_of(c * SPAN, SPAN)
        pos = span_tokens(offs_ref, doc_count, base + lo)
        conv = conv_ref[pl.ds(lo, SPAN), :]
        sig = jax.nn.sigmoid(conv)
        act = conv * sig
        query, scale_q = unit(act[:, 0:128])
        key0, scale_0 = unit(act[:, 128:256])
        key1, scale_1 = unit(act[:, 256:384])
        keys = stack(key0, key1)
        values = stack(act[:, 384:512], act[:, 512:640])
        small = gs_ref[pl.ds(lo, SPAN), 128:256]
        beta, decay, strict, carry, leave, carry_all, _ = span_factors(small, rate, pos)
        state, dstate = s_ref[c], ds_scr[c]
        state_l, dstate_l = state.astype(LOW), dstate.astype(LOW)
        upd, out_grad, keys_l = u_ref[c], do_scr[c], keys.astype(LOW)
        dupd = contract(sc_ref[c], out_grad, 0, 0) + mm(keys * leave, dstate_l, 1, 1)
        dtarget = mm(t_ref[c], dupd, 0, 0)
        pair = stack(dtarget.astype(LOW), out_grad)
        by_upd = contract(pair, upd, 1, 1)
        by_state = contract(pair, state_l, 1, 0)
        dinner = jnp.where(strict, -by_upd[:ROWS] * decay, 0.0)
        dscore = by_upd[ROWS:] * decay[SPAN:, :]
        both = stack(dinner, dscore).astype(LOW)
        reading = contract(both, keys_l, 1, 0)
        read_key = reading[:ROWS] - carry * by_state[:ROWS]
        dquery = reading[ROWS:] + carry[SPAN:] * by_state[ROWS:]
        dleave = leave * contract(upd, dstate_l, 1, 0)
        write_key = contract(both, stack(beta * keys, query).astype(LOW), 0, 0) + dleave
        key_read = jnp.sum(keys * read_key, axis=1, keepdims=True)
        dbeta = jnp.sum(dtarget * values, axis=1, keepdims=True) + key_read
        dcum = beta * key_read - jnp.sum(keys * write_key, axis=1, keepdims=True)
        dcum = dcum[:SPAN] + dcum[SPAN:] + jnp.sum(query * dquery, axis=1, keepdims=True)
        through = jnp.sum(keys * dleave, axis=0, keepdims=True) + carry_all * jnp.sum(
            dstate * state, axis=0, keepdims=True
        )
        through = jnp.sum(through, axis=1, keepdims=True)
        tok1 = lax.broadcasted_iota(jnp.int32, (SPAN, 1), 0)
        dcum = dcum + jnp.where(tok1 == SPAN - 1, through, 0.0)
        tok = lax.broadcasted_iota(jnp.int32, (SPAN, SPAN), 0)
        tok_c = lax.broadcasted_iota(jnp.int32, (SPAN, SPAN), 1)
        upper = jnp.where(tok <= tok_c, 1.0, 0.0).astype(LOW)
        high, rest = halves(jnp.broadcast_to(dcum, (SPAN, 128)))
        dlog = contract(upper, high, 1, 0) + contract(upper, rest, 1, 0)
        soft = softplus(small)
        sig_small = jax.nn.sigmoid(small)
        lane = lax.broadcasted_iota(jnp.int32, (SPAN, 128), 1)
        drate_ref[...] += jnp.sum(jnp.where(lane == 2, -dlog * soft, 0.0), axis=0, keepdims=True)
        dsig = jnp.where(lane == 0, dbeta[:SPAN], dbeta[SPAN:]) * sig_small * (1.0 - sig_small)
        dsmall = jnp.where(lane < 2, dsig, jnp.where(lane == 2, -rate * dlog * sig_small, 0.0))
        dy_ref[pl.ds(lo, SPAN), 768:896] = dsmall.astype(LOW)
        dkey = beta * read_key + write_key
        dvalue = beta * dtarget

        def unit_back(grad, normed, scale):
            return scale * (grad - normed * jnp.sum(grad * normed, axis=1, keepdims=True))

        dact = jnp.concatenate(
            [
                unit_back(dquery, query, scale_q),
                unit_back(dkey[:SPAN], key0, scale_0),
                unit_back(dkey[SPAN:], key1, scale_1),
                dvalue[:SPAN],
                dvalue[SPAN:],
            ],
            axis=1,
        )
        dconv = dact * (sig * (1.0 + conv * (1.0 - sig)))
        here = pre_ref[pl.ds(lo, SPAN), :].astype(WIDE)
        prior_at = pl.multiple_of(jnp.maximum(lo - 16, 0), 16)
        prior = pre_ref[pl.ds(prior_at, 16), :].astype(WIDE)
        prior = jnp.where(c == 0, edge_ref[...].astype(WIDE), prior)
        rows = stack(prior, here)
        dpre = taps_ref[0:1, :] * dconv
        dtaps_ref[0:1, :] += jnp.sum(dconv * here, axis=0, keepdims=True)
        for lag in range(1, 4):
            kept = jnp.where(pos >= lag, dconv, 0.0)
            shifted = rows[16 - lag : 16 - lag + SPAN]
            dtaps_ref[lag : lag + 1, :] += jnp.sum(kept * shifted, axis=0, keepdims=True)
            kept = kept * taps_ref[lag : lag + 1, :]
            dpre = dpre + stack(kept, next_scr[lag])[lag : lag + SPAN]
            next_scr[lag] = kept[0:8]
        dy_ref[pl.ds(lo, SPAN), 0:640] = dpre.astype(LOW)

    def local_step(i, none):
        for u in range(group):
            local(span_count - 1 - (i * group + u))
        return none

    lax.fori_loop(0, span_count // group, local_step, 0)

    none = jnp.zeros((16, 640), WIDE)
    dedge = none
    for lag in range(1, 4):
        dedge = dedge + stack(none, next_scr[lag])[lag : lag + 16]
    dedge_ref[...] = dedge


def vmem_spec():
    return pl.BlockSpec(memory_space=pltpu.VMEM)


def smem_spec():
    return pl.BlockSpec(memory_space=pltpu.SMEM)


def run_forward(offs, rate, pre, gs, edge, taps, gain, state):
    tokens = pre.shape[0]
    spans = tokens // SPAN
    shape = jax.ShapeDtypeStruct
    outs = (
        shape((tokens, HEAD), LOW),
        shape((tokens, HEAD), WIDE),
        shape((tokens, 640), WIDE),
        shape((spans, ROWS, ROWS), LOW),
        shape((spans, ROWS, HEAD), LOW),
        shape((spans, SPAN, ROWS), LOW),
        shape((spans, SPAN, HEAD), LOW),
        shape((spans, HEAD, HEAD), WIDE),
        shape((spans, HEAD, HEAD), WIDE),
        shape((HEAD, HEAD), WIDE),
    )
    return pl.pallas_call(
        functools.partial(forward_kernel, spans, offs.shape[1] - 1, 4),
        out_shape=outs,
        in_specs=[smem_spec(), smem_spec()] + [vmem_spec()] * 6,
        out_specs=[vmem_spec()] * len(outs),
        scratch_shapes=[
            pltpu.VMEM((spans, ROWS, HEAD), LOW),
            pltpu.VMEM((spans, ROWS, HEAD), WIDE),
            pltpu.VMEM((spans, HEAD, HEAD), WIDE),
            pltpu.VMEM((spans, SPAN, HEAD), WIDE),
        ],
        compiler_params=pltpu.CompilerParams(vmem_limit_bytes=VMEM_LIMIT),
        cost_estimate=pl.CostEstimate(
            flops=spans * 60 * 2 * 128**3, bytes_accessed=24 * 1024 * 1024, transcendentals=0
        ),
        name="delta_forward",
    )(offs, rate, pre, gs, edge, taps, gain, state)


def run_backward(offs, rate, pre, gs, edge, taps, gain, saved, dgated, dend):
    tokens = pre.shape[0]
    spans = tokens // SPAN
    shape = jax.ShapeDtypeStruct
    outs = (
        shape((tokens, 896), LOW),
        shape((8, 640), WIDE),
        shape((1, HEAD), WIDE),
        shape((1, HEAD), WIDE),
        shape((16, 640), WIDE),
        shape((HEAD, HEAD), WIDE),
    )
    return pl.pallas_call(
        functools.partial(backward_kernel, spans, offs.shape[1] - 1, 2),
        out_shape=outs,
        in_specs=[smem_spec(), smem_spec()] + [vmem_spec()] * 15,
        out_specs=[vmem_spec()] * len(outs),
        scratch_shapes=[
            pltpu.VMEM((spans, SPAN, HEAD), LOW),
            pltpu.VMEM((spans, HEAD, HEAD), WIDE),
            pltpu.VMEM((spans, HEAD, HEAD), WIDE),
            pltpu.VMEM((4, 8, 640), WIDE),
        ],
        compiler_params=pltpu.CompilerParams(vmem_limit_bytes=VMEM_LIMIT),
        cost_estimate=pl.CostEstimate(
            flops=spans * 80 * 2 * 128**3, bytes_accessed=24 * 1024 * 1024, transcendentals=0
        ),
        name="delta_backward",
    )(offs, rate, pre, gs, edge, taps, gain, *saved, dgated, dend)


def rms_parts(values):
    return values * lax.rsqrt(jnp.mean(values * values, axis=-1, keepdims=True) + EPSILON)


def rms_back(grad_scaled, values):
    scale = lax.rsqrt(jnp.mean(values * values, axis=-1, keepdims=True) + EPSILON)
    normed = values * scale
    return scale * (
        grad_scaled - normed * jnp.mean(grad_scaled * normed, axis=-1, keepdims=True)
    )


def dot_plain(left, right, kind=WIDE):
    return jnp.dot(left, right, preferred_element_type=kind)


def dot_left(left, right, kind=WIDE):
    return contract(left, right, 0, 0).astype(kind)


def dot_right(left, right):
    return contract(left, right, 1, 1)


def per_device(
    tokens, cotangent, offsets, gain_in, w_query, w_key, w_value, w_beta, w_decay, w_outgate,
    conv_query, conv_key, conv_value, decay_scale, gain_head, w_out, gain_ffn, w_gate, w_up,
    w_down,
):
    seq, fsdp = lax.axis_size("seq"), lax.axis_size("fsdp")
    heads = decay_scale.shape[0]
    taps = conv_query.shape[0]
    own_rows = tokens.shape[1]
    shard = w_query.shape[0]
    width = shard * fsdp
    teams = seq // heads
    assert teams * heads == seq and width == heads * HEAD
    place = lax.axis_index("seq")
    head, team = place % heads, place // heads
    member = lax.axis_index("fsdp")
    if teams == 1:
        team_groups, head_groups = None, None
    else:
        team_groups = [[t * heads + h for h in range(heads)] for t in range(teams)]
        head_groups = [[t * heads + h for t in range(teams)] for h in range(heads)]

    def gather_rows(value):
        return lax.all_gather(value, "fsdp", axis=0, tiled=True)

    seq_tokens = lax.all_gather(
        tokens[0], "seq", axis=0, tiled=True, axis_index_groups=team_groups
    )
    length = seq_tokens.shape[0]

    def head_columns(weights, step):
        return lax.dynamic_slice_in_dim(weights, step * width + head * HEAD, HEAD, axis=1)

    small_columns = jnp.concatenate(
        [
            lax.dynamic_slice_in_dim(w_beta, head, 1, axis=1),
            lax.dynamic_slice_in_dim(w_beta, heads + head, 1, axis=1),
            lax.dynamic_slice_in_dim(w_decay, head, 1, axis=1),
            jnp.zeros((shard, HEAD - 3), LOW),
        ],
        axis=1,
    )
    packed = jnp.concatenate(
        [
            head_columns(w_query, 0),
            head_columns(w_key, 0),
            head_columns(w_key, 1),
            head_columns(w_value, 0),
            head_columns(w_value, 1),
            head_columns(w_outgate, 0),
            small_columns,
        ],
        axis=1,
    )
    full_packed = gather_rows(packed)
    vectors = jnp.concatenate(
        [
            gain_in[None],
            gain_ffn[None],
            jnp.pad(gain_head, (0, shard - gain_head.shape[0]))[None],
            conv_query,
            conv_key[:, :shard],
            conv_key[:, shard:],
            conv_value[:, :shard],
            conv_value[:, shard:],
        ],
        axis=0,
    )
    vectors = lax.all_gather(vectors, "fsdp", axis=0)
    full_gain_in = vectors[:, 0].reshape(width).astype(WIDE)
    full_gain_ffn = vectors[:, 1].reshape(width).astype(WIDE)
    full_gain_head = vectors[:, 2, : gain_head.shape[0]].reshape(1, HEAD).astype(WIDE)

    def full_taps(at, pieces):
        part = vectors[:, at : at + pieces * taps].reshape(fsdp, pieces, taps, shard)
        return jnp.transpose(part, (2, 0, 1, 3)).reshape(taps, fsdp * pieces * shard)

    conv_q = full_taps(3, 1)
    conv_k = full_taps(3 + taps, 2)
    conv_v = full_taps(3 + 3 * taps, 2)
    head_taps = jnp.concatenate(
        [
            head_columns(conv_q, 0),
            head_columns(conv_k, 0),
            head_columns(conv_k, 1),
            head_columns(conv_v, 0),
            head_columns(conv_v, 1),
        ],
        axis=1,
    ).astype(WIDE)
    head_taps = jnp.pad(head_taps, ((0, 8 - taps), (0, 0)))
    full_out = gather_rows(w_out)

    def to_columns(value):
        return lax.all_to_all(value, "fsdp", 1, 0, tiled=True)

    cols_gate, cols_up = to_columns(w_gate), to_columns(w_up)
    group_cot = gather_rows(cotangent[0])

    seq_wide = seq_tokens.astype(WIDE)
    normed_low = (rms_parts(seq_wide) * full_gain_in).astype(LOW)
    pre = dot_plain(normed_low, full_packed[:, :640]).astype(LOW)
    gate_small = dot_plain(normed_low, full_packed[:, 640:])
    offs = jnp.concatenate(
        [offsets, jnp.broadcast_to(team * length, (1, 1)).astype(jnp.int32)], axis=1
    )
    rate = lax.dynamic_slice_in_dim(decay_scale, head, 1).reshape(1, 1)
    zero_state = jnp.zeros((HEAD, HEAD), WIDE)
    if teams == 1:
        edge = jnp.zeros((16, 640), LOW)
    else:
        forth = [(i, i + heads) for i in range(seq - heads)]
        back = [(i + heads, i) for i in range(seq - heads)]
        edge = lax.ppermute(pre[-16:], "seq", forth)

    def forward_from(state):
        return run_forward(
            offs, rate, pre, gate_small, edge, head_taps, full_gain_head, state
        )

    state_in = zero_state
    if teams > 1:
        trial = forward_from(zero_state)
        steps, end = trial[7], trial[9]

        def along(c, total):
            return jnp.dot(total, steps[c].T, precision=lax.Precision.HIGHEST)

        whole_map = lax.fori_loop(0, steps.shape[0], along, jnp.eye(HEAD, dtype=WIDE))
        for _ in range(teams - 1):
            out = jnp.dot(state_in, whole_map, precision=lax.Precision.HIGHEST) + end
            state_in = lax.ppermute(out.astype(LOW), "seq", forth).astype(WIDE)
    gated, *saved, _ = forward_from(state_in)

    gated_own = lax.all_to_all(
        gated, "seq", 0, 1, tiled=True, axis_index_groups=team_groups
    )
    inputs = tokens[0].astype(WIDE)
    mixer_res = inputs + dot_plain(gated_own, full_out)

    mid_normed = rms_parts(mixer_res)
    mid_low = (mid_normed * full_gain_ffn).astype(LOW)
    group_mid = gather_rows(mid_low)
    gate_pre = dot_plain(group_mid, cols_gate)
    up_pre = dot_plain(group_mid, cols_up)
    sig = jax.nn.sigmoid(gate_pre)
    act = gate_pre * sig
    hidden = (act * up_pre).astype(LOW)
    grad_hidden = dot_right(group_cot, w_down)
    grad_gate_pre = (grad_hidden * up_pre * (sig * (1.0 + gate_pre * (1.0 - sig)))).astype(LOW)
    grad_up_pre = (grad_hidden * act).astype(LOW)
    grad_mid = dot_right(grad_gate_pre, cols_gate) + dot_right(grad_up_pre, cols_up)
    grad_mid = lax.psum_scatter(
        grad_mid.astype(LOW), "fsdp", scatter_dimension=0, tiled=True
    ).astype(WIDE)
    down_part = lax.psum_scatter(
        dot_plain(hidden, w_down).astype(LOW), "fsdp", scatter_dimension=0, tiled=True
    )
    layer_out = (mixer_res + down_part.astype(WIDE)).astype(LOW)

    grad_res = cotangent[0].astype(WIDE) + rms_back(grad_mid * full_gain_ffn, mixer_res)
    grad_gain_ffn = jnp.sum(grad_mid * mid_normed, axis=0)
    res_low = grad_res.astype(LOW)
    grad_gated = dot_right(res_low, full_out).astype(LOW)
    dgated = lax.all_to_all(
        grad_gated, "seq", 1, 0, tiled=True, axis_index_groups=team_groups
    )

    grad_down = dot_left(hidden, group_cot, LOW)
    grad_gate = dot_left(group_mid, grad_gate_pre, LOW)
    grad_up = dot_left(group_mid, grad_up_pre, LOW)
    grad_out = dot_left(gated_own, res_low, LOW)

    def share(value):
        return lax.psum_scatter(value, "seq", scatter_dimension=0, tiled=True)

    def whole(value):
        return lax.all_gather(value, "seq", axis=0, tiled=True)

    def columns_done(value):
        part = value.reshape(fsdp, seq, shard // seq, value.shape[1])
        part = lax.psum_scatter(part, "seq", scatter_dimension=1, tiled=True)
        part = part.reshape(shard // seq * fsdp, value.shape[1])
        part = lax.all_to_all(part, "fsdp", 0, 1, tiled=True)
        return whole(part).astype(WIDE)

    out_gate, out_up = columns_done(grad_gate), columns_done(grad_up)
    out_down = whole(share(grad_down)).astype(WIDE)
    grad_out = lax.psum_scatter(grad_out, "fsdp", scatter_dimension=0, tiled=True)
    out_out = lax.psum(grad_out, "seq").astype(WIDE)

    def backward_from(dend):
        return run_backward(
            offs, rate, pre, gate_small, edge, head_taps, full_gain_head, saved, dgated, dend
        )

    dend = zero_state
    if teams > 1:
        begin = backward_from(zero_state)[5]
        for _ in range(teams - 1):
            out = lax.dot_general(
                dend, whole_map, (((1,), (1,)), ((), ())), precision=lax.Precision.HIGHEST
            )
            dend = lax.ppermute((out + begin).astype(LOW), "seq", back).astype(WIDE)
    dy, dtaps, dgain, drate, dedge, _ = backward_from(dend)
    if teams > 1:
        from_next = lax.ppermute(dedge.astype(LOW), "seq", back).astype(WIDE)
        tail = (dy[-16:, :640].astype(WIDE) + from_next).astype(LOW)
        dy = lax.dynamic_update_slice(dy, tail, (length - 16, 0))

    grad_normed = dot_right(dy, full_packed)
    grad_gain_in = jnp.sum(grad_normed * rms_parts(seq_wide), axis=0)
    grad_normed = lax.psum_scatter(
        grad_normed.astype(LOW), "seq", scatter_dimension=0, tiled=True,
        axis_index_groups=team_groups,
    ).astype(WIDE)
    input_grad = (grad_res + rms_back(grad_normed * full_gain_in, inputs)).astype(LOW)

    grad_packed = dot_left(normed_low, dy)
    extra = jnp.zeros((fsdp, 16, 896), WIDE)
    extra = extra.at[:, 0, :shard].set(grad_gain_in.reshape(fsdp, shard))
    extra = extra.at[:, 1, :shard].set(grad_gain_ffn.reshape(fsdp, shard))
    gh = gain_head.shape[0]
    extra = extra.at[:, 2, :gh].set(dgain.reshape(fsdp, gh))
    extra = extra.at[:, 3, :HEAD].set(drate)
    extra = extra.at[:, 4 : 4 + taps, :640].set(dtaps[None, :taps])
    combined = jnp.concatenate(
        [grad_packed.reshape(fsdp, shard, 896), extra], axis=1
    ).astype(LOW)
    combined = lax.psum_scatter(
        combined.reshape(fsdp * (shard + 16), 896), "fsdp", scatter_dimension=0, tiled=True
    )
    if teams > 1:
        combined = lax.psum(combined, "seq", axis_index_groups=head_groups)
    combined = lax.all_gather(combined, "seq", axis=0, axis_index_groups=team_groups)

    def by_head(at):
        return jnp.transpose(combined[:, :shard, at : at + HEAD], (1, 0, 2)).reshape(shard, width)

    out_query = by_head(0).astype(WIDE)
    out_key = jnp.concatenate([by_head(128), by_head(256)], axis=1).astype(WIDE)
    out_value = jnp.concatenate([by_head(384), by_head(512)], axis=1).astype(WIDE)
    out_gatew = by_head(640).astype(WIDE)
    smalls = jnp.transpose(combined[:, :shard, 768:771], (1, 2, 0))
    out_beta = smalls[:, 0:2].reshape(shard, 2 * heads).astype(WIDE)
    out_decay = smalls[:, 2].astype(WIDE)
    extras = combined[:, shard:].astype(WIDE)
    if teams > 1:
        pass
    out_gain_in = jnp.sum(extras[:, 0, :shard], axis=0)
    out_gain_ffn = jnp.sum(extras[:, 1, :shard], axis=0)
    out_gain_head = jnp.sum(extras[:, 2, :gh], axis=0)
    out_rate = extras[:, 3, 2]
    tap_rows = extras[:, 4 : 4 + taps]

    def own_taps(at, steps):
        part = jnp.stack(
            [tap_rows[:, :, at + i * HEAD : at + (i + 1) * HEAD] for i in range(steps)], axis=0
        )
        part = jnp.transpose(part, (2, 0, 1, 3)).reshape(taps, steps * width)
        size = steps * shard
        return lax.dynamic_slice_in_dim(part, member * size, size, axis=1)

    return (
        layer_out[None],
        input_grad[None],
        out_gain_in,
        out_query,
        out_key,
        out_value,
        out_beta,
        out_decay,
        out_gatew,
        own_taps(0, 1),
        own_taps(128, 2),
        own_taps(384, 2),
        out_rate,
        out_gain_head,
        out_out,
        out_gain_ffn,
        out_gate,
        out_up,
        out_down,
    )


def solution(mesh):
    rows, lanes = P("fsdp", None), P(None, "fsdp")
    block = P("fsdp", "seq", None)
    return jax.shard_map(
        per_device,
        mesh=mesh,
        in_specs=(
            block, block, rows, P("fsdp"), rows, rows, rows, rows, rows, rows,
            lanes, lanes, lanes, P(), P("fsdp"), rows, P("fsdp"), rows, rows, rows,
        ),
        out_specs=(
            block, block, P("fsdp"), rows, rows, rows, rows, rows, rows,
            lanes, lanes, lanes, P(), P("fsdp"), rows, P("fsdp"), rows, rows, rows,
        ),
        check_vma=False,
    )
```

time: 2550 us -> 1020 us (0.40)
  other arithmetic: 1060 us -> 40.1 us
  matrix products: 344 us -> 69.9 us
  local copies, waits for them, and re-layouts: 250 us -> 60.1 us
  Pallas kernels: 0 us -> 140 us
  blocking collectives: 129 us -> 21.8 us
  waiting for transfers between devices: 686 us -> 636 us
  loops' own time: 30.3 us -> 0 us
    another operation x73 -> x2, other arithmetic: 982 us -> 0.02 us  [own_taps(): jnp.stack([tap_rows[:, :, at + i * HEAD:at + (i + 1) * HEAD] for i in ran...]
    dot_general x157 -> x16, matrix products: 307 us -> 69.9 us  [the longest x10 44.4 us: contract(): lax.dot_general(left, right, (((left_dim,), (right_dim,)), ((), ())), pre...]
    pallas_call x0 -> x2, Pallas kernels: none -> 140 us  [the longest x1 78.8 us: run_forward(): pl.pallas_call(functools.partial(forward_kernel, spans, offs.shape[1] - 1...]
    all_gather x12 -> x9, waiting for transfers between devices: 163 us -> 277 us  [the longest x3 128 us: whole(): return lax.all_gather(value, 'seq', axis=0, tiled=True)]
    reduce_scatter x10 -> x6, waiting for transfers between devices: 270 us -> 164 us  [the longest x1 85.6 us: per_device(): lax.psum_scatter(grad_normed.astype(LOW), 'seq', scatter_dimension=0, til...]
    psum x1, waiting for transfers between devices: 227 us -> 124 us  [per_device(): out_out = lax.psum(grad_out, 'seq').astype(WIDE)]
    psum x2 -> x0, blocking collectives: 78.6 us -> none  [the longest x1 39.4 us: per_device(): rate_sum = lax.psum(grad_rate, ('seq', 'fsdp'))]
    all_to_all x0 -> x4, waiting for transfers between devices: none -> 66.5 us  [the longest x2 51.7 us: to_columns(): return lax.all_to_all(value, 'fsdp', 1, 0, tiled=True)]
  transfers between devices with their start and end apart: 32 -> 20, of which waited for: 18 -> 15; matrix products, arithmetic and copies ran while one was open for 64% -> 11% of each run, Pallas kernels for 0% -> 14%
where the time goes in v1:
time: 1020 us; the launch traced here: 1010 us
  waiting for transfers between devices  636 us (62%)
  Pallas kernels  140 us (14%)
  matrix products  69.9 us (7%)
  local copies, waits for them, and re-layouts  60.1 us (6%)
  other arithmetic  40.1 us (4%)
  starting transfers between devices  29.1 us (3%)
  blocking collectives  21.8 us (2%)
  between operations  14.9 us (1%)
    all_gather x3, waiting for transfers between devices, whole(): return lax.all_gather(value, 'seq', axis=0, tiled=True)  128 us
    psum x1, waiting for transfers between devices, per_device(): out_out = lax.psum(grad_out, 'seq').astype(WIDE)  124 us
    reduce_scatter x1, waiting for transfers between devices, per_device(): lax.psum_scatter(grad_normed.astype(LOW), 'seq', scatter_dimension=0, til...  85.6 us
    pallas_call x1, Pallas kernels, run_forward(): pl.pallas_call(functools.partial(forward_kernel, spans, offs.shape[1] - 1...  78.8 us
    all_gather x1, waiting for transfers between devices, per_device(): lax.all_gather(combined, 'seq', axis=0, axis_index_groups=team_groups)  67.2 us
    all_gather x1, waiting for transfers between devices, per_device(): lax.all_gather(tokens[0], 'seq', axis=0, tiled=True, axis_index_groups=te...  63.6 us
    pallas_call x1, Pallas kernels, run_backward(): pl.pallas_call(functools.partial(backward_kernel, spans, offs.shape[1] -...  60.9 us
    all_to_all x2, waiting for transfers between devices, to_columns(): return lax.all_to_all(value, 'fsdp', 1, 0, tiled=True)  51.7 us
  transfers between devices with their start and end apart: 20, of which 15 were waited for; matrix products, arithmetic and copies ran while one was open for 11% of the time, Pallas kernels for 14%

profile of v1, /device:TPU:0, one launch (start us, length us, event | category | flops | bytes accessed | tf_op | source)
XLA Modules:
  0.0 1011.1 jit_solution(17313580257300661995)
XLA Ops:
  13.9 6.2 all-gather.4
  22.8 63.6 %all-gather.27.cloned.1.call-done = bf16[1,2048,1024]{2,1,0:T(8,128)(2,1)} async-done(((bf16[1,256,1024]{2,1,0:T(8,128)(2,1)}), bf16[1,2048,1024]{2,1,0:T(8,128)(2,1)}) %all-gather.27.cloned.1.call-update) | async-done | bytes 4194320 | tf_op jit(solution)/shard_map/all_gather | solution.py:463
  86.4 3.1 fusion.4
  89.5 18.5 %all-gather.15.cloned.1.call-done = bf16[1024,896]{1,0:T(8,128)(2,1)} async-done(((bf16[256,896]{1,0:T(8,128)(2,1)}), bf16[1024,896]{1,0:T(8,128)(2,1)}) %all-gather.15.cloned.1.call-update) | async-done | bytes 1835024 | tf_op jit(solution)/shard_map/all_gather | solution.py:461
  107.9 5.1 fusion.31.gs_ref
  113.1 4.8 convolution_convert_fusion.pre_ref
  119.1 78.8 %delta_forward.1 = (bf16[2048,128]{1,0:T(8,128)(2,1)}, f32[2048,128]{1,0:T(8,128)}, f32[2048,640]{1,0:T(8,128)}, bf16[32,128,128]{2,1,0:T(8,128)(2,1)}, bf16[32,...) custom-call(s32[1,17]{1,0:T(1,128)} %pad_add_fusion.offs_ref, ...), custom_call_target="tpu_custom_call" | custom-call | flops 8053063680 | bytes 25165824 | tf_op jit(solution)/shard_map/delta_forward/pallas_call | solution.py:364
  200.0 5.5 all-to-all-start
  205.6 14.8 %all-to-all-done = bf16[8,256,128]{1,2,0:T(8,128)(2,1)S(1)} async-done(((bf16[8,256,128]{1,2,0:T(8,128)(2,1)}), bf16[8,256,128]{1,2,0:T(8,128)(2,1)S(1)}, u32[]{:S(2)}, u32[]{:S(2)}) %all-to-all-start) | async-done | bytes 524320 | tf_op jit(solution)/shard_map/all_to_all | solution.py:572
  227.0 4.4 all-to-all-start.1
  233.9 24.9 %all-to-all-done.1 = bf16[256,4,704]{0,2,1:T(8,128)(2,1)} async-done(((bf16[256,4,704]{0,2,1:T(8,128)(2,1)}), bf16[256,4,704]{0,2,1:T(8,128)(2,1)}, u32[]{:S(2)}, u32[]{:S(2)}) %all-to-all-start.1) | async-done | bytes 1441824 | tf_op jit(solution)/shard_map/all_to_all | solution.py:532
  258.8 4.3 all-to-all-start.2
  263.4 2.9 copy.165
  266.3 26.8 %all-to-all-done.2 = bf16[256,4,704]{0,2,1:T(8,128)(2,1)} async-done(((bf16[256,4,704]{0,2,1:T(8,128)(2,1)}), bf16[256,4,704]{0,2,1:T(8,128)(2,1)}, u32[]{:S(2)}, u32[]{:S(2)}) %all-to-all-start.2) | async-done | bytes 1441824 | tf_op jit(solution)/shard_map/all_to_all | solution.py:532
  293.1 2.7 copy.166
  295.8 5.4 fusion.44
  301.2 3.3 fusion.45
  304.5 6.3 multiply_convert_fusion
  313.2 3.2 add_convert_fusion
  316.4 4.5 convolution_convert_fusion.2
  321.0 26.9 %reduce-scatter.11.cloned.1.call-done = bf16[256,1024]{1,0:T(8,128)(2,1)} async-done(((bf16[1024,1024]{1,0:T(8,128)(2,1)}), bf16[256,1024]{1,0:T(8,128)(2,1)}) %reduce-scatter.11.cloned.1.call-update) | async-done | bytes 524304 | tf_op jit(solution)/shard_map/reduce_scatter | solution.py:590
  349.4 33.2 %reduce-scatter.9.cloned.1.call-done = bf16[256,1024]{1,0:T(8,128)(2,1)} async-done(((bf16[1024,1024]{1,0:T(8,128)(2,1)}), bf16[256,1024]{1,0:T(8,128)(2,1)}) %reduce-scatter.9.cloned.1.call-update) | async-done | bytes 524304 | tf_op jit(solution)/shard_map/reduce_scatter | solution.py:593
  388.6 4.4 fusion.10
  396.2 5.5 all-to-all-start.3
  401.8 3.7 convolution_convert_fusion.5
  407.0 3.7 convolution_convert_fusion.4
  412.3 6.5 reduce-scatter.17.cloned.1.call-done
  418.8 8.3 reduce-scatter.15.cloned.1.call-start
  427.2 60.9 %delta_backward.1 = (bf16[2048,896]{1,0:T(8,128)(2,1)}, f32[8,640]{1,0:T(8,128)}, f32[1,128]{1,0:T(1,128)}, f32[1,128]{1,0:T(1,128)}, f32[16,640]{1,0:T(8,128)}, /*index=5*/f32[128,128]{1,0:T(8,128)}) custom-call(s32[1,17]{1,0:T(1,128)} %pad_add_fusion.offs_ref, f32[1,1]{1,0:T(1,128)} %bitcast.2.rate_ref, bf16[2048,640]{1,0:T(8,128)(2,1)} %convolution_convert_fusion.pre_ref, ...), custom_call_target="tpu_custom_call" | custom-call | flops 10737418240 | bytes 25165824 | tf_op jit(solution)/shard_map/delta_backward/pallas_call | solution.py:395
  488.2 8.7 fusion.3
  499.6 8.2 convolution_convert_fusion.3
  511.2 124.5 %all-reduce.8.cloned.1.call-done = (bf16[256,1024]{1,0:T(8,128)(2,1)}, bf16[4,8,32,704]{3,2,1,0:T(8,128)(2,1)}, bf16[4,8,32,704]{3,2,1,0:T(8,128)(2,1)}) async-done(((bf16[256,1024]{1,0:T(8,128)(2,1)}, bf16[4,8,32,704]{3,2,1,0:T(8,128)(2,1)}, bf16[4,8,32,704]{3,2,1,0:T(8,128)(2,1)}), (bf16[256,1024]{1,0:T(8,128)(2,1)}, bf16[4,8,32,704]{3,2,1,0:T(8,128)(2,1)}, ...) | async-done | bytes 3407888 | tf_op jit(solution)/shard_map/psum | solution.py:627
  637.3 7.9 all_to_all.114
  647.9 7.7 all_to_all.115
  656.9 11.7 %reduce-scatter.15.cloned.1.call-done = bf16[272,896]{1,0:T(8,128)(2,1)} async-done(((bf16[1088,896]{1,0:T(8,128)(2,1)}), bf16[272,896]{1,0:T(8,128)(2,1)}) %reduce-scatter.15.cloned.1.call-update) | async-done | bytes 487440 | tf_op jit(solution)/shard_map/reduce_scatter | solution.py:667
  668.8 44.9 %all-gather.25.cloned.1.call-done = bf16[704,1024]{1,0:T(8,128)(2,1)} async-done(((bf16[88,1024]{1,0:T(8,128)(2,1)}), bf16[704,1024]{1,0:T(8,128)(2,1)}) %all-gather.25.cloned.1.call-update) | async-done | bytes 1441808 | tf_op jit(solution)/shard_map/all_gather | solution.py:615
  713.7 3.3 convert_element_type.201
  718.1 85.6 %reduce-scatter.13.cloned.1.call-done = bf16[256,1024]{1,0:T(8,128)(2,1)} async-done(((bf16[2048,1024]{1,0:T(8,128)(2,1)}), bf16[256,1024]{1,0:T(8,128)(2,1)}) %reduce-scatter.13.cloned.1.call-update) | async-done | bytes 524304 | tf_op jit(solution)/shard_map/reduce_scatter | solution.py:650
  807.3 42.1 %all-gather.21.cloned.1.call-done = bf16[256,2816]{1,0:T(8,128)(2,1)} async-done(((bf16[32,2816]{1,0:T(8,128)(2,1)}), bf16[256,2816]{1,0:T(8,128)(2,1)}) %all-gather.21.cloned.1.call-update) | async-done | bytes 1441808 | tf_op jit(solution)/shard_map/all_gather | solution.py:615
  849.4 3.1 convert_element_type.197
  852.5 41.1 %all-gather.23.cloned.1.call-done = bf16[256,2816]{1,0:T(8,128)(2,1)} async-done(((bf16[32,2816]{1,0:T(8,128)(2,1)}), bf16[256,2816]{1,0:T(8,128)(2,1)}) %all-gather.23.cloned.1.call-update) | async-done | bytes 1441808 | tf_op jit(solution)/shard_map/all_gather | solution.py:615
  893.7 3.1 convert_element_type.199
  896.8 67.2 %all-gather.31.cloned.1.call-done = bf16[2176,896]{1,0:T(8,128)(2,1)} async-done(((bf16[272,896]{1,0:T(8,128)(2,1)}), bf16[2176,896]{1,0:T(8,128)(2,1)}) %all-gather.31.cloned.1.call-update) | async-done | bytes 3899408 | tf_op jit(solution)/shard_map/all_gather | solution.py:672
  965.7 3.3 convert_bitcast_fusion
  983.9 2.7 maximum_convert_fusion.1
  986.5 2.9 copy.154
  990.6 2.6 maximum_convert_fusion
  993.2 2.9 copy.153
  (190 shorter events, 80.7 us)
Async XLA Ops:
  7.2 297.3 %copy-start = (bf16[704,1024]{1,0:T(8,128)(2,1)S(1)}, bf16[704,1024]{1,0:T(8,128)(2,1)}, u32[]{:S(2)}) copy-start(bf16[704,1024]{1,0:T(8,128)(2,1)} %param.49) | copy-start | bytes 4325380
  7.2 6.4 copy-start.18
  7.2 6.4 copy-start.19
  7.2 6.4 copy-start.20
  7.2 6.4 copy-start.12
  7.3 6.4 copy-start.11
  7.3 6.4 copy-start.13
  7.3 13.8 %copy-start.21 = (f32[8]{0:T(128)S(1)}, f32[8]{0:T(128)}, u32[]{:S(2)}) copy-start(f32[8]{0:T(128)} %param.43) | copy-start | bytes 100
  7.3 15.0 %copy-start.22 = (s32[1,16]{1,0:T(1,128)S(1)}, s32[1,16]{1,0:T(1,128)}, u32[]{:S(2)}) copy-start(s32[1,16]{1,0:T(1,128)} %param.32) | copy-start | bytes 196
  7.3 79.1 %all-gather.27.cloned.1.call-start = ((), (), s32[]{:S(2)}) async-start(), calls=%async_computation.24 | async-start | bytes 4718592 | tf_op jit(solution)/shard_map/all_gather | solution.py:463
  8.0 99.9 %all-gather.15.cloned.1.call-start = ((), (), s32[]{:S(2)}) async-start(), calls=%async_computation.12 | async-start | bytes 2293760 | tf_op jit(solution)/shard_map/all_gather | solution.py:461
  12.9 192.8 %all-gather.17.cloned.1.call-start = ((), (), s32[]{:S(2)}) async-start(), calls=%async_computation.13 | async-start | bytes 2621440 | tf_op jit(solution)/shard_map/all_gather | solution.py:461
  89.5 23.6 %copy-start.9 = (f32[2048]{0:T(1024)}, f32[2048]{0:T(1024)S(1)}, u32[]{:S(2)}) copy-start(f32[2048]{0:T(1024)S(1)} %add_rsqrt_fusion) | copy-start | bytes 24580
  107.9 5.2 copy-start.3
  107.9 5.2 copy-start.16
  197.9 22.5 %copy-start.2 = (bf16[1,256,1024]{2,1,0:T(8,128)(2,1)S(1)}, bf16[1,256,1024]{2,1,0:T(8,128)(2,1)}, u32[]{:S(2)}) copy-start(bf16[1,256,1024]{2,1,0:T(8,128)(2,1)} %param.30) | copy-start | bytes 1572868
  200.0 20.4 %all-to-all-start = ((bf16[8,256,128]{1,2,0:T(8,128)(2,1)}), bf16[8,256,128]{1,2,0:T(8,128)(2,1)S(1)}, u32[]{:S(2)}, u32[]{:S(2)}) async-start(bf16[8,256,128]{1,2,0:T(8,128)(2,1)} %copy.134), calls=%async_computation | async-start | bytes 1048576 | tf_op jit(solution)/shard_map/all_to_all | solution.py:572
  205.5 90.2 %all-gather.19.cloned.1.call-start = ((), (), s32[]{:S(2)}) async-start(), calls=%async_computation.14 | async-start | bytes 2621440 | tf_op jit(solution)/shard_map/all_gather | solution.py:461
  223.9 80.6 %all-gather.29.cloned.1.call-start = ((), (), s32[]{:S(2)}) async-start(), calls=%async_computation.25 | async-start | bytes 2621440 | tf_op jit(solution)/shard_map/all_gather | solution.py:461
  227.0 31.8 %all-to-all-start.1 = ((bf16[256,4,704]{0,2,1:T(8,128)(2,1)}), bf16[256,4,704]{0,2,1:T(8,128)(2,1)}, u32[]{:S(2)}, u32[]{:S(2)}) async-start(bf16[256,4,704]{0,2,1:T(8,128)(2,1)} %bitcast.166), calls=%async_computation.1 | async-start | bytes 2883584 | tf_op jit(solution)/shard_map/all_to_all | solution.py:532
  258.8 34.3 %all-to-all-start.2 = ((bf16[256,4,704]{0,2,1:T(8,128)(2,1)}), bf16[256,4,704]{0,2,1:T(8,128)(2,1)}, u32[]{:S(2)}, u32[]{:S(2)}) async-start(bf16[256,4,704]{0,2,1:T(8,128)(2,1)} %bitcast.165), calls=%async_computation.2 | async-start | bytes 2883584 | tf_op jit(solution)/shard_map/all_to_all | solution.py:532
  263.1 84.8 %reduce-scatter.11.cloned.1.call-start = ((), (), s32[]{:S(2)}) async-start(), calls=%async_computation.16 | async-start | bytes 2621440 | tf_op jit(solution)/shard_map/reduce_scatter | solution.py:590
  295.8 5.4 copy-start.6
  295.8 5.4 copy-start.15
  304.5 6.3 copy-start.5
  310.8 1.9 copy-start.25
  310.8 1.9 copy-start.26
  310.8 2.4 copy-start.7
  316.4 66.3 %reduce-scatter.9.cloned.1.call-start = ((), (), s32[]{:S(2)}) async-start(), calls=%async_computation.15 | async-start | bytes 2621440 | tf_op jit(solution)/shard_map/reduce_scatter | solution.py:593
  321.0 97.9 %reduce-scatter.17.cloned.1.call-start = ((), (), s32[]{:S(2)}) async-start(), calls=%async_computation.19 | async-start | bytes 2621440 | tf_op jit(solution)/shard_map/reduce_scatter | solution.py:626
  387.2 1.4 copy-start.27
  387.2 122.1 %reduce-scatter.19.cloned.1.call-start = ((), (), s32[]{:S(2)}) async-start(), calls=%async_computation.22 | async-start | bytes 1622016 | tf_op jit(solution)/shard_map/reduce_scatter | solution.py:612
  396.2 30.9 %all-to-all-start.3 = ((bf16[256,8,128]{2,0,1:T(8,128)(2,1)}), bf16[256,8,128]{2,0,1:T(8,128)(2,1)}, u32[]{:S(2)}, u32[]{:S(2)}) async-start(bf16[256,8,128]{2,0,1:T(8,128)(2,1)} %bitcast.159), calls=%async_computation.5 | async-start | bytes 1048576 | tf_op jit(solution)/shard_map/all_to_all | solution.py:602
  401.7 233.9 %all-reduce.8.cloned.1.call-start = ((), (), s32[]{:S(2)}) async-start(), calls=%async_computation.27 | async-start | bytes 7340032 | tf_op jit(solution)/shard_map/psum | solution.py:627
  418.8 249.7 %reduce-scatter.15.cloned.1.call-start = ((), (), s32[]{:S(2)}) async-start(), calls=%async_computation.18 | async-start | bytes 2437120 | tf_op jit(solution)/shard_map/reduce_scatter | solution.py:667
  427.1 61.0 %copy-start.4 = (bf16[1,2048,1024]{2,1,0:T(8,128)(2,1)S(1)}, bf16[1,2048,1024]{2,1,0:T(8,128)(2,1)}, u32[]{:S(2)}) copy-start(bf16[1,2048,1024]{2,1,0:T(8,128)(2,1)} %all-gather.27.cloned.1.call-done) | copy-start | bytes 12582916
  427.1 61.0 %copy-start.10 = (f32[2048]{0:T(1024)S(1)}, f32[2048]{0:T(1024)}, u32[]{:S(2)}) copy-start(f32[2048]{0:T(1024)} %copy-done.9) | copy-start | bytes 24580
  427.1 61.0 %copy-start.17 = (bf16[1024,896]{1,0:T(8,128)(2,1)S(1)}, bf16[1024,896]{1,0:T(8,128)(2,1)}, u32[]{:S(2)}) copy-start(bf16[1024,896]{1,0:T(8,128)(2,1)} %all-gather.15.cloned.1.call-done) | copy-start | bytes 5505028
  488.1 9.3 copy-start.24
  488.1 11.2 %copy-start.14 = (f32[1,128]{1,0:T(1,128)S(1)}, f32[1,128]{1,0:T(1,128)}, u32[]{:S(2)}) copy-start(f32[1,128]{1,0:T(1,128)} %get-tuple-element.103) | copy-start | bytes 1540
  509.3 204.4 %all-gather.25.cloned.1.call-start = ((), (), s32[]{:S(2)}) async-start(), calls=%async_computation.23 | async-start | bytes 1622016 | tf_op jit(solution)/shard_map/all_gather | solution.py:615
  509.8 293.9 %reduce-scatter.13.cloned.1.call-start = ((), (), s32[]{:S(2)}) async-start(), calls=%async_computation.17 | async-start | bytes 4718592 | tf_op jit(solution)/shard_map/reduce_scatter | solution.py:650
  509.9 0.8 copy-start.23
  510.6 338.8 %all-gather.21.cloned.1.call-start = ((), (), s32[]{:S(2)}) async-start(), calls=%async_computation.20 | async-start | bytes 1622016 | tf_op jit(solution)/shard_map/all_gather | solution.py:615
  646.2 247.4 %all-gather.23.cloned.1.call-start = ((), (), s32[]{:S(2)}) async-start(), calls=%async_computation.21 | async-start | bytes 1622016 | tf_op jit(solution)/shard_map/all_gather | solution.py:615
  656.6 307.3 %all-gather.31.cloned.1.call-start = ((), (), s32[]{:S(2)}) async-start(), calls=%async_computation.26 | async-start | bytes 4386816 | tf_op jit(solution)/shard_map/all_gather | solution.py:672
  668.8 48.2 %copy-start.8 = (bf16[256,1024]{1,0:T(8,128)(2,1)S(1)}, bf16[256,1024]{1,0:T(8,128)(2,1)}, u32[]{:S(2)}) copy-start(bf16[256,1024]{1,0:T(8,128)(2,1)} %get-tuple-element.185) | copy-start | bytes 1572868
  999.9 4.5 copy-start.1
Sparse Core Ops, SparseCore 0:
  10.3 76.0 all-gather.26
  88.5 19.3 all-gather.14
  109.5 22.6 all-gather.16
  224.0 29.4 all-gather.18
  254.9 36.2 all-gather.28
  316.5 31.4 reduce-scatter.10
  351.2 31.4 reduce-scatter.8
  387.4 31.4 reduce-scatter.16
  422.6 65.3 reduce-scatter.18
  492.9 142.7 all-reduce.7
  639.0 29.4 reduce-scatter.14
  670.6 43.0 all-gather.24
  717.3 86.3 reduce-scatter.12
  806.6 42.7 all-gather.20
  852.2 41.3 all-gather.22
  895.9 67.9 all-gather.30

commit v2 on v1

--- a/solution.py
+++ b/solution.py
@@ -435,6 +435,187 @@
     return contract(left, right, 1, 1)
 
 
+def exchanged(value, axis, bit):
+    size = lax.axis_size(axis)
+    return lax.ppermute(value, axis, [(i, i ^ bit) for i in range(size)])
+
+
+def near_order(size):
+    order, bit = [0], size // 2
+    while bit:
+        order = order + [o ^ bit for o in order]
+        bit //= 2
+    return order
+
+
+def near_gather(value, axis):
+    bit = lax.axis_size(axis) // 2
+    while bit:
+        value = stack(value, exchanged(value, axis, bit))
+        bit //= 2
+    return value
+
+
+def near_scatter(value, axis):
+    size, bit = lax.axis_size(axis), 1
+    while bit < size:
+        half = value.shape[0] // 2
+        came = exchanged(value[half:].astype(LOW), axis, bit).astype(WIDE)
+        value = value[:half].astype(WIDE) + came
+        bit *= 2
+    return value
+
+
+def near_blocks(value, axis):
+    size, me = lax.axis_size(axis), lax.axis_index(axis)
+    return stack(
+        *[lax.dynamic_index_in_dim(value, me ^ o, 0, False) for o in near_order(size)]
+    )
+
+
+def ordered_gather(value, axis):
+    bit, me = lax.axis_size(axis) // 2, lax.axis_index(axis)
+    value = value[None]
+    while bit:
+        other = exchanged(value, axis, bit)
+        pair = jnp.where(
+            (me & bit) == 0, jnp.stack([value, other], 1), jnp.stack([other, value], 1)
+        )
+        value = pair.reshape((pair.shape[0] * 2,) + value.shape[1:])
+        bit //= 2
+    return value
+
+
+def team_step(value, team, move):
+    size = lax.axis_size("seq")
+    pairs = [(t + i, t + move(i)) for t in range(0, size, team) for i in range(team)]
+    return lax.ppermute(value, "seq", pairs)
+
+
+def spread_gather(value, team):
+    me = lax.axis_index("seq") % team
+    found = []
+    for k in range(team // 2):
+        turned = value if k == 0 else team_step(value, team, lambda i: (i + 2 * k) % team)
+        across = team_step(turned, team, lambda i: i ^ 1)
+        found.append(((me - 2 * k) % team, turned))
+        found.append((((me ^ 1) - 2 * k) % team, across))
+    return found
+
+
+def spread_scatter(block, team):
+    me = lax.axis_index("seq") % team
+    half = team // 2
+    total = None
+    for k in sorted(range(half), key=lambda k: -min(k, half - k)):
+        came = team_step(block(((me ^ 1) + 2 * k) % team), team, lambda i: i ^ 1)
+        pair = block((me + 2 * k) % team).astype(WIDE) + came.astype(WIDE)
+        if k:
+            pair = team_step(pair.astype(LOW), team, lambda i: (i + 2 * k) % team).astype(WIDE)
+        total = pair if total is None else total + pair
+    return total
+
+
+def mixer_outputs_kernel(heads, shard, place_ref, *refs):
+    got_refs, (q_ref, k_ref, v_ref, g_ref, b_ref, d_ref, x_ref) = refs[:heads], refs[heads:]
+    width = heads * HEAD
+    lane_b = lax.broadcasted_iota(jnp.int32, (shard, 2 * heads), 1)
+    lane_d = lax.broadcasted_iota(jnp.int32, (shard, heads), 1)
+    betas = jnp.zeros((shard, 2 * heads), WIDE)
+    decays = jnp.zeros((shard, heads), WIDE)
+    for n in range(heads):
+        got_ref = got_refs[n]
+        h = place_ref[0, n]
+
+        def columns(step):
+            return pl.ds(pl.multiple_of(step * width + h * HEAD, HEAD), HEAD)
+
+        q_ref[:, columns(0)] = got_ref[:shard, 0:128].astype(WIDE)
+        for i in range(2):
+            k_ref[:, columns(i)] = got_ref[:shard, 128 + i * 128 : 256 + i * 128].astype(WIDE)
+            v_ref[:, columns(i)] = got_ref[:shard, 384 + i * 128 : 512 + i * 128].astype(WIDE)
+        g_ref[:, columns(0)] = got_ref[:shard, 640:768].astype(WIDE)
+        last = got_ref[:shard, 768:896].astype(WIDE)
+        betas = jnp.where(lane_b == h, last[:, 0:1], betas)
+        betas = jnp.where(lane_b == heads + h, last[:, 1:2], betas)
+        decays = jnp.where(lane_d == h, last[:, 2:3], decays)
+        x_ref[h] = got_ref[shard:, :].astype(WIDE)
+    b_ref[...] = betas
+    d_ref[...] = decays
+
+
+def mixer_outputs(found, shard):
+    heads = len(found)
+    places = jnp.stack([place for place, _ in found])[None].astype(jnp.int32)
+    rows = found[0][1].shape[0]
+    width = heads * HEAD
+    shape = jax.ShapeDtypeStruct
+    outs = (
+        shape((shard, width), WIDE),
+        shape((shard, 2 * width), WIDE),
+        shape((shard, 2 * width), WIDE),
+        shape((shard, width), WIDE),
+        shape((shard, 2 * heads), WIDE),
+        shape((shard, heads), WIDE),
+        shape((heads, rows - shard, 896), WIDE),
+    )
+    return pl.pallas_call(
+        functools.partial(mixer_outputs_kernel, heads, shard),
+        out_shape=outs,
+        in_specs=[smem_spec()] + [vmem_spec()] * heads,
+        out_specs=[vmem_spec()] * len(outs),
+        compiler_params=pltpu.CompilerParams(vmem_limit_bytes=VMEM_LIMIT),
+        cost_estimate=pl.CostEstimate(flops=0, bytes_accessed=12 * 2**20, transcendentals=0),
+        name="mixer_outputs",
+    )(places, *(value for _, value in found))
+
+
+def ff_outputs_kernel(seq, slab, shard, got_ref, gate_ref, up_ref, down_ref):
+    pieces = [got_ref[s].astype(WIDE) for s in range(seq)]
+    for ref, at in ((gate_ref, 0), (up_ref, slab)):
+        columns = [
+            p[at : at + slab, k * shard : (k + 1) * shard] for k in range(2) for p in pieces
+        ]
+        ref[...] = jnp.concatenate(columns, axis=0).T
+    down_ref[...] = jnp.concatenate([p[2 * slab :] for p in pieces], axis=0)
+
+
+def ff_outputs(got, slab, shard, fsdp):
+    seq, rows, width = got.shape
+    own = seq * slab
+    if slab % 8 or (2 * own) % 128 or (2 * shard) % 128 or fsdp % 2:
+        wide = got.astype(WIDE)
+
+        def turned(at):
+            part = wide[:, at : at + slab].reshape(seq, slab, fsdp, shard)
+            return jnp.transpose(part, (3, 2, 0, 1)).reshape(shard, fsdp * own)
+
+        return (
+            turned(0),
+            turned(slab),
+            wide[:, 2 * slab :].reshape(own, width),
+        )
+    shape = jax.ShapeDtypeStruct
+    return pl.pallas_call(
+        functools.partial(ff_outputs_kernel, seq, slab, shard),
+        out_shape=(
+            shape((shard, fsdp * own), WIDE),
+            shape((shard, fsdp * own), WIDE),
+            shape((own, width), WIDE),
+        ),
+        grid=(fsdp // 2,),
+        in_specs=[pl.BlockSpec((seq, rows, 2 * shard), lambda i: (0, 0, i))],
+        out_specs=(
+            pl.BlockSpec((shard, 2 * own), lambda i: (0, i)),
+            pl.BlockSpec((shard, 2 * own), lambda i: (0, i)),
+            pl.BlockSpec((own, 2 * shard), lambda i: (0, i)),
+        ),
+        compiler_params=pltpu.CompilerParams(vmem_limit_bytes=VMEM_LIMIT),
+        cost_estimate=pl.CostEstimate(flops=0, bytes_accessed=15 * 2**20, transcendentals=0),
+        name="ff_outputs",
+    )(got)
+
+
 def per_device(
     tokens, cotangent, offsets, gain_in, w_query, w_key, w_value, w_beta, w_decay, w_outgate,
     conv_query, conv_key, conv_value, decay_scale, gain_head, w_out, gain_ffn, w_gate, w_up,
@@ -460,10 +641,8 @@
     def gather_rows(value):
         return lax.all_gather(value, "fsdp", axis=0, tiled=True)
 
-    seq_tokens = lax.all_gather(
-        tokens[0], "seq", axis=0, tiled=True, axis_index_groups=team_groups
-    )
-    length = seq_tokens.shape[0]
+    found = spread_gather(tokens[0], heads)
+    length = heads * own_rows
 
     def head_columns(weights, step):
         return lax.dynamic_slice_in_dim(weights, step * width + head * HEAD, HEAD, axis=1)
@@ -489,7 +668,7 @@
         ],
         axis=1,
     )
-    full_packed = gather_rows(packed)
+
     vectors = jnp.concatenate(
         [
             gain_in[None],
@@ -503,7 +682,11 @@
         ],
         axis=0,
     )
-    vectors = lax.all_gather(vectors, "fsdp", axis=0)
+    extra_rows = 32
+    vectors = jnp.pad(vectors, ((0, extra_rows - vectors.shape[0]), (0, 896 - shard)))
+    got = ordered_gather(stack(packed, vectors), "fsdp")
+    full_packed = got[:, :shard].reshape(width, 896)
+    vectors = got[:, shard:, :shard]
     full_gain_in = vectors[:, 0].reshape(width).astype(WIDE)
     full_gain_ffn = vectors[:, 1].reshape(width).astype(WIDE)
     full_gain_head = vectors[:, 2, : gain_head.shape[0]].reshape(1, HEAD).astype(WIDE)
@@ -526,18 +709,24 @@
         axis=1,
     ).astype(WIDE)
     head_taps = jnp.pad(head_taps, ((0, 8 - taps), (0, 0)))
-    full_out = gather_rows(w_out)
+    full_out = ordered_gather(w_out, "fsdp").reshape(width, width)
 
     def to_columns(value):
         return lax.all_to_all(value, "fsdp", 1, 0, tiled=True)
 
     cols_gate, cols_up = to_columns(w_gate), to_columns(w_up)
-    group_cot = gather_rows(cotangent[0])
-
+    group_cot = near_gather(cotangent[0], "fsdp")
+
+    seq_tokens = jnp.zeros((length, width), LOW)
+    for at, rows in found:
+        seq_tokens = lax.dynamic_update_slice(seq_tokens, rows, (at * own_rows, 0))
     seq_wide = seq_tokens.astype(WIDE)
     normed_low = (rms_parts(seq_wide) * full_gain_in).astype(LOW)
     pre = dot_plain(normed_low, full_packed[:, :640]).astype(LOW)
     gate_small = dot_plain(normed_low, full_packed[:, 640:])
+    pre, full_out, cols_gate, cols_up, group_cot = lax.optimization_barrier(
+        (pre, full_out, cols_gate, cols_up, group_cot)
+    )
     offs = jnp.concatenate(
         [offsets, jnp.broadcast_to(team * length, (1, 1)).astype(jnp.int32)], axis=1
     )
@@ -577,7 +766,7 @@
 
     mid_normed = rms_parts(mixer_res)
     mid_low = (mid_normed * full_gain_ffn).astype(LOW)
-    group_mid = gather_rows(mid_low)
+    group_mid = near_gather(mid_low, "fsdp")
     gate_pre = dot_plain(group_mid, cols_gate)
     up_pre = dot_plain(group_mid, cols_up)
     sig = jax.nn.sigmoid(gate_pre)
@@ -587,13 +776,9 @@
     grad_gate_pre = (grad_hidden * up_pre * (sig * (1.0 + gate_pre * (1.0 - sig)))).astype(LOW)
     grad_up_pre = (grad_hidden * act).astype(LOW)
     grad_mid = dot_right(grad_gate_pre, cols_gate) + dot_right(grad_up_pre, cols_up)
-    grad_mid = lax.psum_scatter(
-        grad_mid.astype(LOW), "fsdp", scatter_dimension=0, tiled=True
-    ).astype(WIDE)
-    down_part = lax.psum_scatter(
-        dot_plain(hidden, w_down).astype(LOW), "fsdp", scatter_dimension=0, tiled=True
-    )
-    layer_out = (mixer_res + down_part.astype(WIDE)).astype(LOW)
+    grad_mid = near_scatter(grad_mid, "fsdp")
+    down_part = near_scatter(dot_plain(hidden, w_down), "fsdp")
+    layer_out = (mixer_res + down_part).astype(LOW)
 
     grad_res = cotangent[0].astype(WIDE) + rms_back(grad_mid * full_gain_ffn, mixer_res)
     grad_gain_ffn = jnp.sum(grad_mid * mid_normed, axis=0)
@@ -603,28 +788,25 @@
         grad_gated, "seq", 1, 0, tiled=True, axis_index_groups=team_groups
     )
 
-    grad_down = dot_left(hidden, group_cot, LOW)
-    grad_gate = dot_left(group_mid, grad_gate_pre, LOW)
-    grad_up = dot_left(group_mid, grad_up_pre, LOW)
-    grad_out = dot_left(gated_own, res_low, LOW)
-
-    def share(value):
-        return lax.psum_scatter(value, "seq", scatter_dimension=0, tiled=True)
-
-    def whole(value):
-        return lax.all_gather(value, "seq", axis=0, tiled=True)
-
-    def columns_done(value):
-        part = value.reshape(fsdp, seq, shard // seq, value.shape[1])
-        part = lax.psum_scatter(part, "seq", scatter_dimension=1, tiled=True)
-        part = part.reshape(shard // seq * fsdp, value.shape[1])
-        part = lax.all_to_all(part, "fsdp", 0, 1, tiled=True)
-        return whole(part).astype(WIDE)
-
-    out_gate, out_up = columns_done(grad_gate), columns_done(grad_up)
-    out_down = whole(share(grad_down)).astype(WIDE)
-    grad_out = lax.psum_scatter(grad_out, "fsdp", scatter_dimension=0, tiled=True)
-    out_out = lax.psum(grad_out, "seq").astype(WIDE)
+    own_ff = w_down.shape[0]
+    slab = own_ff // seq
+    slabs = jnp.concatenate(
+        [
+            dot_left(grad_gate_pre, group_mid, LOW).reshape(seq, slab, width),
+            dot_left(grad_up_pre, group_mid, LOW).reshape(seq, slab, width),
+            dot_left(hidden, group_cot, LOW).reshape(seq, slab, width),
+        ],
+        axis=1,
+    )
+    summed = lax.psum_scatter(
+        slabs.reshape(seq * 3 * slab, width), "seq", scatter_dimension=0, tiled=True
+    )
+    turned = lax.all_to_all(summed[: 2 * slab], "fsdp", 1, 1, tiled=True)
+    summed = stack(turned, summed[2 * slab :])
+    slabs = lax.all_gather(summed, "seq", axis=0)
+    out_gate, out_up, out_down = ff_outputs(slabs, slab, shard, fsdp)
+    grad_out = dot_left(gated_own, res_low, LOW).reshape(fsdp, shard, width)
+    grad_out = near_scatter(near_blocks(grad_out, "fsdp"), "fsdp").astype(LOW)
 
     def backward_from(dend):
         return run_backward(
@@ -645,15 +827,27 @@
         tail = (dy[-16:, :640].astype(WIDE) + from_next).astype(LOW)
         dy = lax.dynamic_update_slice(dy, tail, (length - 16, 0))
 
-    grad_normed = dot_right(dy, full_packed)
-    grad_gain_in = jnp.sum(grad_normed * rms_parts(seq_wide), axis=0)
-    grad_normed = lax.psum_scatter(
-        grad_normed.astype(LOW), "seq", scatter_dimension=0, tiled=True,
+    grad_packed = dot_left(normed_low, dy)
+    grad_gain_in = (
+        jnp.sum(grad_packed * full_packed.astype(WIDE), axis=1) / full_gain_in
+    )
+    out_rows = shard // heads
+
+    def token_block(at):
+        rows = lax.dynamic_slice_in_dim(dy, at * own_rows, own_rows, axis=0)
+        outs = lax.dynamic_slice_in_dim(grad_out, at * out_rows, out_rows, axis=0)
+        return stack(dot_right(rows, full_packed).astype(LOW), outs)
+
+    joined = spread_scatter(token_block, heads)
+    grad_normed, own_out = joined[:own_rows], joined[own_rows:].astype(LOW)
+    input_grad = (grad_res + rms_back(grad_normed * full_gain_in, inputs)).astype(LOW)
+    if teams > 1:
+        own_out = lax.psum(own_out, "seq", axis_index_groups=head_groups)
+    out_out = lax.all_to_all(
+        jnp.broadcast_to(own_out[None], (heads, out_rows, width)), "seq", 0, 0,
         axis_index_groups=team_groups,
-    ).astype(WIDE)
-    input_grad = (grad_res + rms_back(grad_normed * full_gain_in, inputs)).astype(LOW)
-
-    grad_packed = dot_left(normed_low, dy)
+    ).reshape(shard, width).astype(WIDE)
+
     extra = jnp.zeros((fsdp, 16, 896), WIDE)
     extra = extra.at[:, 0, :shard].set(grad_gain_in.reshape(fsdp, shard))
     extra = extra.at[:, 1, :shard].set(grad_gain_ffn.reshape(fsdp, shard))
@@ -661,29 +855,13 @@
     extra = extra.at[:, 2, :gh].set(dgain.reshape(fsdp, gh))
     extra = extra.at[:, 3, :HEAD].set(drate)
     extra = extra.at[:, 4 : 4 + taps, :640].set(dtaps[None, :taps])
-    combined = jnp.concatenate(
-        [grad_packed.reshape(fsdp, shard, 896), extra], axis=1
-    ).astype(LOW)
-    combined = lax.psum_scatter(
-        combined.reshape(fsdp * (shard + 16), 896), "fsdp", scatter_dimension=0, tiled=True
-    )
+    combined = jnp.concatenate([grad_packed.reshape(fsdp, shard, 896), extra], axis=1)
+    combined = near_scatter(near_blocks(combined.astype(LOW), "fsdp"), "fsdp").astype(LOW)
     if teams > 1:
         combined = lax.psum(combined, "seq", axis_index_groups=head_groups)
-    combined = lax.all_gather(combined, "seq", axis=0, axis_index_groups=team_groups)
-
-    def by_head(at):
-        return jnp.transpose(combined[:, :shard, at : at + HEAD], (1, 0, 2)).reshape(shard, width)
-
-    out_query = by_head(0).astype(WIDE)
-    out_key = jnp.concatenate([by_head(128), by_head(256)], axis=1).astype(WIDE)
-    out_value = jnp.concatenate([by_head(384), by_head(512)], axis=1).astype(WIDE)
-    out_gatew = by_head(640).astype(WIDE)
-    smalls = jnp.transpose(combined[:, :shard, 768:771], (1, 2, 0))
-    out_beta = smalls[:, 0:2].reshape(shard, 2 * heads).astype(WIDE)
-    out_decay = smalls[:, 2].astype(WIDE)
-    extras = combined[:, shard:].astype(WIDE)
-    if teams > 1:
-        pass
+    out_query, out_key, out_value, out_gatew, out_beta, out_decay, extras = mixer_outputs(
+        spread_gather(combined, heads), shard
+    )
     out_gain_in = jnp.sum(extras[:, 0, :shard], axis=0)
     out_gain_ffn = jnp.sum(extras[:, 1, :shard], axis=0)
     out_gain_head = jnp.sum(extras[:, 2, :gh], axis=0)

time: 1020 us -> 648 us (0.64)
  waiting for transfers between devices: 636 us -> 210 us
  starting transfers between devices: 29.1 us -> 70.1 us
  other arithmetic: 40.1 us -> 54.9 us
  matrix products: 69.9 us -> 57.3 us
    all_gather x9 -> x1, waiting for transfers between devices: 277 us -> 0.01 us  [per_device(): slabs = lax.all_gather(summed, 'seq', axis=0)]
    ppermute x0 -> x37, waiting for transfers between devices: none -> 189 us  [the longest x21 141 us: team_step(): return lax.ppermute(value, 'seq', pairs)]
    reduce_scatter x6 -> x1, waiting for transfers between devices: 164 us -> 0.02 us  [per_device(): lax.psum_scatter(slabs.reshape(seq * 3 * slab, width), 'seq', scatter_dim...]
    psum x1 -> x0, waiting for transfers between devices: 124 us -> none  [per_device(): out_out = lax.psum(grad_out, 'seq').astype(WIDE)]
    all_to_all x2, waiting for transfers between devices: 51.7 us -> 7.28 us  [to_columns(): return lax.all_to_all(value, 'fsdp', 1, 0, tiled=True)]
    ppermute x0 -> x37, starting transfers between devices: none -> 28.7 us  [the longest x21 20.2 us: team_step(): return lax.ppermute(value, 'seq', pairs)]
    all_to_all x1 -> x2, starting transfers between devices: 5.51 us -> 28.1 us  [the longest x1 24.6 us: per_device(): lax.all_to_all(jnp.broadcast_to(own_out[None], (heads, out_rows, width)),...]
    convert_element_type x10 -> x6, other arithmetic: 22.2 us -> 5.96 us  [the longest x1 2.19 us: per_device(): near_scatter(near_blocks(combined.astype(LOW), 'fsdp'), 'fsdp').astype(LOW)]
  transfers between devices with their start and end apart: 20 -> 44, of which waited for: 15 -> 20; matrix products, arithmetic and copies ran while one was open for 11% -> 23% of each run, Pallas kernels for 14% -> 10%
where the time goes in v2:
time: 648 us; the launch traced here: 642 us
  waiting for transfers between devices  210 us (32%)
  Pallas kernels  150 us (23%)
  starting transfers between devices  70.1 us (11%)
  local copies, waits for them, and re-layouts  63.7 us (10%)
  matrix products  57.3 us (9%)
  other arithmetic  54.9 us (8%)
  blocking collectives  19.8 us (3%)
  between operations  15.4 us (2%)
    ppermute x21, waiting for transfers between devices, team_step(): return lax.ppermute(value, 'seq', pairs)  141 us
    pallas_call x1, Pallas kernels, run_forward(): pl.pallas_call(functools.partial(forward_kernel, spans, offs.shape[1] - 1...  78.8 us
    pallas_call x1, Pallas kernels, run_backward(): pl.pallas_call(functools.partial(backward_kernel, spans, offs.shape[1] -...  60.3 us
    ppermute x16, waiting for transfers between devices, exchanged(): return lax.ppermute(value, axis, [(i, i ^ bit) for i in range(size)])  48.3 us
    dot_general x17, matrix products, contract(): lax.dot_general(left, right, (((left_dim,), (right_dim,)), ((), ())), pre...  34.4 us
    all_to_all x1, starting transfers between devices, per_device(): lax.all_to_all(jnp.broadcast_to(own_out[None], (heads, out_rows, width)),...  24.6 us
    dot_general x6, matrix products, dot_plain(): return jnp.dot(left, right, preferred_element_type=kind)  22.9 us
    ppermute x21, starting transfers between devices, team_step(): return lax.ppermute(value, 'seq', pairs)  20.2 us
  transfers between devices with their start and end apart: 44, of which 20 were waited for; matrix products, arithmetic and copies ran while one was open for 23% of the time, Pallas kernels for 10%

profile of v2, /device:TPU:0, one launch (start us, length us, event | category | flops | bytes accessed | tf_op | source)
XLA Modules:
  0.0 641.6 jit_solution(5628687470261574222)
XLA Ops:
  7.2 3.0 collective-permute-start.9
  24.1 2.5 copy.80
  26.6 3.6 all-to-all-start
  30.2 2.6 broadcast_in_dim.31
  34.8 2.5 copy.82
  37.4 2.2 collective-permute-start.5
  40.4 2.7 maximum_select_fusion.4
  43.0 2.8 maximum_select_fusion.5
  45.8 2.3 maximum_select_fusion.2
  52.7 22.5 %collective-permute-done.3 = bf16[256,1024]{1,0:T(8,128)(2,1)} collective-permute-done((bf16[256,1024]{1,0:T(8,128)(2,1)S(1)}, bf16[256,1024]{1,0:T(8,128)(2,1)}, u32[]{:S(2)}, u32[]{:S(2)}) %collective-permute-start.3) | collective-permute-done | bytes 524320 | tf_op jit(solution)/shard_map/ppermute | solution.py:492
  77.6 2.3 maximum_select_fusion.3
  82.6 4.3 all-to-all-start.1
  94.0 3.1 fusion
  98.4 7.3 %all-to-all-done.1 = bf16[256,4,704]{0,2,1:T(8,128)(2,1)} async-done(((bf16[256,4,704]{0,2,1:T(8,128)(2,1)}), bf16[256,4,704]{0,2,1:T(8,128)(2,1)}, u32[]{:S(2)}, u32[]{:S(2)}) %all-to-all-start.1) | async-done | bytes 1441824 | tf_op jit(solution)/shard_map/all_to_all | solution.py:715
  105.7 2.7 copy.99
  115.7 5.0 fusion.21.gs_ref
  123.3 7.7 %convolution_convert_fusion.pre_ref = bf16[2048,640]{1,0:T(8,128)(2,1)} fusion(bf16[1024,896]{1,0:T(8,128)(2,1)} %bitcast.177, bf16[2048,1024]{1,0:T(8,128)(2,1)} %constant_dynamic-update-slice_fusion, f32[1024]{0:T(1024)S(1)} %bitcast.207, f32[2048]{0:T(1024)S(1)} %add_rsqrt_fusion), kind=kOutput, calls=%fused_computation.11 | convolution fusion | flops 2694053888 | bytes 8138752 | tf_op jit(solution)/shard_map/dot_general | solution.py:427
  132.9 3.0 pad_maximum_fusion.1
  137.1 78.8 %delta_forward.1 = (bf16[2048,128]{1,0:T(8,128)(2,1)}, f32[2048,128]{1,0:T(8,128)}, f32[2048,640]{1,0:T(8,128)}, bf16[32,128,128]{2,1,0:T(8,128)(2,1)}, bf16[32,...) custom-call(s32[1,17]{1,0:T(1,128)} %pad_add_fusion.offs_ref, ...), custom_call_target="tpu_custom_call" | custom-call | flops 8053063680 | bytes 25165824 | tf_op jit(solution)/shard_map/delta_forward/pallas_call | solution.py:364
  218.0 19.8 %all_to_all.93 = bf16[8,256,128]{1,2,0:T(8,128)(2,1)S(1)} all-to-all(bf16[8,256,128]{1,2,0:T(8,128)(2,1)} %copy.86), channel_id=1, replica_groups=mesh['seq'=8,'fsdp'=4] {'seq'}, dimensions={0} | all-to-all | bytes 1048576 | tf_op jit(solution)/shard_map/all_to_all | solution.py:761
  241.8 11.8 %collective-permute-done.13 = bf16[256,1024]{1,0:T(8,128)(2,1)S(1)} collective-permute-done((bf16[256,1024]{1,0:T(8,128)(2,1)S(1)}, bf16[256,1024]{1,0:T(8,128)(2,1)S(1)}, u32[]{:S(2)}, u32[]{:S(2)}) %collective-permute-start.13) | collective-permute-done | bytes 524320 | tf_op jit(solution)/shard_map/ppermute | solution.py:440
  258.1 4.6 multiply_convert_fusion.1
  267.8 2.5 pad_maximum_fusion
  270.4 3.8 fusion.65
  283.6 11.7 %collective-permute-done.18 = bf16[256,1024]{1,0:T(8,128)(2,1)S(1)} collective-permute-done((bf16[256,1024]{1,0:T(8,128)(2,1)S(1)}, bf16[256,1024]{1,0:T(8,128)(2,1)S(1)}, u32[]{:S(2)}, u32[]{:S(2)}) %collective-permute-start.18) | collective-permute-done | bytes 524320 | tf_op jit(solution)/shard_map/ppermute | solution.py:440
  295.8 10.1 %collective-permute-done.16 = bf16[256,1024]{1,0:T(8,128)(2,1)S(1)} collective-permute-done((bf16[256,1024]{1,0:T(8,128)(2,1)S(1)}, bf16[256,1024]{1,0:T(8,128)(2,1)S(1)}, u32[]{:S(2)}, u32[]{:S(2)}) %collective-permute-start.16) | collective-permute-done | bytes 524320 | tf_op jit(solution)/shard_map/ppermute | solution.py:440
  305.9 2.3 multiply_add_fusion
  309.9 4.8 all-to-all-start.3
  317.1 11.9 %all-to-all-done.3 = bf16[256,8,128]{2,0,1:T(8,128)(2,1)S(1)} async-done(((bf16[256,8,128]{2,0,1:T(8,128)(2,1)}), bf16[256,8,128]{2,0,1:T(8,128)(2,1)S(1)}, u32[]{:S(2)}, u32[]{:S(2)}) %all-to-all-start.3) | async-done | bytes 524320 | tf_op jit(solution)/shard_map/all_to_all | solution.py:787
  329.7 60.3 %delta_backward.1 = (bf16[2048,896]{1,0:T(8,128)(2,1)}, f32[8,640]{1,0:T(8,128)}, f32[1,128]{1,0:T(1,128)}, f32[1,128]{1,0:T(1,128)}, f32[16,640]{1,0:T(8,128)}, /*index=5*/f32[128,128]{1,0:T(8,128)}) custom-call(s32[1,17]{1,0:T(1,128)} %pad_add_fusion.offs_ref, f32[1,1]{1,0:T(1,128)} %bitcast.2.rate_ref, bf16[2048,640]{1,0:T(8,128)(2,1)} %convolution_convert_fusion.pre_ref, ...), custom_call_target="tpu_custom_call" | custom-call | flops 10737418240 | bytes 25165824 | tf_op jit(solution)/shard_map/delta_backward/pallas_call | solution.py:395
  392.7 10.1 %multiply_reduce_fusion = (f32[1024]{0:T(1024)S(1)}, bf16[1024,896]{1,0:T(8,128)(2,1)}) fusion(bf16[4,256,896]{2,1,0:T(8,128)(2,1)} %slice.314, bf16[2048,896]{1,0:T(8,128)(2,1)} %get-tuple-element.121, bf16[2048,1024]{1,0:T(8,128)(2,1)} %constant_dynamic-update-slice_fusion, f32[1024]{0:T(1024)S(1)} %bitcast.208, f32[2048]{0:T(1024)S(1)} %copy-done.25), kind=kOutput, calls=%fused_computation.10 | convolution fusion | flops 3770153984 | bytes 11550720 | tf_op jit(solution)/shard_map/dot_general | solution.py:20
  406.0 3.5 all-to-all-start.5
  410.4 2.6 fusion.27
  419.9 2.5 convolution_convert_fusion.5
  430.1 12.4 %collective-permute-done.20 = bf16[256,1024]{1,0:T(8,128)(2,1)S(1)} collective-permute-done((bf16[256,1024]{1,0:T(8,128)(2,1)S(1)}, bf16[256,1024]{1,0:T(8,128)(2,1)S(1)}, u32[]{:S(2)}, u32[]{:S(2)}) %collective-permute-start.20) | collective-permute-done | bytes 524320 | tf_op jit(solution)/shard_map/ppermute | solution.py:440
  449.6 15.7 %collective-permute-done.21 = bf16[288,1024]{1,0:T(8,128)(2,1)S(1)} collective-permute-done((bf16[288,1024]{1,0:T(8,128)(2,1)S(1)}, bf16[288,1024]{1,0:T(8,128)(2,1)S(1)}, u32[]{:S(2)}, u32[]{:S(2)}) %collective-permute-start.21) | collective-permute-done | bytes 589856 | tf_op jit(solution)/shard_map/ppermute | solution.py:492
  465.6 25.0 %collective-permute-done.23 = bf16[288,1024]{1,0:T(8,128)(2,1)S(1)} collective-permute-done((bf16[288,1024]{1,0:T(8,128)(2,1)S(1)}, bf16[288,1024]{1,0:T(8,128)(2,1)S(1)}, u32[]{:S(2)}, u32[]{:S(2)}) %collective-permute-start.23) | collective-permute-done | bytes 589856 | tf_op jit(solution)/shard_map/ppermute | solution.py:492
  491.0 16.6 %collective-permute-done.25 = bf16[288,1024]{1,0:T(8,128)(2,1)S(1)} collective-permute-done((bf16[288,1024]{1,0:T(8,128)(2,1)S(1)}, bf16[288,1024]{1,0:T(8,128)(2,1)S(1)}, u32[]{:S(2)}, u32[]{:S(2)}) %collective-permute-start.25) | collective-permute-done | bytes 589856 | tf_op jit(solution)/shard_map/ppermute | solution.py:492
  510.4 2.4 convolution_convert_fusion.6
  515.5 3.7 collective-permute-done.27
  519.3 8.0 %collective-permute-done.22 = bf16[288,1024]{1,0:T(8,128)(2,1)} collective-permute-done((bf16[288,1024]{1,0:T(8,128)(2,1)S(1)}, bf16[288,1024]{1,0:T(8,128)(2,1)}, u32[]{:S(2)}, u32[]{:S(2)}) %collective-permute-start.22) | collective-permute-done | bytes 589856 | tf_op jit(solution)/shard_map/ppermute | solution.py:492
  528.7 11.1 %collective-permute-done.26 = bf16[288,1024]{1,0:T(8,128)(2,1)} collective-permute-done((bf16[288,1024]{1,0:T(8,128)(2,1)}, bf16[288,1024]{1,0:T(8,128)(2,1)}, u32[]{:S(2)}, u32[]{:S(2)}) %collective-permute-start.26) | collective-permute-done | bytes 589856 | tf_op jit(solution)/shard_map/ppermute | solution.py:492
  542.8 24.6 %all-to-all-start.4 = ((bf16[8,32,1024]{2,1,0:T(8,128)(2,1)}), bf16[8,32,1024]{2,1,0:T(8,128)(2,1)}, u32[]{:S(2)}, u32[]{:S(2)}) async-start(bf16[8,32,1024]{2,1,0:T(8,128)(2,1)} %broadcast_in_dim.79), calls=%async_computation.4 | async-start | bytes 1048576 | tf_op jit(solution)/shard_map/all_to_all | solution.py:846
  569.8 17.5 %collective-permute-done.33.refs_4_ = bf16[272,896]{1,0:T(8,128)(2,1)} collective-permute-done((bf16[272,896]{1,0:T(8,128)(2,1)}, bf16[272,896]{1,0:T(8,128)(2,1)}, u32[]{:S(2)}, u32[]{:S(2)}) %collective-permute-start.33) | collective-permute-done | bytes 487456 | tf_op jit(solution)/shard_map/ppermute | solution.py:492
  590.5 11.1 %collective-permute-done.34.refs_5_ = bf16[272,896]{1,0:T(8,128)(2,1)S(1)} collective-permute-done((bf16[272,896]{1,0:T(8,128)(2,1)}, bf16[272,896]{1,0:T(8,128)(2,1)S(1)}, u32[]{:S(2)}, u32[]{:S(2)}) %collective-permute-start.34) | collective-permute-done | bytes 487456 | tf_op jit(solution)/shard_map/ppermute | solution.py:492
  601.6 8.9 %collective-permute-done.32.refs_3_ = bf16[272,896]{1,0:T(8,128)(2,1)S(1)} collective-permute-done((bf16[272,896]{1,0:T(8,128)(2,1)}, bf16[272,896]{1,0:T(8,128)(2,1)S(1)}, u32[]{:S(2)}, u32[]{:S(2)}) %collective-permute-start.32) | collective-permute-done | bytes 487456 | tf_op jit(solution)/shard_map/ppermute | solution.py:492
  611.3 5.7 mixer_outputs.1
  629.2 5.4 ff_outputs.1
  (273 shorter events, 135.0 us)
Async XLA Ops:
  7.2 246.6 %copy-start = (bf16[704,1024]{1,0:T(8,128)(2,1)S(1)}, bf16[704,1024]{1,0:T(8,128)(2,1)}, u32[]{:S(2)}) copy-start(bf16[704,1024]{1,0:T(8,128)(2,1)} %param.49) | copy-start | bytes 4325380
  7.2 32.4 %collective-permute-start.9 = (bf16[1,256,1024]{2,1,0:T(8,128)(2,1)}, bf16[1,256,1024]{2,1,0:T(8,128)(2,1)}, u32[]{:S(2)}, u32[]{:S(2)}) collective-permute-start(bf16[1,256,1024]{2,1,0:T(8,128)(2,1)} %bitcast.173), channel_id=1, source_target_pairs={{0,2},{1,3},{2,0},{3,1},{4,6},{5,7},{6,4},{7,5},{8,10},{9,11},{10,... | collective-permute-start | bytes 1572872 | tf_op jit(solution)/shard_map/ppermute | solution.py:440
  19.0 18.4 %collective-permute-start.7 = (bf16[1,288,896]{2,1,0:T(8,128)(2,1)}, bf16[1,288,896]{2,1,0:T(8,128)(2,1)}, u32[]{:S(2)}, u32[]{:S(2)}) collective-permute-start(bf16[1,288,896]{2,1,0:T(8,128)(2,1)} %get-tuple-element.247), channel_id=1, source_target_pairs={{0,2},{1,3},{2,0},{3,1},{4,6},{5,7},{6,4},{7,5},{8,10},{9,11},{10,... | collective-permute-start | bytes 1548296 | tf_op jit(solution)/shard_map/ppermute | solution.py:440
  19.2 29.0 %collective-permute-start.1 = (bf16[256,1024]{1,0:T(8,128)(2,1)S(1)}, bf16[256,1024]{1,0:T(8,128)(2,1)}, u32[]{:S(2)}, u32[]{:S(2)}) collective-permute-start(bf16[256,1024]{1,0:T(8,128)(2,1)S(1)} %bitcast.156), channel_id=1, source_target_pairs={{0,8},{4,12},{8,16},{12,20},{16,24},{20,28},{24,0},{28,4},{1,9},{5... | collective-permute-start | bytes 1572872 | tf_op jit(solution)/shard_map/ppermute | solution.py:492
  21.1 29.9 %collective-permute-start = (bf16[256,1024]{1,0:T(8,128)(2,1)S(1)}, bf16[256,1024]{1,0:T(8,128)(2,1)}, u32[]{:S(2)}, u32[]{:S(2)}) collective-permute-start(bf16[256,1024]{1,0:T(8,128)(2,1)S(1)} %bitcast.157), channel_id=1, source_target_pairs={{0,4},{4,0},{8,12},{12,8},{16,20},{20,16},{24,28},{28,24},{1,5},{5... | collective-permute-start | bytes 1572872 | tf_op jit(solution)/shard_map/ppermute | solution.py:492
  22.6 25.6 %collective-permute-start.11 = (bf16[256,1024]{1,0:T(8,128)(2,1)}, bf16[256,1024]{1,0:T(8,128)(2,1)}, u32[]{:S(2)}, u32[]{:S(2)}) collective-permute-start(bf16[256,1024]{1,0:T(8,128)(2,1)} %bitcast.19), channel_id=1, source_target_pairs={{0,2},{1,3},{2,0},{3,1},{4,6},{5,7},{6,4},{7,5},{8,10},{9,11},{10,... | collective-permute-start | bytes 1572872 | tf_op jit(solution)/shard_map/ppermute | solution.py:440
  26.6 56.0 %all-to-all-start = ((bf16[256,4,704]{0,2,1:T(8,128)(2,1)}), bf16[256,4,704]{0,2,1:T(8,128)(2,1)S(1)}, u32[]{:S(2)}, u32[]{:S(2)}) async-start(bf16[256,4,704]{0,2,1:T(8,128)(2,1)} %bitcast.168), calls=%async_computation | async-start | bytes 2883584 | tf_op jit(solution)/shard_map/all_to_all | solution.py:715
  37.4 14.5 %collective-permute-start.5 = (bf16[256,1024]{1,0:T(8,128)(2,1)S(1)}, bf16[256,1024]{1,0:T(8,128)(2,1)}, u32[]{:S(2)}, u32[]{:S(2)}) collective-permute-start(bf16[256,1024]{1,0:T(8,128)(2,1)S(1)} %bitcast.158), channel_id=1, source_target_pairs={{0,24},{4,28},{8,0},{12,4},{16,8},{20,12},{24,16},{28,20},{1,25},{... | collective-permute-start | bytes 1572872 | tf_op jit(solution)/shard_map/ppermute | solution.py:492
  39.6 35.6 %collective-permute-start.3 = (bf16[256,1024]{1,0:T(8,128)(2,1)S(1)}, bf16[256,1024]{1,0:T(8,128)(2,1)}, u32[]{:S(2)}, u32[]{:S(2)}) collective-permute-start(bf16[256,1024]{1,0:T(8,128)(2,1)S(1)} %bitcast.159), channel_id=1, source_target_pairs={{0,16},{4,20},{8,24},{12,28},{16,0},{20,4},{24,8},{28,12},{1,17},{... | collective-permute-start | bytes 1572872 | tf_op jit(solution)/shard_map/ppermute | solution.py:492
  48.2 60.3 %collective-permute-start.8 = (bf16[2,288,896]{2,1,0:T(8,128)(2,1)}, bf16[2,288,896]{2,1,0:T(8,128)(2,1)}, u32[]{:S(2)}, u32[]{:S(2)}) collective-permute-start(bf16[2,288,896]{2,1,0:T(8,128)(2,1)} %maximum_select_fusion.5), channel_id=1, source_target_pairs={{0,1},{1,0},{2,3},{3,2},{4,5},{5,4},{6,7},{7,6},{8,9},{9,8},{10,11... | collective-permute-start | bytes 3096584 | tf_op jit(solution)/shard_map/ppermute | solution.py:440
  48.2 33.6 %collective-permute-start.2 = (bf16[256,1024]{1,0:T(8,128)(2,1)}, bf16[256,1024]{1,0:T(8,128)(2,1)S(1)}, u32[]{:S(2)}, u32[]{:S(2)}) collective-permute-start(bf16[256,1024]{1,0:T(8,128)(2,1)} %collective-permute-done.1), channel_id=1, source_target_pairs={{0,4},{4,0},{8,12},{12,8},{16,20},{20,16},{24,28},{28,24},{1,5},{5... | collective-permute-start | bytes 1572872 | tf_op jit(solution)/shard_map/ppermute | solution.py:492
  51.0 81.9 %collective-permute-start.12 = (bf16[512,1024]{1,0:T(8,128)(2,1)}, bf16[512,1024]{1,0:T(8,128)(2,1)}, u32[]{:S(2)}, u32[]{:S(2)}) collective-permute-start(bf16[512,1024]{1,0:T(8,128)(2,1)} %pad_maximum_fusion.3), channel_id=1, source_target_pairs={{0,1},{1,0},{2,3},{3,2},{4,5},{5,4},{6,7},{7,6},{8,9},{9,8},{10,11... | collective-permute-start | bytes 3145736 | tf_op jit(solution)/shard_map/ppermute | solution.py:440
  51.9 40.2 %collective-permute-start.6 = (bf16[256,1024]{1,0:T(8,128)(2,1)}, bf16[256,1024]{1,0:T(8,128)(2,1)}, u32[]{:S(2)}, u32[]{:S(2)}) collective-permute-start(bf16[256,1024]{1,0:T(8,128)(2,1)} %collective-permute-done.5), channel_id=1, source_target_pairs={{0,4},{4,0},{8,12},{12,8},{16,20},{20,16},{24,28},{28,24},{1,5},{5... | collective-permute-start | bytes 1572872 | tf_op jit(solution)/shard_map/ppermute | solution.py:492
  75.2 14.2 %collective-permute-start.4 = (bf16[256,1024]{1,0:T(8,128)(2,1)}, bf16[256,1024]{1,0:T(8,128)(2,1)S(1)}, u32[]{:S(2)}, u32[]{:S(2)}) collective-permute-start(bf16[256,1024]{1,0:T(8,128)(2,1)} %collective-permute-done.3), channel_id=1, source_target_pairs={{0,4},{4,0},{8,12},{12,8},{16,20},{20,16},{24,28},{28,24},{1,5},{5... | collective-permute-start | bytes 1572872 | tf_op jit(solution)/shard_map/ppermute | solution.py:492
  81.8 49.2 %collective-permute-start.10 = (bf16[2,256,1024]{2,1,0:T(8,128)(2,1)}, bf16[2,256,1024]{2,1,0:T(8,128)(2,1)}, u32[]{:S(2)}, u32[]{:S(2)}) collective-permute-start(bf16[2,256,1024]{2,1,0:T(8,128)(2,1)} %maximum_select_fusion.3), channel_id=1, source_target_pairs={{0,1},{1,0},{2,3},{3,2},{4,5},{5,4},{6,7},{7,6},{8,9},{9,8},{10,11... | collective-permute-start | bytes 3145736 | tf_op jit(solution)/shard_map/ppermute | solution.py:440
  82.6 23.1 %all-to-all-start.1 = ((bf16[256,4,704]{0,2,1:T(8,128)(2,1)}), bf16[256,4,704]{0,2,1:T(8,128)(2,1)}, u32[]{:S(2)}, u32[]{:S(2)}) async-start(bf16[256,4,704]{0,2,1:T(8,128)(2,1)} %bitcast.169), calls=%async_computation.1 | async-start | bytes 2883584 | tf_op jit(solution)/shard_map/all_to_all | solution.py:715
  87.0 317.3 %reduce-scatter.2.cloned.1.call-start = ((), (), s32[]{:S(2)}) async-start(), calls=%async_computation.7 | async-start | bytes 4866048 | tf_op jit(solution)/shard_map/reduce_scatter | solution.py:801
  97.1 26.2 %copy-start.24 = (f32[2048]{0:T(1024)}, f32[2048]{0:T(1024)S(1)}, u32[]{:S(2)}) copy-start(f32[2048]{0:T(1024)S(1)} %add_rsqrt_fusion) | copy-start | bytes 24580
  241.0 12.6 %collective-permute-start.13 = (bf16[256,1024]{1,0:T(8,128)(2,1)S(1)}, bf16[256,1024]{1,0:T(8,128)(2,1)S(1)}, u32[]{:S(2)}, u32[]{:S(2)}) collective-permute-start(bf16[256,1024]{1,0:T(8,128)(2,1)S(1)} %multiply_convert_fusion.3), channel_id=1, source_target_pairs={{0,2},{1,3},{2,0},{3,1},{4,6},{5,7},{6,4},{7,5},{8,10},{9,11},{10,... | collective-permute-start | bytes 1572872 | tf_op jit(solution)/shard_map/ppermute | solution.py:440
  253.7 2.7 collective-permute-start.14
  276.3 3.6 collective-permute-start.17
  279.7 2.7 collective-permute-start.15
  280.5 14.8 %collective-permute-start.18 = (bf16[256,1024]{1,0:T(8,128)(2,1)S(1)}, bf16[256,1024]{1,0:T(8,128)(2,1)S(1)}, u32[]{:S(2)}, u32[]{:S(2)}) collective-permute-start(bf16[256,1024]{1,0:T(8,128)(2,1)S(1)} %slice.397), channel_id=1, source_target_pairs={{0,2},{1,3},{2,0},{3,1},{4,6},{5,7},{6,4},{7,5},{8,10},{9,11},{10,... | collective-permute-start | bytes 1572872 | tf_op jit(solution)/shard_map/ppermute | solution.py:440
  282.9 23.0 %collective-permute-start.16 = (bf16[256,1024]{1,0:T(8,128)(2,1)S(1)}, bf16[256,1024]{1,0:T(8,128)(2,1)S(1)}, u32[]{:S(2)}, u32[]{:S(2)}) collective-permute-start(bf16[256,1024]{1,0:T(8,128)(2,1)S(1)} %slice.398), channel_id=1, source_target_pairs={{0,2},{1,3},{2,0},{3,1},{4,6},{5,7},{6,4},{7,5},{8,10},{9,11},{10,... | collective-permute-start | bytes 1572872 | tf_op jit(solution)/shard_map/ppermute | solution.py:440
  309.9 19.0 %all-to-all-start.3 = ((bf16[256,8,128]{2,0,1:T(8,128)(2,1)}), bf16[256,8,128]{2,0,1:T(8,128)(2,1)S(1)}, u32[]{:S(2)}, u32[]{:S(2)}) async-start(bf16[256,8,128]{2,0,1:T(8,128)(2,1)} %bitcast.149), calls=%async_computation.3 | async-start | bytes 1048576 | tf_op jit(solution)/shard_map/all_to_all | solution.py:787
  317.1 109.4 %collective-permute-start.19 = (bf16[512,1024]{1,0:T(8,128)(2,1)}, bf16[512,1024]{1,0:T(8,128)(2,1)}, u32[]{:S(2)}, u32[]{:S(2)}) collective-permute-start(bf16[512,1024]{1,0:T(8,128)(2,1)} %pad_maximum_fusion.5), channel_id=1, source_target_pairs={{0,1},{1,0},{2,3},{3,2},{4,5},{5,4},{6,7},{7,6},{8,9},{9,8},{10,11... | collective-permute-start | bytes 3145736 | tf_op jit(solution)/shard_map/ppermute | solution.py:440
  329.7 62.9 %copy-start.25 = (f32[2048]{0:T(1024)S(1)}, f32[2048]{0:T(1024)}, u32[]{:S(2)}) copy-start(f32[2048]{0:T(1024)} %copy-done.24) | copy-start | bytes 24580
  406.0 10.5 %all-to-all-start.5 = ((bf16[176,4,256]{2,0,1:T(8,128)(2,1)}), bf16[176,4,256]{2,0,1:T(8,128)(2,1)S(1)}, u32[]{:S(2)}, u32[]{:S(2)}) async-start(bf16[176,4,256]{2,0,1:T(8,128)(2,1)} %bitcast.150), calls=%async_computation.6 | async-start | bytes 720896 | tf_op jit(solution)/shard_map/all_to_all | solution.py:804
  409.5 219.7 %all-gather.3.cloned.1.call-start = ((), (), s32[]{:S(2)}) async-start(), calls=%async_computation.8 | async-start | bytes 4866048 | tf_op jit(solution)/shard_map/all_gather | solution.py:806
  419.8 28.3 %collective-permute-start.28 = (bf16[544,896]{1,0:T(8,128)(2,1)S(1)}, bf16[544,896]{1,0:T(8,128)(2,1)S(1)}, u32[]{:S(2)}, u32[]{:S(2)}) collective-permute-start(bf16[544,896]{1,0:T(8,128)(2,1)S(1)} %pad_maximum_fusion.6), channel_id=1, source_target_pairs={{0,1},{1,0},{2,3},{3,2},{4,5},{5,4},{6,7},{7,6},{8,9},{9,8},{10,11... | collective-permute-start | bytes 2924552 | tf_op jit(solution)/shard_map/ppermute | solution.py:440
  428.2 14.4 %collective-permute-start.20 = (bf16[256,1024]{1,0:T(8,128)(2,1)S(1)}, bf16[256,1024]{1,0:T(8,128)(2,1)S(1)}, u32[]{:S(2)}, u32[]{:S(2)}) collective-permute-start(bf16[256,1024]{1,0:T(8,128)(2,1)S(1)} %slice.396), channel_id=1, source_target_pairs={{0,2},{1,3},{2,0},{3,1},{4,6},{5,7},{6,4},{7,5},{8,10},{9,11},{10,... | collective-permute-start | bytes 1572872 | tf_op jit(solution)/shard_map/ppermute | solution.py:440
  442.8 22.4 %collective-permute-start.21 = (bf16[288,1024]{1,0:T(8,128)(2,1)S(1)}, bf16[288,1024]{1,0:T(8,128)(2,1)S(1)}, u32[]{:S(2)}, u32[]{:S(2)}) collective-permute-start(bf16[288,1024]{1,0:T(8,128)(2,1)S(1)} %pad_maximum_fusion.7), channel_id=1, source_target_pairs={{0,4},{4,0},{8,12},{12,8},{16,20},{20,16},{24,28},{28,24},{1,5},{5... | collective-permute-start | bytes 1769480 | tf_op jit(solution)/shard_map/ppermute | solution.py:492
  444.4 46.2 %collective-permute-start.23 = (bf16[288,1024]{1,0:T(8,128)(2,1)S(1)}, bf16[288,1024]{1,0:T(8,128)(2,1)S(1)}, u32[]{:S(2)}, u32[]{:S(2)}) collective-permute-start(bf16[288,1024]{1,0:T(8,128)(2,1)S(1)} %pad_maximum_fusion.8), channel_id=1, source_target_pairs={{0,4},{4,0},{8,12},{12,8},{16,20},{20,16},{24,28},{28,24},{1,5},{5... | collective-permute-start | bytes 1769480 | tf_op jit(solution)/shard_map/ppermute | solution.py:492
  445.1 62.5 %collective-permute-start.25 = (bf16[288,1024]{1,0:T(8,128)(2,1)S(1)}, bf16[288,1024]{1,0:T(8,128)(2,1)S(1)}, u32[]{:S(2)}, u32[]{:S(2)}) collective-permute-start(bf16[288,1024]{1,0:T(8,128)(2,1)S(1)} %pad_maximum_fusion.9), channel_id=1, source_target_pairs={{0,4},{4,0},{8,12},{12,8},{16,20},{20,16},{24,28},{28,24},{1,5},{5... | collective-permute-start | bytes 1769480 | tf_op jit(solution)/shard_map/ppermute | solution.py:492
  447.4 71.7 %collective-permute-start.27 = (bf16[288,1024]{1,0:T(8,128)(2,1)}, bf16[288,1024]{1,0:T(8,128)(2,1)}, u32[]{:S(2)}, u32[]{:S(2)}) collective-permute-start(bf16[288,1024]{1,0:T(8,128)(2,1)} %pad_maximum_fusion.10), channel_id=1, source_target_pairs={{0,4},{4,0},{8,12},{12,8},{16,20},{20,16},{24,28},{28,24},{1,5},{5... | collective-permute-start | bytes 1769480 | tf_op jit(solution)/shard_map/ppermute | solution.py:492
  448.3 42.5 %copy-start.7 = (f32[544,896]{1,0:T(8,128)}, f32[544,896]{1,0:T(8,128)S(1)}, u32[]{:S(2)}) copy-start(f32[544,896]{1,0:T(8,128)S(1)} %convert_add_fusion.1) | copy-start | bytes 5849092
  449.2 63.7 %collective-permute-start.29 = (bf16[272,896]{1,0:T(8,128)(2,1)}, bf16[272,896]{1,0:T(8,128)(2,1)}, u32[]{:S(2)}, u32[]{:S(2)}) collective-permute-start(bf16[272,896]{1,0:T(8,128)(2,1)} %slice.399), channel_id=1, source_target_pairs={{0,2},{1,3},{2,0},{3,1},{4,6},{5,7},{6,4},{7,5},{8,10},{9,11},{10,... | collective-permute-start | bytes 1462280 | tf_op jit(solution)/shard_map/ppermute | solution.py:440
  465.5 61.8 %collective-permute-start.22 = (bf16[288,1024]{1,0:T(8,128)(2,1)S(1)}, bf16[288,1024]{1,0:T(8,128)(2,1)}, u32[]{:S(2)}, u32[]{:S(2)}) collective-permute-start(bf16[288,1024]{1,0:T(8,128)(2,1)S(1)} %add_convert_fusion.2), channel_id=1, source_target_pairs={{0,16},{4,20},{8,24},{12,28},{16,0},{20,4},{24,8},{28,12},{1,17},{... | collective-permute-start | bytes 1769480 | tf_op jit(solution)/shard_map/ppermute | solution.py:492
  490.8 36.5 %collective-permute-start.24 = (bf16[288,1024]{1,0:T(8,128)(2,1)S(1)}, bf16[288,1024]{1,0:T(8,128)(2,1)}, u32[]{:S(2)}, u32[]{:S(2)}) collective-permute-start(bf16[288,1024]{1,0:T(8,128)(2,1)S(1)} %add_convert_fusion.1), channel_id=1, source_target_pairs={{0,8},{4,12},{8,16},{12,20},{16,24},{20,28},{24,0},{28,4},{1,9},{5... | collective-permute-start | bytes 1769480 | tf_op jit(solution)/shard_map/ppermute | solution.py:492
  508.6 31.2 %collective-permute-start.26 = (bf16[288,1024]{1,0:T(8,128)(2,1)}, bf16[288,1024]{1,0:T(8,128)(2,1)}, u32[]{:S(2)}, u32[]{:S(2)}) collective-permute-start(bf16[288,1024]{1,0:T(8,128)(2,1)} %add_convert_fusion), channel_id=1, source_target_pairs={{0,24},{4,28},{8,0},{12,4},{16,8},{20,12},{24,16},{28,20},{1,25},{... | collective-permute-start | bytes 1769480 | tf_op jit(solution)/shard_map/ppermute | solution.py:492
  515.0 52.7 %collective-permute-start.35 = (bf16[272,896]{1,0:T(8,128)(2,1)}, bf16[272,896]{1,0:T(8,128)(2,1)}, u32[]{:S(2)}, u32[]{:S(2)}) collective-permute-start(bf16[272,896]{1,0:T(8,128)(2,1)} %fusion.18.refs_0_), channel_id=1, source_target_pairs={{0,24},{4,28},{8,0},{12,4},{16,8},{20,12},{24,16},{28,20},{1,25},{... | collective-permute-start | bytes 1462280 | tf_op jit(solution)/shard_map/ppermute | solution.py:492
  519.2 68.2 %collective-permute-start.33 = (bf16[272,896]{1,0:T(8,128)(2,1)}, bf16[272,896]{1,0:T(8,128)(2,1)}, u32[]{:S(2)}, u32[]{:S(2)}) collective-permute-start(bf16[272,896]{1,0:T(8,128)(2,1)} %fusion.18.refs_0_), channel_id=1, source_target_pairs={{0,16},{4,20},{8,24},{12,28},{16,0},{20,4},{24,8},{28,12},{1,17},{... | collective-permute-start | bytes 1462280 | tf_op jit(solution)/shard_map/ppermute | solution.py:492
  527.3 61.5 %collective-permute-start.31 = (bf16[272,896]{1,0:T(8,128)(2,1)}, bf16[272,896]{1,0:T(8,128)(2,1)}, u32[]{:S(2)}, u32[]{:S(2)}) collective-permute-start(bf16[272,896]{1,0:T(8,128)(2,1)} %fusion.18.refs_0_), channel_id=1, source_target_pairs={{0,8},{4,12},{8,16},{12,20},{16,24},{20,28},{24,0},{28,4},{1,9},{5... | collective-permute-start | bytes 1462280 | tf_op jit(solution)/shard_map/ppermute | solution.py:492
  527.3 63.2 %collective-permute-start.30 = (bf16[272,896]{1,0:T(8,128)(2,1)}, bf16[272,896]{1,0:T(8,128)(2,1)}, u32[]{:S(2)}, u32[]{:S(2)}) collective-permute-start(bf16[272,896]{1,0:T(8,128)(2,1)} %fusion.18.refs_0_), channel_id=1, source_target_pairs={{0,4},{4,0},{8,12},{12,8},{16,20},{20,16},{24,28},{28,24},{1,5},{5... | collective-permute-start | bytes 1462280 | tf_op jit(solution)/shard_map/ppermute | solution.py:492
  542.8 84.3 %all-to-all-start.4 = ((bf16[8,32,1024]{2,1,0:T(8,128)(2,1)}), bf16[8,32,1024]{2,1,0:T(8,128)(2,1)}, u32[]{:S(2)}, u32[]{:S(2)}) async-start(bf16[8,32,1024]{2,1,0:T(8,128)(2,1)} %broadcast_in_dim.79), calls=%async_computation.4 | async-start | bytes 1048576 | tf_op jit(solution)/shard_map/all_to_all | solution.py:846
  567.7 22.8 %collective-permute-start.36 = (bf16[272,896]{1,0:T(8,128)(2,1)}, bf16[272,896]{1,0:T(8,128)(2,1)S(1)}, u32[]{:S(2)}, u32[]{:S(2)}) collective-permute-start(bf16[272,896]{1,0:T(8,128)(2,1)} %collective-permute-done.35.refs_6_), channel_id=1, source_target_pairs={{0,4},{4,0},{8,12},{12,8},{16,20},{20,16},{24,28},{28,24},{1,5},{5... | collective-permute-start | bytes 1462280 | tf_op jit(solution)/shard_map/ppermute | solution.py:492
  587.3 14.3 %collective-permute-start.34 = (bf16[272,896]{1,0:T(8,128)(2,1)}, bf16[272,896]{1,0:T(8,128)(2,1)S(1)}, u32[]{:S(2)}, u32[]{:S(2)}) collective-permute-start(bf16[272,896]{1,0:T(8,128)(2,1)} %collective-permute-done.33.refs_4_), channel_id=1, source_target_pairs={{0,4},{4,0},{8,12},{12,8},{16,20},{20,16},{24,28},{28,24},{1,5},{5... | collective-permute-start | bytes 1462280 | tf_op jit(solution)/shard_map/ppermute | solution.py:492
  588.7 21.8 %collective-permute-start.32 = (bf16[272,896]{1,0:T(8,128)(2,1)}, bf16[272,896]{1,0:T(8,128)(2,1)S(1)}, u32[]{:S(2)}, u32[]{:S(2)}) collective-permute-start(bf16[272,896]{1,0:T(8,128)(2,1)} %collective-permute-done.31.refs_2_), channel_id=1, source_target_pairs={{0,4},{4,0},{8,12},{12,8},{16,20},{20,16},{24,28},{28,24},{1,5},{5... | collective-permute-start | bytes 1462280 | tf_op jit(solution)/shard_map/ppermute | solution.py:492
  (32 other events, 181.0 us)
Sparse Core Ops, SparseCore 0:
  270.5 92.4 reduce-scatter.1
  418.5 112.2 all-gather.2

commit v3 on v2

v3 whole, which is shorter than its diff:
```python
import functools

import jax
import jax.numpy as jnp
from jax import lax
from jax.experimental import pallas as pl
from jax.experimental.pallas import tpu as pltpu
from jax.sharding import PartitionSpec as P

SPAN = 64
ROWS = 128
HEAD = 128
EPSILON = 1e-06
LOW = jnp.bfloat16
WIDE = jnp.float32
VMEM_LIMIT = 56 * 1024 * 1024


def contract(left, right, left_dim, right_dim):
    return lax.dot_general(
        left, right, (((left_dim,), (right_dim,)), ((), ())), preferred_element_type=WIDE
    )


def halves(value):
    high = value.astype(LOW)
    return high, (value - high.astype(WIDE)).astype(LOW)


def mm(left, right, left_dim=1, right_dim=0):
    return contract(left.astype(LOW), right.astype(LOW), left_dim, right_dim)


def mm3(left, right, left_dim=1, right_dim=0):
    lh, ll = halves(left)
    rh, rl = halves(right)
    return (
        contract(lh, rh, left_dim, right_dim)
        + contract(lh, rl, left_dim, right_dim)
        + contract(ll, rh, left_dim, right_dim)
    )


def stack(*parts):
    return jnp.concatenate(parts, axis=0)


def row_maps():
    row = lax.broadcasted_iota(jnp.int32, (ROWS, ROWS), 0)
    col = lax.broadcasted_iota(jnp.int32, (ROWS, ROWS), 1)
    tok, step = row & (SPAN - 1), row >> 6
    tok_c, step_c = col & (SPAN - 1), col >> 6
    return tok, step, tok_c, step_c


def span_tokens(offs_ref, doc_count, first):
    place = first + lax.broadcasted_iota(jnp.int32, (SPAN, 1), 0)
    begin = jnp.zeros((SPAN, 1), jnp.int32)
    for j in range(doc_count):
        start = offs_ref[0, j]
        begin = jnp.where(place >= start, start, begin)
    return place - begin


def softplus(value):
    return jnp.maximum(value, 0.0) + jnp.log1p(jnp.exp(-jnp.abs(value)))


def decay_sums(small, rate):
    logs = -rate * softplus(small)
    tok = lax.broadcasted_iota(jnp.int32, (SPAN, SPAN), 0)
    tok_c = lax.broadcasted_iota(jnp.int32, (SPAN, SPAN), 1)
    lower = jnp.where(tok >= tok_c, 1.0, 0.0).astype(LOW)
    tok_w = lax.broadcasted_iota(jnp.int32, (SPAN, ROWS), 0)
    tok_wc = lax.broadcasted_iota(jnp.int32, (SPAN, ROWS), 1) & (SPAN - 1)
    upper = jnp.where(tok_w <= tok_wc, 1.0, 0.0).astype(LOW)
    high, rest = halves(logs)
    cols = contract(lower, high, 1, 0) + contract(lower, rest, 1, 0)
    rows = contract(high, upper, 0, 0) + contract(rest, upper, 0, 0)
    return cols[:, 2:3], rows[2:3, :]


def unit(values):
    scale = lax.rsqrt(jnp.sum(values * values, axis=1, keepdims=True) + EPSILON)
    return values * scale, scale


def span_factors(small, rate, pos):
    sig = jax.nn.sigmoid(small)
    cum, cum_row = decay_sums(small, rate)
    beta = stack(sig[:, 0:1], sig[:, 1:2])
    cum2, pos2 = stack(cum, cum), stack(pos, pos)
    tok, step, tok_c, step_c = row_maps()
    before = tok > tok_c
    here = tok == tok_c
    reach = (before | (here & (step >= step_c))) & (tok - tok_c <= pos2)
    decay = jnp.where(reach, jnp.exp(jnp.where(reach, cum2 - cum_row, 0.0)), 0.0)
    strict = before | (here & (step > step_c))
    tok1 = tok[:, 0:1]
    carry = jnp.where(pos2 > tok1, jnp.exp(cum2), 0.0)
    end, end_pos = cum[SPAN - 1 : SPAN], pos[SPAN - 1 : SPAN]
    leave = jnp.where(SPAN - 1 - tok1 <= end_pos, jnp.exp(end - cum2), 0.0)
    carry_all = jnp.where(end_pos >= SPAN, jnp.exp(end), 0.0)
    return beta, decay, strict, carry, leave, carry_all, tok ^ tok_c


def unit_lower_inverse(strict_part, apart):
    row = lax.broadcasted_iota(jnp.int32, (ROWS, ROWS), 0)
    col = lax.broadcasted_iota(jnp.int32, (ROWS, ROWS), 1)
    inverse = jnp.where(row == col, 1.0, 0.0) - jnp.where(apart == 0, strict_part, 0.0)
    for level in range(6):
        block = jnp.where((apart >> level) == 1, strict_part, 0.0)
        inverse = inverse - mm(mm(inverse, block), inverse)
    return inverse


def conv_rows(prior, here):
    return stack(prior.astype(WIDE), here.astype(WIDE))


def forward_kernel(
    span_count, doc_count, group,
    offs_ref, rate_ref, pre_ref, prior_ref, small_ref, gate_ref, edge_ref, taps_ref, gain_ref,
    state_ref,
    conv_ref, t_ref, sc_ref, qh_ref, a_ref, gated_ref, mixed_ref, u_ref, s_ref, end_ref,
    w_scr, u0_scr, b_scr, o0_scr, a_scr, qh_scr,
):
    step = pl.program_id(0)
    base = offs_ref[0, doc_count]
    rate = rate_ref[0, 0]
    prior = jnp.where(step == 0, edge_ref[...].astype(WIDE), prior_ref[...].astype(WIDE))

    for u in range(group):
        c = step * group + u
        here = pre_ref[u * SPAN : (u + 1) * SPAN, :].astype(WIDE)
        if u:
            prior = pre_ref[u * SPAN - 16 : u * SPAN, :].astype(WIDE)
        rows = stack(prior, here)
        pos = span_tokens(offs_ref, doc_count, base + c * SPAN)
        conv = taps_ref[0:1, :] * here
        for lag in range(1, 4):
            shifted = rows[16 - lag : 16 - lag + SPAN]
            conv = conv + jnp.where(pos >= lag, taps_ref[lag : lag + 1, :] * shifted, 0.0)
        conv_ref[u * SPAN : (u + 1) * SPAN, :] = conv
        act = conv * jax.nn.sigmoid(conv)
        query, _ = unit(act[:, 0:128])
        key0, _ = unit(act[:, 128:256])
        key1, _ = unit(act[:, 256:384])
        keys = stack(key0, key1)
        values = stack(act[:, 384:512], act[:, 512:640])
        small = small_ref[u * SPAN : (u + 1) * SPAN, :]
        beta, decay, strict, carry, leave, carry_all, apart = span_factors(small, rate, pos)
        inner = mm(keys, keys, 1, 1)
        inverse = unit_lower_inverse(jnp.where(strict, beta * decay * inner, 0.0), apart)
        t_ref[u] = inverse.astype(LOW)
        both = mm(inverse, jnp.concatenate([(beta * carry) * keys, beta * values], axis=1))
        weight, fresh = both[:, :HEAD], both[:, HEAD:]
        w_scr[c] = weight.astype(LOW)
        u0_scr[c] = fresh
        leaving = (keys * leave).astype(LOW)
        row = lax.broadcasted_iota(jnp.int32, (HEAD, HEAD), 0)
        col = lax.broadcasted_iota(jnp.int32, (HEAD, HEAD), 1)
        step_map = jnp.where(row == col, carry_all, 0.0) - mm(leaving, weight, 0, 0)
        a_ref[u] = step_map
        a_scr[c] = step_map
        b_scr[c] = mm(fresh, leaving, 0, 0)
        scores = mm(query, keys, 1, 1) * decay[SPAN:, :]
        sc_ref[u] = scores.astype(LOW)
        mixed_both = mm(scores, both)
        reach = (carry[SPAN:] * query - mixed_both[:, :HEAD]).astype(LOW)
        qh_ref[u] = reach
        qh_scr[c] = reach
        o0_scr[c] = mixed_both[:, HEAD:]

    def chain(c, state):
        s_ref[c] = state
        low = state.astype(LOW)
        u_ref[c] = (u0_scr[c] - contract(w_scr[c], low, 1, 1)).astype(LOW)
        mixed = o0_scr[c] + contract(qh_scr[c], low, 1, 1)
        lo = pl.multiple_of(c * SPAN, SPAN)
        mixed_ref[pl.ds(lo, SPAN), :] = mixed
        gate = gate_ref[pl.ds(lo, SPAN), :]
        scale = lax.rsqrt(jnp.mean(mixed * mixed, axis=1, keepdims=True) + EPSILON)
        gated_ref[pl.ds(lo, SPAN), :] = (
            mixed * scale * gain_ref[...] * (gate * jax.nn.sigmoid(gate))
        ).astype(LOW)
        return mm3(state, a_scr[c], 1, 1) + b_scr[c]

    def chain_step(i, state):
        for u in range(4):
            state = chain(i * 4 + u, state)
        return state

    @pl.when(step == pl.num_programs(0) - 1)
    def _():
        end_ref[...] = lax.fori_loop(0, span_count // 4, chain_step, state_ref[...])


def gate_back_kernel(
    span_count,
    gate_ref, gain_ref, mixed_ref, qh_ref, a_ref, dgated_ref, dend_ref,
    do_ref, ds_ref, dgate_ref, dgain_ref, dbegin_ref,
    f_scr,
):
    dgain_ref[...] = jnp.zeros_like(dgain_ref)

    def gate_back(c):
        lo = pl.multiple_of(c * SPAN, SPAN)
        mixed = mixed_ref[pl.ds(lo, SPAN), :]
        gate = gate_ref[pl.ds(lo, SPAN), :]
        scale = lax.rsqrt(jnp.mean(mixed * mixed, axis=1, keepdims=True) + EPSILON)
        normed = mixed * scale
        sig = jax.nn.sigmoid(gate)
        grad = dgated_ref[pl.ds(lo, SPAN), :].astype(WIDE)
        by_gain = grad * normed
        dgate_ref[pl.ds(lo, SPAN), :] = (
            by_gain * gain_ref[...] * (sig * (1.0 + gate * (1.0 - sig)))
        ).astype(LOW)
        dgain_ref[...] += jnp.sum(by_gain * (gate * sig), axis=0, keepdims=True)
        dn = grad * (gate * sig) * gain_ref[...]
        dmixed = scale * (dn - normed * jnp.mean(dn * normed, axis=1, keepdims=True))
        do_low = dmixed.astype(LOW)
        do_ref[c] = do_low
        f_scr[c] = contract(do_low, qh_ref[c], 0, 0)

    def gate_step(i, none):
        for u in range(4):
            gate_back(i * 4 + u)
        return none

    lax.fori_loop(0, span_count // 4, gate_step, 0)

    def chain_step(i, grad):
        for u in range(4):
            c = span_count - 1 - (i * 4 + u)
            ds_ref[c] = grad
            grad = mm3(grad, a_ref[c]) + f_scr[c]
        return grad

    dbegin_ref[...] = lax.fori_loop(0, span_count // 4, chain_step, dend_ref[...])


def backward_kernel(
    at_block, doc_count,
    offs_ref, rate_ref, pre_ref, prior_ref, small_ref, edge_ref, taps_ref,
    conv_ref, t_ref, u_ref, sc_ref, s_ref, do_ref, ds_ref, dgate_ref,
    next_in, dtaps_in, drate_in, *refs,
):
    dy_ref, next_ref, dtaps_ref, drate_ref = refs[-4:]
    block = at_block(pl.program_id(0))
    base = offs_ref[0, doc_count]
    rate = rate_ref[0, 0]

    @pl.when(pl.program_id(0) == 0)
    def _():
        next_ref[...] = next_in[...]
        dtaps_ref[...] = dtaps_in[...]
        drate_ref[...] = drate_in[...]

    dy_ref[:, 640:768] = dgate_ref[...]
    for n in (1, 0):
        lo, hi = n * SPAN, (n + 1) * SPAN
        pos = span_tokens(offs_ref, doc_count, base + block * 2 * SPAN + lo)
        conv = conv_ref[lo:hi, :]
        sig = jax.nn.sigmoid(conv)
        act = conv * sig
        query, scale_q = unit(act[:, 0:128])
        key0, scale_0 = unit(act[:, 128:256])
        key1, scale_1 = unit(act[:, 256:384])
        keys = stack(key0, key1)
        values = stack(act[:, 384:512], act[:, 512:640])
        small = small_ref[lo:hi, :]
        beta, decay, strict, carry, leave, carry_all, _ = span_factors(small, rate, pos)
        state, dstate = s_ref[n], ds_ref[n]
        state_l, dstate_l = state.astype(LOW), dstate.astype(LOW)
        upd, out_grad, keys_l = u_ref[n], do_ref[n], keys.astype(LOW)
        dupd = contract(sc_ref[n], out_grad, 0, 0) + mm(keys * leave, dstate_l, 1, 1)
        dtarget = mm(t_ref[n], dupd, 0, 0)
        pair = stack(dtarget.astype(LOW), out_grad)
        by_upd = contract(pair, upd, 1, 1)
        by_state = contract(pair, state_l, 1, 0)
        dinner = jnp.where(strict, -by_upd[:ROWS] * decay, 0.0)
        dscore = by_upd[ROWS:] * decay[SPAN:, :]
        both = stack(dinner, dscore).astype(LOW)
        reading = contract(both, keys_l, 1, 0)
        read_key = reading[:ROWS] - carry * by_state[:ROWS]
        dquery = reading[ROWS:] + carry[SPAN:] * by_state[ROWS:]
        dleave = leave * contract(upd, dstate_l, 1, 0)
        write_key = contract(both, stack(beta * keys, query).astype(LOW), 0, 0) + dleave
        key_read = jnp.sum(keys * read_key, axis=1, keepdims=True)
        dbeta = jnp.sum(dtarget * values, axis=1, keepdims=True) + key_read
        dcum = beta * key_read - jnp.sum(keys * write_key, axis=1, keepdims=True)
        dcum = dcum[:SPAN] + dcum[SPAN:] + jnp.sum(query * dquery, axis=1, keepdims=True)
        through = jnp.sum(keys * dleave, axis=0, keepdims=True) + carry_all * jnp.sum(
            dstate * state, axis=0, keepdims=True
        )
        through = jnp.sum(through, axis=1, keepdims=True)
        tok1 = lax.broadcasted_iota(jnp.int32, (SPAN, 1), 0)
        dcum = dcum + jnp.where(tok1 == SPAN - 1, through, 0.0)
        tok = lax.broadcasted_iota(jnp.int32, (SPAN, SPAN), 0)
        tok_c = lax.broadcasted_iota(jnp.int32, (SPAN, SPAN), 1)
        upper = jnp.where(tok <= tok_c, 1.0, 0.0).astype(LOW)
        high, rest = halves(jnp.broadcast_to(dcum, (SPAN, 128)))
        dlog = contract(upper, high, 1, 0) + contract(upper, rest, 1, 0)
        soft = softplus(small)
        sig_small = jax.nn.sigmoid(small)
        lane = lax.broadcasted_iota(jnp.int32, (SPAN, 128), 1)
        drate_ref[...] += jnp.sum(jnp.where(lane == 2, -dlog * soft, 0.0), axis=0, keepdims=True)
        dsig = jnp.where(lane == 0, dbeta[:SPAN], dbeta[SPAN:]) * sig_small * (1.0 - sig_small)
        dsmall = jnp.where(lane < 2, dsig, jnp.where(lane == 2, -rate * dlog * sig_small, 0.0))
        dy_ref[lo:hi, 768:896] = dsmall.astype(LOW)
        dkey = beta * read_key + write_key
        dvalue = beta * dtarget

        def unit_back(grad, normed, scale):
            return scale * (grad - normed * jnp.sum(grad * normed, axis=1, keepdims=True))

        dact = jnp.concatenate(
            [
                unit_back(dquery, query, scale_q),
                unit_back(dkey[:SPAN], key0, scale_0),
                unit_back(dkey[SPAN:], key1, scale_1),
                dvalue[:SPAN],
                dvalue[SPAN:],
            ],
            axis=1,
        )
        dconv = dact * (sig * (1.0 + conv * (1.0 - sig)))
        here = pre_ref[lo:hi, :].astype(WIDE)
        if n:
            prior = pre_ref[lo - 16 : lo, :].astype(WIDE)
        else:
            prior = jnp.where(
                block == 0, edge_ref[...].astype(WIDE), prior_ref[...].astype(WIDE)
            )
        rows = stack(prior, here)
        dpre = taps_ref[0:1, :] * dconv
        dtaps_ref[0:1, :] += jnp.sum(dconv * here, axis=0, keepdims=True)
        for lag in range(1, 4):
            kept = jnp.where(pos >= lag, dconv, 0.0)
            shifted = rows[16 - lag : 16 - lag + SPAN]
            dtaps_ref[lag : lag + 1, :] += jnp.sum(kept * shifted, axis=0, keepdims=True)
            kept = kept * taps_ref[lag : lag + 1, :]
            dpre = dpre + stack(kept, next_ref[lag])[lag : lag + SPAN]
            next_ref[lag] = kept[0:8]
        dy_ref[lo:hi, 0:640] = dpre.astype(LOW)


def vmem_spec():
    return pl.BlockSpec(memory_space=pltpu.VMEM)


def smem_spec():
    return pl.BlockSpec(memory_space=pltpu.SMEM)


def fixed(shape):
    return pl.BlockSpec(shape, lambda *_: (0,) * len(shape))


def estimate(flops, mib):
    return pl.CostEstimate(flops=int(flops), bytes_accessed=int(mib * 2**20), transcendentals=0)


def run_forward(offs, rate, pre, gs, edge, taps, gain, state):
    tokens = pre.shape[0]
    spans = tokens // SPAN
    group = 4
    shape = jax.ShapeDtypeStruct
    outs = (
        (shape((tokens, 640), WIDE), pl.BlockSpec((group * SPAN, 640), lambda i: (i, 0))),
        (shape((spans, ROWS, ROWS), LOW), pl.BlockSpec((group, ROWS, ROWS), lambda i: (i, 0, 0))),
        (shape((spans, SPAN, ROWS), LOW), pl.BlockSpec((group, SPAN, ROWS), lambda i: (i, 0, 0))),
        (shape((spans, SPAN, HEAD), LOW), pl.BlockSpec((group, SPAN, HEAD), lambda i: (i, 0, 0))),
        (shape((spans, HEAD, HEAD), WIDE), pl.BlockSpec((group, HEAD, HEAD), lambda i: (i, 0, 0))),
        (shape((tokens, HEAD), LOW), fixed((tokens, HEAD))),
        (shape((tokens, HEAD), WIDE), fixed((tokens, HEAD))),
        (shape((spans, ROWS, HEAD), LOW), fixed((spans, ROWS, HEAD))),
        (shape((spans, HEAD, HEAD), WIDE), fixed((spans, HEAD, HEAD))),
        (shape((HEAD, HEAD), WIDE), fixed((HEAD, HEAD))),
    )
    return pl.pallas_call(
        functools.partial(forward_kernel, spans, offs.shape[1] - 1, group),
        out_shape=[o for o, _ in outs],
        grid=(spans // group,),
        in_specs=[
            smem_spec(),
            smem_spec(),
            pl.BlockSpec((group * SPAN, 640), lambda i: (i, 0)),
            pl.BlockSpec((16, 640), lambda i: (jnp.maximum(i * (group * SPAN // 16) - 1, 0), 0)),
            pl.BlockSpec((group * SPAN, HEAD), lambda i: (i, 1)),
            fixed((tokens, HEAD)),
            fixed((16, 640)),
            fixed((8, 640)),
            fixed((1, HEAD)),
            fixed((HEAD, HEAD)),
        ],
        out_specs=[b for _, b in outs],
        scratch_shapes=[
            pltpu.VMEM((spans, ROWS, HEAD), LOW),
            pltpu.VMEM((spans, ROWS, HEAD), WIDE),
            pltpu.VMEM((spans, HEAD, HEAD), WIDE),
            pltpu.VMEM((spans, SPAN, HEAD), WIDE),
            pltpu.VMEM((spans, HEAD, HEAD), WIDE),
            pltpu.VMEM((spans, SPAN, HEAD), LOW),
        ],
        compiler_params=pltpu.CompilerParams(vmem_limit_bytes=VMEM_LIMIT),
        cost_estimate=estimate(70e9, 24),
        name="delta_forward",
    )(offs, rate, pre, pre, gs, gs, edge, taps, gain, state)


def run_gate_back(gs, gain, mixed, qh, steps, dgated, dend):
    tokens = mixed.shape[0]
    spans = tokens // SPAN
    shape = jax.ShapeDtypeStruct
    return pl.pallas_call(
        functools.partial(gate_back_kernel, spans),
        out_shape=(
            shape((spans, SPAN, HEAD), LOW),
            shape((spans, HEAD, HEAD), WIDE),
            shape((tokens, HEAD), LOW),
            shape((1, HEAD), WIDE),
            shape((HEAD, HEAD), WIDE),
        ),
        grid=(1,),
        in_specs=[
            fixed((tokens, HEAD)),
            fixed((1, HEAD)),
            fixed((tokens, HEAD)),
            fixed((spans, SPAN, HEAD)),
            fixed((spans, HEAD, HEAD)),
            fixed((tokens, HEAD)),
            fixed((HEAD, HEAD)),
        ],
        out_specs=(
            fixed((spans, SPAN, HEAD)),
            fixed((spans, HEAD, HEAD)),
            fixed((tokens, HEAD)),
            fixed((1, HEAD)),
            fixed((HEAD, HEAD)),
        ),
        scratch_shapes=[pltpu.VMEM((spans, HEAD, HEAD), WIDE)],
        compiler_params=pltpu.CompilerParams(vmem_limit_bytes=VMEM_LIMIT),
        cost_estimate=estimate(15e9, 8),
        name="delta_gate_back",
    )(gs, gain, mixed, qh, steps, dgated, dend)


def run_backward(last, steps, offs, rate, pre, gs, edge, taps, saved, carried, dy):
    conv, inverse, upd, scores, states, do, ds, dgate = saved
    tokens = pre.shape[0]

    def at(i):
        return last - i

    def rows(columns, lane=0):
        return pl.BlockSpec((2 * SPAN, columns), lambda i: (at(i), lane))

    def spans(a, b):
        return pl.BlockSpec((2, a, b), lambda i: (at(i), 0, 0))

    shape = jax.ShapeDtypeStruct
    carried_specs = [fixed((4, 8, 640)), fixed((8, 640)), fixed((1, HEAD))]
    operands = [offs, rate, pre, pre, gs, edge, taps, conv, inverse, upd, scores, states, do, ds]
    operands += [dgate, *carried]
    in_specs = [
        smem_spec(),
        smem_spec(),
        rows(640),
        pl.BlockSpec((16, 640), lambda i: (jnp.maximum(at(i) * (2 * SPAN // 16) - 1, 0), 0)),
        rows(HEAD, 1),
        fixed((16, 640)),
        fixed((8, 640)),
        rows(640),
        spans(ROWS, ROWS),
        spans(ROWS, HEAD),
        spans(SPAN, ROWS),
        spans(HEAD, HEAD),
        spans(SPAN, HEAD),
        spans(HEAD, HEAD),
        rows(HEAD),
        *carried_specs,
    ]
    aliases = {}
    if dy is not None:
        aliases = {len(operands): 0}
        operands.append(dy)
        in_specs.append(pl.BlockSpec(memory_space=pl.ANY))
    dy, *carried = pl.pallas_call(
        functools.partial(backward_kernel, at, offs.shape[1] - 1),
        out_shape=(
            shape((tokens, 896), LOW),
            shape((4, 8, 640), WIDE),
            shape((8, 640), WIDE),
            shape((1, HEAD), WIDE),
        ),
        grid=(steps,),
        in_specs=in_specs,
        out_specs=(rows(896), *carried_specs),
        input_output_aliases=aliases,
        compiler_params=pltpu.CompilerParams(vmem_limit_bytes=VMEM_LIMIT),
        cost_estimate=estimate(4e9 * steps, 1.3 * steps),
        name="delta_backward",
    )(*operands)
    return dy, carried


def input_blocks_kernel(at_ref, dy_ref, out_ref, w_ref, send_ref, keep_ref):
    count = dy_ref.shape[0]
    block = contract(dy_ref[...], w_ref[...], 1, 1).astype(LOW)
    for n, to_ref in enumerate((send_ref, keep_ref)):

        @pl.when(pl.program_id(0) == n)
        def _():
            to_ref[:count, :] = block
            to_ref[count:, :] = out_ref[...]


def input_blocks(places, dy, grad_out, weights, count, out_rows):
    width = weights.shape[0]
    return pl.pallas_call(
        input_blocks_kernel,
        out_shape=[jax.ShapeDtypeStruct((count + out_rows, width), LOW)] * 2,
        grid_spec=pltpu.PrefetchScalarGridSpec(
            num_scalar_prefetch=1,
            grid=(2,),
            in_specs=[
                pl.BlockSpec((count, 896), lambda i, p: (p[i], 0)),
                pl.BlockSpec((out_rows, width), lambda i, p: (p[i], 0)),
                fixed(weights.shape),
            ],
            out_specs=[fixed((count + out_rows, width))] * 2,
        ),
        compiler_params=pltpu.CompilerParams(vmem_limit_bytes=VMEM_LIMIT),
        cost_estimate=estimate(4 * count * width * 896, 4),
        name="input_blocks",
    )(jnp.stack(places).astype(jnp.int32), dy, grad_out, weights)


def pack_kernel(
    heads, taps,
    place_ref, q_ref, k0_ref, k1_ref, v0_ref, v1_ref, g_ref, beta_ref, decay_ref, gin_ref,
    gff_ref, gh_ref, cq_ref, ck_ref, cv_ref, out_ref,
):
    h = place_ref[0]
    shard = q_ref.shape[0]
    for i, ref in enumerate((q_ref, k0_ref, k1_ref, v0_ref, v1_ref, g_ref)):
        out_ref[:shard, i * HEAD : (i + 1) * HEAD] = ref[...]
    beta, decay = beta_ref[...].astype(WIDE), decay_ref[...].astype(WIDE)

    def row_of(values, at):
        row = lax.broadcasted_iota(jnp.int32, values.shape, 0)
        return jnp.sum(jnp.where(row == at, values, 0.0), axis=0, keepdims=True)

    row = lax.broadcasted_iota(jnp.int32, (HEAD, shard), 0)
    small = jnp.where(row == 0, row_of(beta, h), 0.0)
    small = jnp.where(row == 1, row_of(beta, heads + h), small)
    small = jnp.where(row == 2, row_of(decay, h), small)
    out_ref[:shard, 6 * HEAD :] = small.T.astype(LOW)
    out_ref[shard:, :] = jnp.zeros((out_ref.shape[0] - shard, out_ref.shape[1]), LOW)
    vectors = stack(
        *[ref[...].astype(WIDE) for ref in (gin_ref, gff_ref, gh_ref, cq_ref)],
        *[
            ref[:, i * shard : (i + 1) * shard].astype(WIDE)
            for ref in (ck_ref, cv_ref)
            for i in range(2)
        ],
        jnp.zeros((32 - 3 - 5 * taps, shard), WIDE),
    )
    out_ref[shard:, :shard] = vectors.astype(LOW)


def pack_weights(
    head, w_query, w_key, w_value, w_outgate, w_beta, w_decay, gain_in, gain_ffn, gain_head,
    conv_query, conv_key, conv_value,
):
    shard, heads = w_decay.shape
    taps = conv_query.shape[0]

    def part(step):
        return pl.BlockSpec((shard, HEAD), lambda i, h: (0, step * heads + h[0]))

    small = (
        w_beta.T, w_decay.T, gain_in[None], gain_ffn[None],
        jnp.pad(gain_head, (0, shard - gain_head.shape[0]))[None],
        conv_query, conv_key, conv_value,
    )
    return pl.pallas_call(
        functools.partial(pack_kernel, heads, taps),
        out_shape=jax.ShapeDtypeStruct((shard + 32, 896), LOW),
        grid_spec=pltpu.PrefetchScalarGridSpec(
            num_scalar_prefetch=1,
            grid=(1,),
            in_specs=[part(0), part(0), part(1), part(0), part(1), part(0)]
            + [fixed(a.shape) for a in small],
            out_specs=fixed((shard + 32, 896)),
        ),
        compiler_params=pltpu.CompilerParams(vmem_limit_bytes=VMEM_LIMIT),
        cost_estimate=estimate(0, 2),
        name="pack_weights",
    )(head.reshape(1), w_query, w_key, w_key, w_value, w_value, w_outgate, *small)


def project_kernel(place_ref, tok_ref, other_ref, gain_ref, w_ref, *refs):
    low_ref, pre_ref, gs_ref = refs[-3:]
    values = jnp.where(pl.program_id(0) == 0, tok_ref[...], other_ref[...]).astype(WIDE)
    scale = lax.rsqrt(jnp.mean(values * values, axis=1, keepdims=True) + EPSILON)
    normed = (values * scale * gain_ref[...]).astype(LOW)
    low_ref[...] = normed
    pre_ref[...] = contract(normed, w_ref[:, :640], 1, 0).astype(LOW)
    gs_ref[...] = contract(normed, w_ref[:, 640:], 1, 0)


def project(places, rows, other, gain, weights, length, filled):
    count, width = rows.shape
    shape = jax.ShapeDtypeStruct
    operands = [places, rows, other, gain, weights]
    in_specs = [fixed(a.shape) for a in operands[1:]]
    aliases = {}
    if filled is not None:
        aliases = {len(operands) + i: i for i in range(3)}
        operands += filled
        in_specs += [pl.BlockSpec(memory_space=pl.ANY)] * 3
    return pl.pallas_call(
        project_kernel,
        out_shape=[shape((length, n), t) for n, t in ((width, LOW), (640, LOW), (256, WIDE))],
        grid_spec=pltpu.PrefetchScalarGridSpec(
            num_scalar_prefetch=1,
            grid=(2,),
            in_specs=in_specs,
            out_specs=[
                pl.BlockSpec((count, n), lambda i, p: (p[i], 0)) for n in (width, 640, 256)
            ],
        ),
        input_output_aliases=aliases,
        compiler_params=pltpu.CompilerParams(vmem_limit_bytes=VMEM_LIMIT),
        cost_estimate=estimate(4 * count * width * 896, 6),
        name="project",
    )(*operands)


def rms_parts(values):
    return values * lax.rsqrt(jnp.mean(values * values, axis=-1, keepdims=True) + EPSILON)


def rms_back(grad_scaled, values):
    scale = lax.rsqrt(jnp.mean(values * values, axis=-1, keepdims=True) + EPSILON)
    normed = values * scale
    return scale * (
        grad_scaled - normed * jnp.mean(grad_scaled * normed, axis=-1, keepdims=True)
    )


def dot_plain(left, right, kind=WIDE):
    return jnp.dot(left, right, preferred_element_type=kind)


def dot_left(left, right, kind=WIDE):
    return contract(left, right, 0, 0).astype(kind)


def dot_right(left, right):
    return contract(left, right, 1, 1)


def exchanged(value, axis, bit):
    size = lax.axis_size(axis)
    return lax.ppermute(value, axis, [(i, i ^ bit) for i in range(size)])


def near_order(size):
    order, bit = [0], size // 2
    while bit:
        order = order + [o ^ bit for o in order]
        bit //= 2
    return order


def near_gather(value, axis, first=None):
    bit = lax.axis_size(axis) // 2
    while bit:
        value = stack(value, exchanged(value, axis, bit) if first is None else first)
        first = None
        bit //= 2
    return value


def near_scatter(value, axis):
    size, bit = lax.axis_size(axis), 1
    while bit < size:
        half = value.shape[0] // 2
        came = exchanged(value[half:].astype(LOW), axis, bit).astype(WIDE)
        value = value[:half].astype(WIDE) + came
        bit *= 2
    return value


def near_blocks(value, axis):
    size, me = lax.axis_size(axis), lax.axis_index(axis)
    return stack(
        *[lax.dynamic_index_in_dim(value, me ^ o, 0, False) for o in near_order(size)]
    )


def ordered_step(value, other, axis, bit):
    mine_first = (lax.axis_index(axis) & bit) == 0
    pair = jnp.where(mine_first, jnp.stack([value, other], 1), jnp.stack([other, value], 1))
    return pair.reshape((pair.shape[0] * 2,) + value.shape[1:])


def ordered_gather(value, axis, first=None):
    bit = lax.axis_size(axis) // 2
    value = value[None]
    while bit:
        other = exchanged(value, axis, bit) if first is None else first[None]
        value = ordered_step(value, other, axis, bit)
        first = None
        bit //= 2
    return value


def far_exchange(value, axis):
    return exchanged(value, axis, lax.axis_size(axis) // 2)


def after(value, *done):
    return lax.optimization_barrier((value, *done))[0]


def team_step(value, team, move):
    size = lax.axis_size("seq")
    pairs = [(t + i, t + move(i)) for t in range(0, size, team) for i in range(team)]
    return lax.ppermute(value, "seq", pairs)


def turn(value, team, by):
    return team_step(value, team, lambda i: (i + 2 * by) % team)


def cross(value, team):
    return team_step(value, team, lambda i: i ^ 1)


def turns(team):
    half = team // 2
    return [0] + [k for n in range(1, half // 2 + 1) for k in dict.fromkeys((n, half - n))]


def gather_stages(value, team, ties=()):
    me = lax.axis_index("seq") % team
    half = team // 2
    turned, found, before = {0: value}, [], ()
    if half > 1:
        turned[1] = turn(value, team, 1)
    if half > 2:
        turned[half - 1] = turn(value, team, -1)
    for k in turns(team):
        across = cross(after(turned[k], *before, *ties), team)
        stage = [across]
        for n in (k + 1, k - 1):
            if 0 < n < half and n not in turned and k:
                turned[n] = turn(turned[k], team, 1 if n > k else -1)
                stage.append(turned[n])
        before = (across,)
        found.append(((me - 2 * k) % team, turned[k], ((me ^ 1) - 2 * k) % team, across))
        yield stage
    yield found


def last_of(stages):
    for stage in stages:
        pass
    return stage


def team_places(team):
    me = lax.axis_index("seq") % team
    return [
        (((me ^ 1) + 2 * k) % team, (me + 2 * k) % team) for k in reversed(turns(team))
    ]


def scatter_stages(blocks, team, ties=()):
    half = team // 2
    passing, leaving, before = {}, None, ()
    for (send, keep), k in zip(blocks, reversed(turns(team))):
        came = cross(after(send, *before, *ties), team)
        stage = [came]
        if leaving is not None:
            pair, n = leaving
            forward = 2 * n <= half
            to = n - 1 if forward else (n + 1) % half
            moved = turn(pair.astype(LOW), team, 1 if forward else -1)
            stage.append(moved)
            passing[to] = passing.get(to, []) + [moved]
        yield stage
        before = (came,)
        pair = keep.astype(WIDE) + came.astype(WIDE)
        for moved in passing.pop(k, []):
            pair = pair + moved.astype(WIDE)
        leaving = (pair, k)
    yield pair


def mixer_outputs_kernel(heads, taps, fsdp, place_ref, *refs):
    got_refs, out_refs, refs = refs[:heads], refs[heads : 2 * heads], refs[2 * heads :]
    (q_ref, k_ref, v_ref, g_ref, b_ref, d_ref, gin_ref, gff_ref, gh_ref, rate_ref, cq_ref,
     ck_ref, cv_ref, out_ref) = refs
    member = place_ref[0, heads]
    shard = q_ref.shape[0]
    gains = gh_ref.shape[1]
    width = heads * HEAD
    lane_r = lax.broadcasted_iota(jnp.int32, (1, heads), 1)
    rates = jnp.zeros((1, heads), WIDE)
    vectors = jnp.zeros((8, shard), WIDE)
    for n in range(heads):
        got_ref = got_refs[n]
        h = place_ref[0, n]

        def columns(step):
            return pl.ds(pl.multiple_of(step * width + h * HEAD, HEAD), HEAD)

        q_ref[:, columns(0)] = got_ref[:shard, 0:128].astype(WIDE)
        for i in range(2):
            k_ref[:, columns(i)] = got_ref[:shard, 128 + i * 128 : 256 + i * 128].astype(WIDE)
            v_ref[:, columns(i)] = got_ref[:shard, 384 + i * 128 : 512 + i * 128].astype(WIDE)
        g_ref[:, columns(0)] = got_ref[:shard, 640:768].astype(WIDE)
        last = got_ref[:shard, 768:896].astype(WIDE).T
        b_ref[pl.ds(h, 1), :] = last[0:1]
        b_ref[pl.ds(heads + h, 1), :] = last[1:2]
        d_ref[pl.ds(h, 1), :] = last[2:3]
        extra = got_ref[shard:, :].astype(WIDE)
        vectors = vectors + extra[0:8, :shard]
        rates = jnp.where(lane_r == h, extra[3:4, 2:3], rates)
        rows = out_refs[n].shape[0]
        out_ref[pl.ds(pl.multiple_of(h * rows, rows), rows), :] = out_refs[n][...].astype(WIDE)
        for ref, at, steps in ((cq_ref, 0, 1), (ck_ref, 128, 2), (cv_ref, 384, 2)):
            per = ref.shape[1] // HEAD
            for i in range(steps):
                slot = i * heads + h - member * per

                @pl.when((slot >= 0) & (slot < per))
                def _():
                    to = pl.ds(pl.multiple_of(slot * HEAD, HEAD), HEAD)
                    ref[:, to] = extra[4 : 4 + taps, at + i * HEAD : at + (i + 1) * HEAD]

    rate_ref[...] = rates
    gin_ref[...] = vectors[0:1]
    gff_ref[...] = vectors[1:2]
    gh_ref[...] = vectors[2:3, :gains]


def mixer_outputs(found, found_out, shard, gains, taps, fsdp, member):
    found, found_out = (
        [one for a, x, b, y in pairs for one in ((a, x), (b, y))] for pairs in (found, found_out)
    )
    heads = len(found)
    places = jnp.stack([place for place, _ in found] + [member])[None].astype(jnp.int32)
    width = heads * HEAD
    shape = jax.ShapeDtypeStruct
    outs = (
        shape((shard, width), WIDE),
        shape((shard, 2 * width), WIDE),
        shape((shard, 2 * width), WIDE),
        shape((shard, width), WIDE),
        shape((2 * heads, shard), WIDE),
        shape((heads, shard), WIDE),
        shape((1, shard), WIDE),
        shape((1, shard), WIDE),
        shape((1, gains), WIDE),
        shape((1, heads), WIDE),
        shape((taps, shard), WIDE),
        shape((taps, 2 * shard), WIDE),
        shape((taps, 2 * shard), WIDE),
        shape((shard, width), WIDE),
    )
    return pl.pallas_call(
        functools.partial(mixer_outputs_kernel, heads, taps, fsdp),
        out_shape=outs,
        in_specs=[smem_spec()] + [vmem_spec()] * (2 * heads),
        out_specs=[vmem_spec()] * len(outs),
        compiler_params=pltpu.CompilerParams(vmem_limit_bytes=VMEM_LIMIT),
        cost_estimate=estimate(0, 12),
        name="mixer_outputs",
    )(places, *(value for _, value in found), *(value for _, value in found_out))


def ff_outputs_kernel(count, slab, shard, place_ref, *refs):
    got_refs, (gate_ref, up_ref, down_ref), held = refs[:count], refs[count : count + 3], refs[-1]
    own = count * slab
    for n, got_ref in enumerate(got_refs):
        at = place_ref[n] * slab
        piece = got_ref[...].astype(WIDE)
        for m in range(2):
            for k in range(2):
                to = pl.multiple_of(k * own + at, 8)
                held[m, pl.ds(to, slab), :] = piece[
                    m * slab : (m + 1) * slab, k * shard : (k + 1) * shard
                ]
        down_ref[pl.ds(pl.multiple_of(at, 8), slab), :] = piece[2 * slab :]
    gate_ref[...] = held[0].T
    up_ref[...] = held[1].T


def ff_outputs(found, slab, shard, fsdp):
    found = [one for a, x, b, y in found for one in ((a, x), (b, y))]
    count, (rows, width) = len(found), found[0][1].shape
    own = count * slab
    shape = jax.ShapeDtypeStruct
    return pl.pallas_call(
        functools.partial(ff_outputs_kernel, count, slab, shard),
        out_shape=(
            shape((shard, fsdp * own), WIDE),
            shape((shard, fsdp * own), WIDE),
            shape((own, width), WIDE),
        ),
        grid_spec=pltpu.PrefetchScalarGridSpec(
            num_scalar_prefetch=1,
            grid=(fsdp // 2,),
            in_specs=[pl.BlockSpec((rows, 2 * shard), lambda i, p: (0, i))] * count,
            out_specs=(
                pl.BlockSpec((shard, 2 * own), lambda i, p: (0, i)),
                pl.BlockSpec((shard, 2 * own), lambda i, p: (0, i)),
                pl.BlockSpec((own, 2 * shard), lambda i, p: (0, i)),
            ),
            scratch_shapes=[pltpu.VMEM((2, 2 * own, shard), WIDE)],
        ),
        compiler_params=pltpu.CompilerParams(vmem_limit_bytes=VMEM_LIMIT),
        cost_estimate=estimate(0, 15),
        name="ff_outputs",
    )(jnp.stack([p for p, _ in found]).astype(jnp.int32), *(x for _, x in found))


def ff_outputs_plain(got, slab, shard, fsdp):
    seq, rows, width = got.shape
    own = seq * slab
    wide = got.astype(WIDE)

    def turned(at):
        part = wide[:, at : at + slab].reshape(seq, slab, fsdp, shard)
        return jnp.transpose(part, (3, 2, 0, 1)).reshape(shard, fsdp * own)

    return turned(0), turned(slab), wide[:, 2 * slab :].reshape(own, width)


def per_device(
    tokens, cotangent, offsets, gain_in, w_query, w_key, w_value, w_beta, w_decay, w_outgate,
    conv_query, conv_key, conv_value, decay_scale, gain_head, w_out, gain_ffn, w_gate, w_up,
    w_down,
):
    seq, fsdp = lax.axis_size("seq"), lax.axis_size("fsdp")
    heads = decay_scale.shape[0]
    taps = conv_query.shape[0]
    own_rows = tokens.shape[1]
    shard = w_query.shape[0]
    width = shard * fsdp
    teams = seq // heads
    assert teams * heads == seq and width == heads * HEAD
    place = lax.axis_index("seq")
    head, team = place % heads, place // heads
    member = lax.axis_index("fsdp")
    if teams == 1:
        team_groups, head_groups = None, None
    else:
        team_groups = [[t * heads + h for h in range(heads)] for t in range(teams)]
        head_groups = [[t * heads + h for t in range(teams)] for h in range(heads)]

    def gather_rows(value):
        return lax.all_gather(value, "fsdp", axis=0, tiled=True)

    found = last_of(gather_stages(tokens[0], heads))
    length = heads * own_rows

    near = found[0][3]
    packed = pack_weights(
        head, after(w_query, near), w_key, w_value, w_outgate, w_beta, w_decay, gain_in,
        gain_ffn, gain_head, conv_query, conv_key, conv_value,
    )
    far_packed = far_exchange(packed, "fsdp")
    far_packed = after(far_packed, *(rows for _, rows, _, _ in found[1:-1]))
    got = ordered_gather(packed, "fsdp", far_packed)
    full_packed = got[:, :shard].reshape(width, 896)
    vectors = got[:, shard:, :shard]
    full_gain_in = vectors[:, 0].reshape(width).astype(WIDE)
    full_gain_ffn = vectors[:, 1].reshape(width).astype(WIDE)
    full_gain_head = vectors[:, 2, : gain_head.shape[0]].reshape(1, HEAD).astype(WIDE)

    def head_taps_of(row, pieces, step):
        column = step * width + head * HEAD
        inside = column % (pieces * shard)
        at = (column // (pieces * shard), row + inside // shard * taps, inside % shard)
        return lax.dynamic_slice(vectors, at, (1, taps, HEAD))[0]

    head_taps = jnp.concatenate(
        [head_taps_of(3, 1, 0)]
        + [head_taps_of(3 + taps, 2, i) for i in range(2)]
        + [head_taps_of(3 + 3 * taps, 2, i) for i in range(2)],
        axis=1,
    ).astype(WIDE)
    head_taps = jnp.pad(head_taps, ((0, 8 - taps), (0, 0)))
    def column_blocks(value):
        return jnp.transpose(value.reshape(shard, fsdp, value.shape[1] // fsdp), (1, 0, 2))

    gate_blocks, up_blocks = column_blocks(after(w_gate, near)), column_blocks(after(w_up, near))
    full_packed, gate_blocks, up_blocks = lax.optimization_barrier(
        (full_packed, gate_blocks, up_blocks)
    )
    filled = None
    for n, (at, rows, at_other, other) in enumerate(found):
        places = jnp.stack([at, at_other]).astype(jnp.int32)
        filled = project(places, rows, other, full_gain_in[None], full_packed, length, filled)
        if n == 0:
            w_out, gate_blocks, up_blocks, cot, *filled = lax.optimization_barrier(
                (w_out, gate_blocks, up_blocks, cotangent[0], *filled)
            )
            cols_gate = lax.all_to_all(gate_blocks, "fsdp", 0, 0)
            cols_up = lax.all_to_all(up_blocks, "fsdp", 0, 0)
            far_out, far_cot = far_exchange(w_out, "fsdp"), far_exchange(cot, "fsdp")
    normed_low, pre, gate_small = filled
    offs = jnp.concatenate(
        [offsets, jnp.broadcast_to(team * length, (1, 1)).astype(jnp.int32)], axis=1
    )
    rate = lax.dynamic_slice_in_dim(decay_scale, head, 1).reshape(1, 1)
    zero_state = jnp.zeros((HEAD, HEAD), WIDE)
    if teams == 1:
        edge = jnp.zeros((16, 640), LOW)
    else:
        forth = [(i, i + heads) for i in range(seq - heads)]
        back = [(i + heads, i) for i in range(seq - heads)]
        edge = lax.ppermute(pre[-16:], "seq", forth)

    def forward_from(state):
        return run_forward(
            offs, rate, pre, gate_small, edge, head_taps, full_gain_head, state
        )

    state_in = zero_state
    if teams > 1:
        trial = forward_from(zero_state)
        steps, end = trial[4], trial[9]

        def along(c, total):
            return jnp.dot(total, steps[c].T, precision=lax.Precision.HIGHEST)

        whole_map = lax.fori_loop(0, steps.shape[0], along, jnp.eye(HEAD, dtype=WIDE))
        for _ in range(teams - 1):
            out = jnp.dot(state_in, whole_map, precision=lax.Precision.HIGHEST) + end
            state_in = lax.ppermute(out.astype(LOW), "seq", forth).astype(WIDE)
    conv, inverse, scores, reach, steps, gated, mixed, upd, states, _ = forward_from(state_in)
    gated, far_out, cols_gate, cols_up, far_cot = lax.optimization_barrier(
        (gated, far_out, cols_gate, cols_up, far_cot)
    )
    full_out = ordered_gather(w_out, "fsdp", far_out).reshape(width, width)
    group_cot = near_gather(cot, "fsdp", far_cot)
    cols_gate, cols_up = (a.reshape(width, a.shape[2]) for a in (cols_gate, cols_up))

    gated_own = lax.all_to_all(
        gated, "seq", 0, 1, tiled=True, axis_index_groups=team_groups
    )
    inputs = tokens[0].astype(WIDE)
    mixer_res = inputs + dot_plain(gated_own, full_out)

    mid_normed = rms_parts(mixer_res)
    mid_low = (mid_normed * full_gain_ffn).astype(LOW)
    group_mid = near_gather(mid_low, "fsdp")
    gate_pre = dot_plain(group_mid, cols_gate)
    up_pre = dot_plain(group_mid, cols_up)
    sig = jax.nn.sigmoid(gate_pre)
    act = gate_pre * sig
    hidden = (act * up_pre).astype(LOW)
    grad_hidden = dot_right(group_cot, w_down)
    grad_gate_pre = (grad_hidden * up_pre * (sig * (1.0 + gate_pre * (1.0 - sig)))).astype(LOW)
    grad_up_pre = (grad_hidden * act).astype(LOW)
    grad_mid = dot_right(grad_gate_pre, cols_gate) + dot_right(grad_up_pre, cols_up)
    grad_gate_pre, grad_up_pre, grad_mid = lax.optimization_barrier(
        (grad_gate_pre, grad_up_pre, grad_mid)
    )
    grad_mid = near_scatter(grad_mid, "fsdp")

    grad_res = cotangent[0].astype(WIDE) + rms_back(grad_mid * full_gain_ffn, mixer_res)
    grad_gain_ffn = jnp.sum(grad_mid * mid_normed, axis=0)
    res_low = grad_res.astype(LOW)
    grad_gated = dot_right(res_low, full_out).astype(LOW)
    own_ff = w_down.shape[0]
    slab = own_ff // seq
    slabs = jnp.concatenate(
        [
            dot_left(grad_gate_pre, group_mid, LOW).reshape(seq, slab, width),
            dot_left(grad_up_pre, group_mid, LOW).reshape(seq, slab, width),
            dot_left(hidden, group_cot, LOW).reshape(seq, slab, width),
        ],
        axis=1,
    )
    permuted = teams == 1 and slab % 8 == 0 and own_ff * 2 % HEAD == 0 and fsdp % 2 == 0

    def turned_columns(summed):
        turned = lax.all_to_all(summed[: 2 * slab], "fsdp", 1, 1, tiled=True)
        return stack(turned, summed[2 * slab :])

    def feed_forward_sums():
        if not permuted:
            summed = lax.psum_scatter(
                slabs.reshape(seq * 3 * slab, width), "seq", scatter_dimension=0, tiled=True
            )
            yield [summed]
            slabs_done = lax.all_gather(turned_columns(summed), "seq", axis=0)
            yield ff_outputs_plain(slabs_done, slab, shard, fsdp)
            return
        blocks = [
            [lax.dynamic_index_in_dim(slabs, p, 0, False) for p in pair]
            for pair in team_places(heads)
        ]
        for stage in scatter_stages(blocks, heads, ties):
            if isinstance(stage, list):
                yield stage
        mine = turned_columns(after(stage.astype(LOW), *ties))
        yield [mine]
        for stage in gather_stages(mine, heads, ties):
            if isinstance(stage[0], tuple):
                break
            yield stage
        yield ff_outputs(stage, slab, shard, fsdp)

    ties, sums = [], feed_forward_sums()
    brought = [next(sums)]

    def beside(value):
        if not isinstance(brought[-1], tuple):
            ties[:] = [value]
            brought.append(next(sums))

    def settled(value):
        stage = brought[-1]
        return value if isinstance(stage, tuple) else after(value, *stage)

    beside(grad_gated)
    dgated = lax.all_to_all(
        grad_gated, "seq", 1, 0, tiled=True, axis_index_groups=team_groups
    )
    dgated = settled(dgated)
    beside(dgated)
    down_part = near_scatter(dot_plain(after(hidden, dgated), w_down), "fsdp")
    layer_out = (mixer_res + down_part).astype(LOW)
    grad_out = dot_left(after(gated_own, dgated), res_low, LOW).reshape(fsdp, shard, width)
    grad_out = near_scatter(near_blocks(grad_out, "fsdp"), "fsdp").astype(LOW)

    def gate_back_from(dend):
        return run_gate_back(
            gate_small, full_gain_head, mixed, reach, steps, dgated, dend
        )

    dend = zero_state
    if teams > 1:
        begin = gate_back_from(zero_state)[4]
        for _ in range(teams - 1):
            out = lax.dot_general(
                dend, whole_map, (((1,), (1,)), ((), ())), precision=lax.Precision.HIGHEST
            )
            dend = lax.ppermute((out + begin).astype(LOW), "seq", back).astype(WIDE)
    do, ds, dgate, dgain, _ = gate_back_from(dend)
    carried = [
        jnp.zeros((4, 8, 640), WIDE), jnp.zeros((8, 640), WIDE), jnp.zeros((1, HEAD), WIDE)
    ]
    dy, calls = None, 6
    left = length // (2 * SPAN)
    for call in range(calls, 0, -1):
        steps_here = -(-left // call)
        carried[0] = settled(carried[0] if dy is not None else after(carried[0], do))
        beside(carried[0])
        dy, carried = run_backward(
            left - 1, steps_here, offs, rate, pre, gate_small, edge, head_taps,
            (conv, inverse, upd, scores, states, do, ds, dgate), carried, dy,
        )
        carried = list(carried)
        left -= steps_here
    dy = settled(dy)
    following, dtaps, drate = carried
    if teams > 1:
        none = jnp.zeros((16, 640), WIDE)
        dedge = sum(stack(none, following[lag])[lag : lag + 16] for lag in range(1, 4))
        from_next = lax.ppermute(dedge.astype(LOW), "seq", back).astype(WIDE)
        tail = (dy[-16:, :640].astype(WIDE) + from_next).astype(LOW)
        dy = lax.dynamic_update_slice(dy, tail, (length - 16, 0))

    out_rows = shard // heads

    blocks = [
        list(input_blocks(places, dy, grad_out, full_packed, own_rows, out_rows))
        for places in team_places(heads)
    ]
    while not isinstance(brought[-1], tuple):
        beside(dy)
    out_gate, out_up, out_down = brought[-1]
    sent = scatter_stages(blocks, heads)
    stage = next(sent)
    grad_packed = dot_left(normed_low, after(dy, blocks[0][0]))
    stage = next(sent)
    stage = next(sent)
    stage = next(sent)
    ready = (stage[0],)
    joined = next(sent)
    grad_normed, own_out = joined[:own_rows], joined[own_rows:].astype(LOW)
    input_grad = (grad_res + rms_back(grad_normed * full_gain_in, inputs)).astype(LOW)
    if teams > 1:
        own_out = lax.psum(own_out, "seq", axis_index_groups=head_groups)
    found_out = last_of(gather_stages(own_out, heads))

    grad_gain_in = (
        jnp.sum(grad_packed * full_packed.astype(WIDE), axis=1) / full_gain_in
    )
    extra = jnp.zeros((fsdp, 16, 896), WIDE)
    extra = extra.at[:, 0, :shard].set(grad_gain_in.reshape(fsdp, shard))
    extra = extra.at[:, 1, :shard].set(grad_gain_ffn.reshape(fsdp, shard))
    gh = gain_head.shape[0]
    extra = extra.at[:, 2, :gh].set(dgain.reshape(fsdp, gh))
    extra = extra.at[:, 3, :HEAD].set(drate)
    extra = extra.at[:, 4 : 4 + taps, :640].set(dtaps[None, :taps])
    combined = jnp.concatenate([grad_packed.reshape(fsdp, shard, 896), extra], axis=1)
    combined = near_scatter(near_blocks(combined.astype(LOW), "fsdp"), "fsdp").astype(LOW)
    if teams > 1:
        combined = lax.psum(combined, "seq", axis_index_groups=head_groups)
    (out_query, out_key, out_value, out_gatew, out_beta, out_decay, out_gain_in, out_gain_ffn,
     out_gain_head, out_rate, out_cq, out_ck, out_cv, out_out) = mixer_outputs(
        last_of(gather_stages(after(combined, *ready), heads)), found_out, shard, gain_head.shape[0], taps, fsdp, member
    )

    return (
        layer_out[None],
        input_grad[None],
        out_gain_in[0],
        out_query,
        out_key,
        out_value,
        out_beta.T,
        out_decay.T,
        out_gatew,
        out_cq,
        out_ck,
        out_cv,
        out_rate[0],
        out_gain_head[0],
        out_out,
        out_gain_ffn[0],
        out_gate,
        out_up,
        out_down,
    )


def solution(mesh):
    rows, lanes = P("fsdp", None), P(None, "fsdp")
    block = P("fsdp", "seq", None)
    return jax.shard_map(
        per_device,
        mesh=mesh,
        in_specs=(
            block, block, rows, P("fsdp"), rows, rows, rows, rows, rows, rows,
            lanes, lanes, lanes, P(), P("fsdp"), rows, P("fsdp"), rows, rows, rows,
        ),
        out_specs=(
            block, block, P("fsdp"), rows, rows, rows, rows, rows, rows,
            lanes, lanes, lanes, P(), P("fsdp"), rows, P("fsdp"), rows, rows, rows,
        ),
        check_vma=False,
    )
```

time: 648 us -> 579 us (0.89)
  waiting for transfers between devices: 210 us -> 150 us
  Pallas kernels: 150 us -> 202 us
  matrix products: 57.3 us -> 33.1 us
  blocking collectives: 19.8 us -> 0 us
  local copies, waits for them, and re-layouts: 63.7 us -> 46.1 us
  starting transfers between devices: 70.1 us -> 85.7 us
  between operations: 15.4 us -> 2.16 us
    pallas_call x3 -> x18, Pallas kernels: 71.4 us -> 126 us  [the longest x6 57.6 us: run_backward(): pl.pallas_call(functools.partial(backward_kernel, at, offs.shape[1] - 1),...]
    ppermute x16, waiting for transfers between devices: 48.3 us -> 18.3 us  [exchanged(): return lax.ppermute(value, axis, [(i, i ^ bit) for i in range(size)])]
    ppermute x21 -> x42, starting transfers between devices: 20.2 us -> 50 us  [team_step(): return lax.ppermute(value, 'seq', pairs)]
    ppermute x21 -> x42, waiting for transfers between devices: 141 us -> 120 us  [team_step(): return lax.ppermute(value, 'seq', pairs)]
    all_to_all x1 -> x0, blocking collectives: 19.8 us -> none  [per_device(): lax.all_to_all(gated, 'seq', 0, 1, tiled=True, axis_index_groups=team_gro...]
    all_to_all x4, starting transfers between devices: 36 us -> 18.2 us  [the longest x1 6.06 us: per_device(): lax.all_to_all(gated, 'seq', 0, 1, tiled=True, axis_index_groups=team_gro...]
    dot_general x6 -> x4, matrix products: 22.9 us -> 7.93 us  [dot_plain(): return jnp.dot(left, right, preferred_element_type=kind)]
    dynamic_update_slice x8 -> x0, local copies, waits for them, and re-layouts: 11.9 us -> none  [per_device(): seq_tokens = lax.dynamic_update_slice(seq_tokens, rows, (at * own_rows, 0))]
  transfers between devices with their start and end apart: 44 -> 63, of which waited for: 20 -> 29; matrix products, arithmetic and copies ran while one was open for 23% -> 16% of each run, Pallas kernels for 10% -> 34%
where the time goes in v3:
time: 579 us; the launch traced here: 569 us
  Pallas kernels  202 us (35%)
  waiting for transfers between devices  150 us (26%)
  starting transfers between devices  85.7 us (15%)
  other arithmetic  49 us (8%)
  local copies, waits for them, and re-layouts  46.1 us (8%)
  matrix products  33.1 us (6%)
    ppermute x42, waiting for transfers between devices, team_step(): return lax.ppermute(value, 'seq', pairs)  120 us
    pallas_call x1, Pallas kernels, run_forward(): pl.pallas_call(functools.partial(forward_kernel, spans, offs.shape[1] - 1...  76.2 us
    pallas_call x6, Pallas kernels, run_backward(): pl.pallas_call(functools.partial(backward_kernel, at, offs.shape[1] - 1),...  57.6 us
    ppermute x42, starting transfers between devices, team_step(): return lax.ppermute(value, 'seq', pairs)  50 us
    dot_general x9, matrix products, contract(): lax.dot_general(left, right, (((left_dim,), (right_dim,)), ((), ())), pre...  25.2 us
    pallas_call x4, Pallas kernels, input_blocks(): pl.pallas_call(input_blocks_kernel, out_shape=[jax.ShapeDtypeStruct((coun...  21 us
    pallas_call x4, Pallas kernels, project(): pl.pallas_call(project_kernel, out_shape=[shape((length, n), t) for n, t...  20.5 us
    ppermute x16, waiting for transfers between devices, exchanged(): return lax.ppermute(value, axis, [(i, i ^ bit) for i in range(size)])  18.3 us
  transfers between devices with their start and end apart: 63, of which 29 were waited for; matrix products, arithmetic and copies ran while one was open for 16% of the time, Pallas kernels for 34%

profile of v3, /device:TPU:0, one launch (start us, length us, event | category | flops | bytes accessed | tf_op | source)
XLA Modules:
  0.0 568.9 jit_solution(5608693225578899333)
XLA Ops:
  11.2 4.6 collective-permute-done.3.other_ref
  20.6 9.2 %collective-permute-done.2.tok_ref = bf16[256,1024]{1,0:T(8,128)(2,1)S(1)} collective-permute-done((bf16[256,1024]{1,0:T(8,128)(2,1)}, bf16[256,1024]{1,0:T(8,128)(2,1)S(1)}, u32[]{:S(2)}, u32[]{:S(2)}) %collective-permute-start.2) | collective-permute-done | bytes 524320 | tf_op jit(solution)/shard_map/ppermute | solution.py:734
  44.9 3.9 collective-permute-done.4.other_ref
  52.9 5.1 project.4
  58.0 4.5 all-to-all-start
  67.6 5.1 project.5
  74.3 5.1 project.6
  82.4 5.1 project.7
  87.5 3.6 all-to-all-start.1
  92.3 76.2 %delta_forward.1 = (f32[2048,640]{1,0:T(8,128)}, bf16[32,128,128]{2,1,0:T(8,128)(2,1)}, bf16[32,64,128]{2,1,0:T(8,128)(2,1)}, bf16[32,64,128]{2,1,0:T(8,128)(2,1...) custom-call(s32[1,17]{1,0:T(1,128)} %pad_add_fusion.offs_ref, ...), custom_call_target="tpu_custom_call" | custom-call | flops 70000001024 | bytes 25165824 | tf_op jit(solution)/shard_map/delta_forward/pallas_call | solution.py:382
  173.9 6.1 %all-to-all-start.2 = ((bf16[8,256,128]{1,2,0:T(8,128)(2,1)}), bf16[8,256,128]{1,2,0:T(8,128)(2,1)S(1)}, u32[]{:S(2)}, u32[]{:S(2)}) async-start(bf16[8,256,128]{1,2,0:T(8,128)(2,1)} %copy.67), calls=%async_computation.2 | async-start | bytes 1048576 | tf_op jit(solution)/shard_map/all_to_all | solution.py:1058
  184.9 9.7 %all-to-all-done.2 = bf16[8,256,128]{1,2,0:T(8,128)(2,1)S(1)} async-done(((bf16[8,256,128]{1,2,0:T(8,128)(2,1)}), bf16[8,256,128]{1,2,0:T(8,128)(2,1)S(1)}, u32[]{:S(2)}, u32[]{:S(2)}) %all-to-all-start.2) | async-done | bytes 524320 | tf_op jit(solution)/shard_map/all_to_all | solution.py:1058
  201.5 9.8 %collective-permute-done.12 = bf16[256,1024]{1,0:T(8,128)(2,1)S(1)} collective-permute-done((bf16[256,1024]{1,0:T(8,128)(2,1)S(1)}, bf16[256,1024]{1,0:T(8,128)(2,1)S(1)}, u32[]{:S(2)}, u32[]{:S(2)}) %collective-permute-start.12) | collective-permute-done | bytes 524320 | tf_op jit(solution)/shard_map/ppermute | solution.py:669
  218.0 3.8 multiply_convert_fusion
  229.3 3.6 convolution_convert_fusion.3
  244.3 6.6 %collective-permute-done.16 = bf16[256,1024]{1,0:T(8,128)(2,1)S(1)} collective-permute-done((bf16[256,1024]{1,0:T(8,128)(2,1)S(1)}, bf16[256,1024]{1,0:T(8,128)(2,1)S(1)}, u32[]{:S(2)}, u32[]{:S(2)}) %collective-permute-start.16) | collective-permute-done | bytes 524320 | tf_op jit(solution)/shard_map/ppermute | solution.py:669
  254.9 4.7 all-to-all-start.3
  266.1 17.3 %collective-permute-done.19 = bf16[264,1024]{1,0:T(8,128)(2,1)} collective-permute-done((bf16[264,1024]{1,0:T(8,128)(2,1)}, bf16[264,1024]{1,0:T(8,128)(2,1)}, u32[]{:S(2)}, u32[]{:S(2)}) %collective-permute-start.19) | collective-permute-done | bytes 540704 | tf_op jit(solution)/shard_map/ppermute | solution.py:734
  290.8 7.4 %collective-permute-done.22 = bf16[264,1024]{1,0:T(8,128)(2,1)S(1)} collective-permute-done((bf16[264,1024]{1,0:T(8,128)(2,1)}, bf16[264,1024]{1,0:T(8,128)(2,1)S(1)}, u32[]{:S(2)}, u32[]{:S(2)}) %collective-permute-start.22) | collective-permute-done | bytes 540704 | tf_op jit(solution)/shard_map/ppermute | solution.py:734
  301.2 12.3 %delta_gate_back.1 = (bf16[32,64,128]{2,1,0:T(8,128)(2,1)}, f32[32,128,128]{2,1,0:T(8,128)}, bf16[2048,128]{1,0:T(8,128)(2,1)}, f32[1,128]{1,0:T(1,128)}, f32[128,128]{1,0:T(8,128)}) custom-call(f32[2048,256]{1,0:T(8,128)} %get-tuple-element.230.small_ref.gate_ref, f32[1,128]{1,0:T(1,128)} %reshape.528.gain_ref, f32[2048,128]{1,0:T(8,128)} %get-tuple-element.252.mixed_ref, ...), custom_call_target="tpu_custom_call" | custom-call | flops 15000000512 | bytes 8388608 | tf_op jit(solution)/shard_map/delta_gate_back/pallas_call | solution.py:417
  324.7 10.4 %delta_backward.6 = (bf16[2048,896]{1,0:T(8,128)(2,1)}, f32[4,8,640]{2,1,0:T(8,128)}, f32[8,640]{1,0:T(8,128)}, f32[1,128]{1,0:T(1,128)}) custom-call(s32[1,17]{1,0:T(1,128)} %pad_add_fusion.offs_ref, f32[1,1]{1,0:T(1,128)} %bitcast.2.rate_ref, bf16[2048,640]{1,0:T(8,128)(2,1)} %get-tuple-element.229.pre_ref.prior_ref, ...), custom_call_target="tpu_custom_call" | custom-call | flops 12000000000 | bytes 4089446 | tf_op jit(solution)/shard_map/delta_backward/pallas_call | solution.py:490
  338.5 4.1 all-to-all-start.4
  342.6 10.4 %delta_backward.7 = (bf16[2048,896]{1,0:T(8,128)(2,1)}, f32[4,8,640]{2,1,0:T(8,128)}, f32[8,640]{1,0:T(8,128)}, f32[1,128]{1,0:T(1,128)}) custom-call(s32[1,17]{1,0:T(1,128)} %pad_add_fusion.offs_ref, f32[1,1]{1,0:T(1,128)} %bitcast.2.rate_ref, bf16[2048,640]{1,0:T(8,128)(2,1)} %get-tuple-element.229.pre_ref.prior_ref, ...), custom_call_target="tpu_custom_call", output_to_operand_aliasing={{0}: (18, {})} | custom-call | flops 12000000000 | bytes 4089446 | tf_op jit(solution)/shard_map/delta_backward/pallas_call | solution.py:490
  354.2 3.8 collective-permute-start.30
  358.3 10.4 %delta_backward.8 = (bf16[2048,896]{1,0:T(8,128)(2,1)}, f32[4,8,640]{2,1,0:T(8,128)}, f32[8,640]{1,0:T(8,128)}, f32[1,128]{1,0:T(1,128)}) custom-call(s32[1,17]{1,0:T(1,128)} %pad_add_fusion.offs_ref, f32[1,1]{1,0:T(1,128)} %bitcast.2.rate_ref, bf16[2048,640]{1,0:T(8,128)(2,1)} %get-tuple-element.229.pre_ref.prior_ref, ...), custom_call_target="tpu_custom_call", output_to_operand_aliasing={{0}: (18, {})} | custom-call | flops 12000000000 | bytes 4089446 | tf_op jit(solution)/shard_map/delta_backward/pallas_call | solution.py:490
  368.8 3.3 collective-permute-done.26.refs_1_
  372.6 10.4 %delta_backward.9 = (bf16[2048,896]{1,0:T(8,128)(2,1)}, f32[4,8,640]{2,1,0:T(8,128)}, f32[8,640]{1,0:T(8,128)}, f32[1,128]{1,0:T(1,128)}) custom-call(s32[1,17]{1,0:T(1,128)} %pad_add_fusion.offs_ref, f32[1,1]{1,0:T(1,128)} %bitcast.2.rate_ref, bf16[2048,640]{1,0:T(8,128)(2,1)} %get-tuple-element.229.pre_ref.prior_ref, ...), custom_call_target="tpu_custom_call", output_to_operand_aliasing={{0}: (18, {})} | custom-call | flops 12000000000 | bytes 4089446 | tf_op jit(solution)/shard_map/delta_backward/pallas_call | solution.py:490
  385.4 8.5 %collective-permute-done.29.refs_6_ = bf16[264,1024]{1,0:T(8,128)(2,1)S(1)} collective-permute-done((bf16[264,1024]{1,0:T(8,128)(2,1)S(1)}, bf16[264,1024]{1,0:T(8,128)(2,1)S(1)}, u32[]{:S(2)}, u32[]{:S(2)}) %collective-permute-start.29) | collective-permute-done | bytes 540704 | tf_op jit(solution)/shard_map/ppermute | solution.py:734
  394.2 7.9 %delta_backward.10 = (bf16[2048,896]{1,0:T(8,128)(2,1)}, f32[4,8,640]{2,1,0:T(8,128)}, f32[8,640]{1,0:T(8,128)}, f32[1,128]{1,0:T(1,128)}) custom-call(s32[1,17]{1,0:T(1,128)} %pad_add_fusion.offs_ref, f32[1,1]{1,0:T(1,128)} %bitcast.2.rate_ref, bf16[2048,640]{1,0:T(8,128)(2,1)} %get-tuple-element.229.pre_ref.prior_ref, ...), custom_call_target="tpu_custom_call", output_to_operand_aliasing={{0}: (18, {})} | custom-call | flops 8000000000 | bytes 2726297 | tf_op jit(solution)/shard_map/delta_backward/pallas_call | solution.py:490
  402.1 5.6 collective-permute-done.31.refs_5_
  408.1 7.9 %delta_backward.11 = (bf16[2048,896]{1,0:T(8,128)(2,1)}, f32[4,8,640]{2,1,0:T(8,128)}, f32[8,640]{1,0:T(8,128)}, f32[1,128]{1,0:T(1,128)}) custom-call(s32[1,17]{1,0:T(1,128)} %pad_add_fusion.offs_ref, f32[1,1]{1,0:T(1,128)} %bitcast.2.rate_ref, bf16[2048,640]{1,0:T(8,128)(2,1)} %get-tuple-element.229.pre_ref.prior_ref, ...), custom_call_target="tpu_custom_call", output_to_operand_aliasing={{0}: (18, {})} | custom-call | flops 8000000000 | bytes 2726297 | tf_op jit(solution)/shard_map/delta_backward/pallas_call | solution.py:490
  416.7 4.0 collective-permute-done.32.refs_7_
  421.5 5.5 input_blocks.7
  427.3 8.0 %multiply_reduce_fusion = (f32[1024]{0:T(1024)S(1)}, bf16[1024,896]{1,0:T(8,128)(2,1)}) fusion(bf16[1024,896]{1,0:T(8,128)(2,1)S(1)} %bitcast.165, bf16[2048,1024]{1,0:T(8,128)(2,1)} %get-tuple-element.306, bf16[2048,896]{1,0:T(8,128)(2,1)S(1)} %copy-done.2), kind=kOutput, calls=%fused_computation.5 | convolution fusion | flops 3761765376 | bytes 11538432 | tf_op jit(solution)/shard_map/dot_general | solution.py:20
  439.2 5.4 input_blocks.6
  452.2 5.0 input_blocks.5
  457.2 3.4 collective-permute-done.36
  465.7 5.1 input_blocks.4
  470.8 5.0 collective-permute-done.37
  485.9 4.3 collective-permute-done.38
  496.9 4.7 collective-permute-done.44.refs_1_
  501.5 3.5 collective-permute-start.47
  505.1 14.6 %collective-permute-done.45.refs_2_ = bf16[272,896]{1,0:T(8,128)(2,1)} collective-permute-done((bf16[272,896]{1,0:T(8,128)(2,1)}, bf16[272,896]{1,0:T(8,128)(2,1)}, u32[]{:S(2)}, u32[]{:S(2)}) %collective-permute-start.45) | collective-permute-done | bytes 487456 | tf_op jit(solution)/shard_map/ppermute | solution.py:734
  523.6 5.3 collective-permute-done.47.refs_4_
  531.8 6.7 %ff_outputs.1 = (f32[256,2816]{1,0:T(8,128)}, f32[256,2816]{1,0:T(8,128)}, f32[704,1024]{1,0:T(8,128)}) custom-call(s32[8]{0:T(128)} %stack.195.place_ref, bf16[264,1024]{1,0:T(8,128)(2,1)} %copy-done.20, bf16[264,1024]{1,0:T(8,128)(2,1)} %copy-done.28, bf16[264,1024]{1,0:T(8,128)(2,1)} %copy-done.26, bf16[264,1024]{1,0:T(8,128)(2,1)} %copy-done.29, ...), custom_call_target="tpu_custom_call" | custom-call | bytes 15728640 | tf_op jit(solution)/shard_map/ff_outputs/pallas_call | solution.py:911
  538.5 3.8 collective-permute-start.54
  554.0 7.4 %collective-permute-done.57.refs_15_ = bf16[32,1024]{1,0:T(8,128)(2,1)S(1)} collective-permute-done((bf16[32,1024]{1,0:T(8,128)(2,1)S(1)}, bf16[32,1024]{1,0:T(8,128)(2,1)S(1)}, u32[]{:S(2)}, u32[]{:S(2)}) %collective-permute-start.57) | collective-permute-done | bytes 65568 | tf_op jit(solution)/shard_map/ppermute | solution.py:734
  562.2 6.3 %mixer_outputs.1 = (f32[256,1024]{1,0:T(8,128)}, f32[256,2048]{1,0:T(8,128)}, f32[256,2048]{1,0:T(8,128)}, f32[256,1024]{1,0:T(8,128)}, f32[16,256]{1,0:T(8,128)...) custom-call(s32[1,9]{1,0:T(1,128)} %bitcast.218, ...), custom_call_target="tpu_custom_call" | custom-call | bytes 12582912 | tf_op jit(solution)/shard_map/mixer_outputs/pallas_call | solution.py:878
  (336 shorter events, 182.1 us)
Async XLA Ops:
  0.7 15.1 %collective-permute-start.3 = (bf16[256,1024]{1,0:T(8,128)(2,1)}, bf16[256,1024]{1,0:T(8,128)(2,1)S(1)}, u32[]{:S(2)}, u32[]{:S(2)}) collective-permute-start(bf16[256,1024]{1,0:T(8,128)(2,1)} %bitcast.169), channel_id=1, source_target_pairs={{0,4},{4,0},{8,12},{12,8},{16,20},{20,16},{24,28},{28,24},{1,5},{5... | collective-permute-start | bytes 1572872 | tf_op jit(solution)/shard_map/ppermute | solution.py:734
  3.7 16.9 %collective-permute-start = (bf16[256,1024]{1,0:T(8,128)(2,1)}, bf16[256,1024]{1,0:T(8,128)(2,1)S(1)}, u32[]{:S(2)}, u32[]{:S(2)}) collective-permute-start(bf16[256,1024]{1,0:T(8,128)(2,1)} %bitcast.170), channel_id=1, source_target_pairs={{0,8},{4,12},{8,16},{12,20},{16,24},{20,28},{24,0},{28,4},{1,9},{5... | collective-permute-start | bytes 1572872 | tf_op jit(solution)/shard_map/ppermute | solution.py:734
  5.3 24.5 %collective-permute-start.2 = (bf16[256,1024]{1,0:T(8,128)(2,1)}, bf16[256,1024]{1,0:T(8,128)(2,1)S(1)}, u32[]{:S(2)}, u32[]{:S(2)}) collective-permute-start(bf16[256,1024]{1,0:T(8,128)(2,1)} %bitcast.171), channel_id=1, source_target_pairs={{0,24},{4,28},{8,0},{12,4},{16,8},{20,12},{24,16},{28,20},{1,25},{... | collective-permute-start | bytes 1572872 | tf_op jit(solution)/shard_map/ppermute | solution.py:734
  34.1 16.1 %collective-permute-start.8 = (bf16[2,288,896]{2,1,0:T(8,128)(2,1)}, bf16[2,288,896]{2,1,0:T(8,128)(2,1)S(1)}, u32[]{:S(2)}, u32[]{:S(2)}) collective-permute-start(bf16[2,288,896]{2,1,0:T(8,128)(2,1)} %maximum_select_fusion.5), channel_id=1, source_target_pairs={{0,1},{1,0},{2,3},{3,2},{4,5},{5,4},{6,7},{7,6},{8,9},{9,8},{10,11... | collective-permute-start | bytes 3096584 | tf_op jit(solution)/shard_map/ppermute | solution.py:669
  34.1 14.7 %collective-permute-start.4 = (bf16[256,1024]{1,0:T(8,128)(2,1)}, bf16[256,1024]{1,0:T(8,128)(2,1)}, u32[]{:S(2)}, u32[]{:S(2)}) collective-permute-start(bf16[256,1024]{1,0:T(8,128)(2,1)} %copy-done.35), channel_id=1, source_target_pairs={{0,4},{4,0},{8,12},{12,8},{16,20},{20,16},{24,28},{28,24},{1,5},{5... | collective-permute-start | bytes 1572872 | tf_op jit(solution)/shard_map/ppermute | solution.py:734
  43.1 20.6 %collective-permute-start.1 = (bf16[256,1024]{1,0:T(8,128)(2,1)}, bf16[256,1024]{1,0:T(8,128)(2,1)}, u32[]{:S(2)}, u32[]{:S(2)}) collective-permute-start(bf16[256,1024]{1,0:T(8,128)(2,1)} %copy-done.35), channel_id=1, source_target_pairs={{0,8},{4,12},{8,16},{12,20},{16,24},{20,28},{24,0},{28,4},{1,9},{5... | collective-permute-start | bytes 1572872 | tf_op jit(solution)/shard_map/ppermute | solution.py:734
  48.8 14.9 %collective-permute-start.5 = (bf16[256,1024]{1,0:T(8,128)(2,1)}, bf16[256,1024]{1,0:T(8,128)(2,1)}, u32[]{:S(2)}, u32[]{:S(2)}) collective-permute-start(bf16[256,1024]{1,0:T(8,128)(2,1)} %copy-done.34), channel_id=1, source_target_pairs={{0,4},{4,0},{8,12},{12,8},{16,20},{20,16},{24,28},{28,24},{1,5},{5... | collective-permute-start | bytes 1572872 | tf_op jit(solution)/shard_map/ppermute | solution.py:734
  58.0 29.5 %all-to-all-start = ((bf16[4,256,704]{1,2,0:T(8,128)(2,1)}), bf16[4,256,704]{1,2,0:T(8,128)(2,1)}, u32[]{:S(2)}, u32[]{:S(2)}) async-start(bf16[4,256,704]{1,2,0:T(8,128)(2,1)} %bitcast.178), calls=%async_computation | async-start | bytes 2883584 | tf_op jit(solution)/shard_map/all_to_all | solution.py:1017
  63.7 18.7 %collective-permute-start.6 = (bf16[256,1024]{1,0:T(8,128)(2,1)}, bf16[256,1024]{1,0:T(8,128)(2,1)}, u32[]{:S(2)}, u32[]{:S(2)}) collective-permute-start(bf16[256,1024]{1,0:T(8,128)(2,1)} %collective-permute-done.1.tok_ref), channel_id=1, source_target_pairs={{0,4},{4,0},{8,12},{12,8},{16,20},{20,16},{24,28},{28,24},{1,5},{5... | collective-permute-start | bytes 1572872 | tf_op jit(solution)/shard_map/ppermute | solution.py:734
  65.6 102.8 %collective-permute-start.10 = (bf16[256,1024]{1,0:T(8,128)(2,1)}, bf16[256,1024]{1,0:T(8,128)(2,1)}, u32[]{:S(2)}, u32[]{:S(2)}) collective-permute-start(bf16[256,1024]{1,0:T(8,128)(2,1)} %bitcast.182), channel_id=1, source_target_pairs={{0,2},{1,3},{2,0},{3,1},{4,6},{5,7},{6,4},{7,5},{8,10},{9,11},{10,... | collective-permute-start | bytes 1572872 | tf_op jit(solution)/shard_map/ppermute | solution.py:669
  67.6 100.9 %collective-permute-start.9 = (bf16[256,1024]{1,0:T(8,128)(2,1)}, bf16[256,1024]{1,0:T(8,128)(2,1)}, u32[]{:S(2)}, u32[]{:S(2)}) collective-permute-start(bf16[256,1024]{1,0:T(8,128)(2,1)} %param.45), channel_id=1, source_target_pairs={{0,2},{1,3},{2,0},{3,1},{4,6},{5,7},{6,4},{7,5},{8,10},{9,11},{10,... | collective-permute-start | bytes 1572872 | tf_op jit(solution)/shard_map/ppermute | solution.py:669
  87.5 81.0 %all-to-all-start.1 = ((bf16[4,256,704]{1,2,0:T(8,128)(2,1)}), bf16[4,256,704]{1,2,0:T(8,128)(2,1)S(1)}, u32[]{:S(2)}, u32[]{:S(2)}) async-start(bf16[4,256,704]{1,2,0:T(8,128)(2,1)} %bitcast.19), calls=%async_computation.1 | async-start | bytes 2883584 | tf_op jit(solution)/shard_map/all_to_all | solution.py:1018
  173.9 20.7 %all-to-all-start.2 = ((bf16[8,256,128]{1,2,0:T(8,128)(2,1)}), bf16[8,256,128]{1,2,0:T(8,128)(2,1)S(1)}, u32[]{:S(2)}, u32[]{:S(2)}) async-start(bf16[8,256,128]{1,2,0:T(8,128)(2,1)} %copy.67), calls=%async_computation.2 | async-start | bytes 1048576 | tf_op jit(solution)/shard_map/all_to_all | solution.py:1058
  237.0 13.9 %collective-permute-start.16 = (bf16[256,1024]{1,0:T(8,128)(2,1)S(1)}, bf16[256,1024]{1,0:T(8,128)(2,1)S(1)}, u32[]{:S(2)}, u32[]{:S(2)}) collective-permute-start(bf16[256,1024]{1,0:T(8,128)(2,1)S(1)} %slice.300), channel_id=1, source_target_pairs={{0,2},{1,3},{2,0},{3,1},{4,6},{5,7},{6,4},{7,5},{8,10},{9,11},{10,... | collective-permute-start | bytes 1572872 | tf_op jit(solution)/shard_map/ppermute | solution.py:669
  242.5 17.2 %collective-permute-start.17 = (bf16[264,1024]{1,0:T(8,128)(2,1)}, bf16[264,1024]{1,0:T(8,128)(2,1)}, u32[]{:S(2)}, u32[]{:S(2)}) collective-permute-start(bf16[264,1024]{1,0:T(8,128)(2,1)} %get-tuple-element.344), channel_id=1, source_target_pairs={{0,4},{4,0},{8,12},{12,8},{16,20},{20,16},{24,28},{28,24},{1,5},{5... | collective-permute-start | bytes 1622024 | tf_op jit(solution)/shard_map/ppermute | solution.py:734
  254.9 30.4 %all-to-all-start.3 = ((bf16[256,8,128]{2,0,1:T(8,128)(2,1)}), bf16[256,8,128]{2,0,1:T(8,128)(2,1)}, u32[]{:S(2)}, u32[]{:S(2)}) async-start(bf16[256,8,128]{2,0,1:T(8,128)(2,1)} %copy_bitcast_fusion), calls=%async_computation.3 | async-start | bytes 1048576 | tf_op jit(solution)/shard_map/all_to_all | solution.py:1138
  261.9 21.5 %collective-permute-start.19 = (bf16[264,1024]{1,0:T(8,128)(2,1)}, bf16[264,1024]{1,0:T(8,128)(2,1)}, u32[]{:S(2)}, u32[]{:S(2)}) collective-permute-start(bf16[264,1024]{1,0:T(8,128)(2,1)} %fusion.9), channel_id=1, source_target_pairs={{0,8},{4,12},{8,16},{12,20},{16,24},{20,28},{24,0},{28,4},{1,9},{5... | collective-permute-start | bytes 1622024 | tf_op jit(solution)/shard_map/ppermute | solution.py:734
  264.0 19.4 %collective-permute-start.18 = (bf16[264,1024]{1,0:T(8,128)(2,1)}, bf16[264,1024]{1,0:T(8,128)(2,1)}, u32[]{:S(2)}, u32[]{:S(2)}) collective-permute-start(bf16[264,1024]{1,0:T(8,128)(2,1)} %get-tuple-element.244), channel_id=1, source_target_pairs={{0,4},{4,0},{8,12},{12,8},{16,20},{20,16},{24,28},{28,24},{1,5},{5... | collective-permute-start | bytes 1622024 | tf_op jit(solution)/shard_map/ppermute | solution.py:734
  290.8 26.7 %collective-permute-start.33 = (bf16[512,1024]{1,0:T(8,128)(2,1)}, bf16[512,1024]{1,0:T(8,128)(2,1)}, u32[]{:S(2)}, u32[]{:S(2)}) collective-permute-start(bf16[512,1024]{1,0:T(8,128)(2,1)} %pad_maximum_fusion.4), channel_id=1, source_target_pairs={{0,1},{1,0},{2,3},{3,2},{4,5},{5,4},{6,7},{7,6},{8,9},{9,8},{10,11... | collective-permute-start | bytes 3145736 | tf_op jit(solution)/shard_map/ppermute | solution.py:669
  301.2 20.0 %collective-permute-start.23 = (bf16[264,1024]{1,0:T(8,128)(2,1)}, bf16[264,1024]{1,0:T(8,128)(2,1)}, u32[]{:S(2)}, u32[]{:S(2)}) collective-permute-start(bf16[264,1024]{1,0:T(8,128)(2,1)} %get-tuple-element.341), channel_id=1, source_target_pairs={{0,24},{4,28},{8,0},{12,4},{16,8},{20,12},{24,16},{28,20},{1,25},{... | collective-permute-start | bytes 1622024 | tf_op jit(solution)/shard_map/ppermute | solution.py:734
  315.5 20.6 %collective-permute-start.25 = (bf16[264,1024]{1,0:T(8,128)(2,1)}, bf16[264,1024]{1,0:T(8,128)(2,1)S(1)}, u32[]{:S(2)}, u32[]{:S(2)}) collective-permute-start(bf16[264,1024]{1,0:T(8,128)(2,1)} %get-tuple-element.340), channel_id=1, source_target_pairs={{0,8},{4,12},{8,16},{12,20},{16,24},{20,28},{24,0},{28,4},{1,9},{5... | collective-permute-start | bytes 1622024 | tf_op jit(solution)/shard_map/ppermute | solution.py:734
  319.4 15.7 %collective-permute-start.34 = (bf16[256,1024]{1,0:T(8,128)(2,1)S(1)}, bf16[256,1024]{1,0:T(8,128)(2,1)S(1)}, u32[]{:S(2)}, u32[]{:S(2)}) collective-permute-start(bf16[256,1024]{1,0:T(8,128)(2,1)S(1)} %slice.298), channel_id=1, source_target_pairs={{0,2},{1,3},{2,0},{3,1},{4,6},{5,7},{6,4},{7,5},{8,10},{9,11},{10,... | collective-permute-start | bytes 1572872 | tf_op jit(solution)/shard_map/ppermute | solution.py:669
  321.2 14.9 %collective-permute-start.24 = (bf16[264,1024]{1,0:T(8,128)(2,1)S(1)}, bf16[264,1024]{1,0:T(8,128)(2,1)S(1)}, u32[]{:S(2)}, u32[]{:S(2)}) collective-permute-start(bf16[264,1024]{1,0:T(8,128)(2,1)S(1)} %copy-done.33), channel_id=1, source_target_pairs={{0,4},{4,0},{8,12},{12,8},{16,20},{20,16},{24,28},{28,24},{1,5},{5... | collective-permute-start | bytes 1622024 | tf_op jit(solution)/shard_map/ppermute | solution.py:734
  338.5 14.6 %all-to-all-start.4 = ((bf16[176,4,256]{2,0,1:T(8,128)(2,1)}), bf16[176,4,256]{2,0,1:T(8,128)(2,1)}, u32[]{:S(2)}, u32[]{:S(2)}) async-start(bf16[176,4,256]{2,0,1:T(8,128)(2,1)} %bitcast.196), calls=%async_computation.4 | async-start | bytes 720896 | tf_op jit(solution)/shard_map/all_to_all | solution.py:1098
  354.1 18.0 %collective-permute-start.27 = (bf16[264,1024]{1,0:T(8,128)(2,1)S(1)}, bf16[264,1024]{1,0:T(8,128)(2,1)S(1)}, u32[]{:S(2)}, u32[]{:S(2)}) collective-permute-start(bf16[264,1024]{1,0:T(8,128)(2,1)S(1)} %pad_maximum_fusion.6.refs_0_), channel_id=1, source_target_pairs={{0,8},{4,12},{8,16},{12,20},{16,24},{20,28},{24,0},{28,4},{1,9},{5... | collective-permute-start | bytes 1622024 | tf_op jit(solution)/shard_map/ppermute | solution.py:734
  354.2 39.6 %collective-permute-start.30 = (bf16[264,1024]{1,0:T(8,128)(2,1)S(1)}, bf16[264,1024]{1,0:T(8,128)(2,1)S(1)}, u32[]{:S(2)}, u32[]{:S(2)}) collective-permute-start(bf16[264,1024]{1,0:T(8,128)(2,1)S(1)} %pad_maximum_fusion.6.refs_0_), channel_id=1, source_target_pairs={{0,24},{4,28},{8,0},{12,4},{16,8},{20,12},{24,16},{28,20},{1,25},{... | collective-permute-start | bytes 1622024 | tf_op jit(solution)/shard_map/ppermute | solution.py:734
  358.0 14.1 %collective-permute-start.26 = (bf16[264,1024]{1,0:T(8,128)(2,1)S(1)}, bf16[264,1024]{1,0:T(8,128)(2,1)S(1)}, u32[]{:S(2)}, u32[]{:S(2)}) collective-permute-start(bf16[264,1024]{1,0:T(8,128)(2,1)S(1)} %pad_maximum_fusion.6.refs_0_), channel_id=1, source_target_pairs={{0,4},{4,0},{8,12},{12,8},{16,20},{20,16},{24,28},{28,24},{1,5},{5... | collective-permute-start | bytes 1622024 | tf_op jit(solution)/shard_map/ppermute | solution.py:734
  372.1 13.3 %collective-permute-start.28 = (bf16[264,1024]{1,0:T(8,128)(2,1)S(1)}, bf16[264,1024]{1,0:T(8,128)(2,1)S(1)}, u32[]{:S(2)}, u32[]{:S(2)}) collective-permute-start(bf16[264,1024]{1,0:T(8,128)(2,1)S(1)} %collective-permute-done.27.refs_2_), channel_id=1, source_target_pairs={{0,4},{4,0},{8,12},{12,8},{16,20},{20,16},{24,28},{28,24},{1,5},{5... | collective-permute-start | bytes 1622024 | tf_op jit(solution)/shard_map/ppermute | solution.py:734
  372.4 21.4 %collective-permute-start.29 = (bf16[264,1024]{1,0:T(8,128)(2,1)S(1)}, bf16[264,1024]{1,0:T(8,128)(2,1)S(1)}, u32[]{:S(2)}, u32[]{:S(2)}) collective-permute-start(bf16[264,1024]{1,0:T(8,128)(2,1)S(1)} %collective-permute-done.27.refs_2_), channel_id=1, source_target_pairs={{0,8},{4,12},{8,16},{12,20},{16,24},{20,28},{24,0},{28,4},{1,9},{5... | collective-permute-start | bytes 1622024 | tf_op jit(solution)/shard_map/ppermute | solution.py:734
  393.9 13.9 %collective-permute-start.31 = (bf16[264,1024]{1,0:T(8,128)(2,1)S(1)}, bf16[264,1024]{1,0:T(8,128)(2,1)S(1)}, u32[]{:S(2)}, u32[]{:S(2)}) collective-permute-start(bf16[264,1024]{1,0:T(8,128)(2,1)S(1)} %collective-permute-done.30.refs_4_), channel_id=1, source_target_pairs={{0,4},{4,0},{8,12},{12,8},{16,20},{20,16},{24,28},{28,24},{1,5},{5... | collective-permute-start | bytes 1622024 | tf_op jit(solution)/shard_map/ppermute | solution.py:734
  427.0 17.5 %collective-permute-start.35 = (bf16[288,1024]{1,0:T(8,128)(2,1)}, bf16[288,1024]{1,0:T(8,128)(2,1)}, u32[]{:S(2)}, u32[]{:S(2)}) collective-permute-start(bf16[288,1024]{1,0:T(8,128)(2,1)} %get-tuple-element.299), channel_id=1, source_target_pairs={{0,4},{4,0},{8,12},{12,8},{16,20},{20,16},{24,28},{28,24},{1,5},{5... | collective-permute-start | bytes 1769480 | tf_op jit(solution)/shard_map/ppermute | solution.py:734
  438.5 23.8 %collective-permute-start.42 = (bf16[544,896]{1,0:T(8,128)(2,1)S(1)}, bf16[544,896]{1,0:T(8,128)(2,1)S(1)}, u32[]{:S(2)}, u32[]{:S(2)}) collective-permute-start(bf16[544,896]{1,0:T(8,128)(2,1)S(1)} %pad_maximum_fusion.5), channel_id=1, source_target_pairs={{0,1},{1,0},{2,3},{3,2},{4,5},{5,4},{6,7},{7,6},{8,9},{9,8},{10,11... | collective-permute-start | bytes 2924552 | tf_op jit(solution)/shard_map/ppermute | solution.py:669
  444.6 16.0 %collective-permute-start.36 = (bf16[288,1024]{1,0:T(8,128)(2,1)}, bf16[288,1024]{1,0:T(8,128)(2,1)S(1)}, u32[]{:S(2)}, u32[]{:S(2)}) collective-permute-start(bf16[288,1024]{1,0:T(8,128)(2,1)} %get-tuple-element.300), channel_id=1, source_target_pairs={{0,4},{4,0},{8,12},{12,8},{16,20},{20,16},{24,28},{28,24},{1,5},{5... | collective-permute-start | bytes 1769480 | tf_op jit(solution)/shard_map/ppermute | solution.py:734
  452.0 41.5 %collective-permute-start.20 = (bf16[512,1024]{1,0:T(8,128)(2,1)}, bf16[512,1024]{1,0:T(8,128)(2,1)}, u32[]{:S(2)}, u32[]{:S(2)}) collective-permute-start(bf16[512,1024]{1,0:T(8,128)(2,1)} %slice.296), channel_id=1, source_target_pairs={{0,1},{1,0},{2,3},{3,2},{4,5},{5,4},{6,7},{7,6},{8,9},{9,8},{10,11... | collective-permute-start | bytes 3145736 | tf_op jit(solution)/shard_map/ppermute | solution.py:669
  460.6 15.3 %collective-permute-start.37 = (bf16[288,1024]{1,0:T(8,128)(2,1)}, bf16[288,1024]{1,0:T(8,128)(2,1)}, u32[]{:S(2)}, u32[]{:S(2)}) collective-permute-start(bf16[288,1024]{1,0:T(8,128)(2,1)} %get-tuple-element.301), channel_id=1, source_target_pairs={{0,4},{4,0},{8,12},{12,8},{16,20},{20,16},{24,28},{28,24},{1,5},{5... | collective-permute-start | bytes 1769480 | tf_op jit(solution)/shard_map/ppermute | solution.py:734
  463.4 15.3 %collective-permute-start.43 = (bf16[272,896]{1,0:T(8,128)(2,1)}, bf16[272,896]{1,0:T(8,128)(2,1)}, u32[]{:S(2)}, u32[]{:S(2)}) collective-permute-start(bf16[272,896]{1,0:T(8,128)(2,1)} %slice.301), channel_id=1, source_target_pairs={{0,2},{1,3},{2,0},{3,1},{4,6},{5,7},{6,4},{7,5},{8,10},{9,11},{10,... | collective-permute-start | bytes 1462280 | tf_op jit(solution)/shard_map/ppermute | solution.py:669
  465.6 18.2 %collective-permute-start.40 = (bf16[288,1024]{1,0:T(8,128)(2,1)S(1)}, bf16[288,1024]{1,0:T(8,128)(2,1)S(1)}, u32[]{:S(2)}, u32[]{:S(2)}) collective-permute-start(bf16[288,1024]{1,0:T(8,128)(2,1)S(1)} %add_convert_fusion.1), channel_id=1, source_target_pairs={{0,8},{4,12},{8,16},{12,20},{16,24},{20,28},{24,0},{28,4},{1,9},{5... | collective-permute-start | bytes 1769480 | tf_op jit(solution)/shard_map/ppermute | solution.py:734
  475.9 14.4 %collective-permute-start.38 = (bf16[288,1024]{1,0:T(8,128)(2,1)}, bf16[288,1024]{1,0:T(8,128)(2,1)}, u32[]{:S(2)}, u32[]{:S(2)}) collective-permute-start(bf16[288,1024]{1,0:T(8,128)(2,1)} %get-tuple-element.302), channel_id=1, source_target_pairs={{0,4},{4,0},{8,12},{12,8},{16,20},{20,16},{24,28},{28,24},{1,5},{5... | collective-permute-start | bytes 1769480 | tf_op jit(solution)/shard_map/ppermute | solution.py:734
  478.6 41.3 %collective-permute-start.39 = (bf16[288,1024]{1,0:T(8,128)(2,1)}, bf16[288,1024]{1,0:T(8,128)(2,1)}, u32[]{:S(2)}, u32[]{:S(2)}) collective-permute-start(bf16[288,1024]{1,0:T(8,128)(2,1)} %add_convert_fusion.2), channel_id=1, source_target_pairs={{0,24},{4,28},{8,0},{12,4},{16,8},{20,12},{24,16},{28,20},{1,25},{... | collective-permute-start | bytes 1769480 | tf_op jit(solution)/shard_map/ppermute | solution.py:734
  485.9 34.0 %collective-permute-start.41 = (bf16[288,1024]{1,0:T(8,128)(2,1)}, bf16[288,1024]{1,0:T(8,128)(2,1)}, u32[]{:S(2)}, u32[]{:S(2)}) collective-permute-start(bf16[288,1024]{1,0:T(8,128)(2,1)} %add_convert_fusion), channel_id=1, source_target_pairs={{0,8},{4,12},{8,16},{12,20},{16,24},{20,28},{24,0},{28,4},{1,9},{5... | collective-permute-start | bytes 1769480 | tf_op jit(solution)/shard_map/ppermute | solution.py:734
  490.2 29.4 %collective-permute-start.45 = (bf16[272,896]{1,0:T(8,128)(2,1)}, bf16[272,896]{1,0:T(8,128)(2,1)}, u32[]{:S(2)}, u32[]{:S(2)}) collective-permute-start(bf16[272,896]{1,0:T(8,128)(2,1)} %fusion.19.refs_0_), channel_id=1, source_target_pairs={{0,8},{4,12},{8,16},{12,20},{16,24},{20,28},{24,0},{28,4},{1,9},{5... | collective-permute-start | bytes 1462280 | tf_op jit(solution)/shard_map/ppermute | solution.py:734
  495.9 34.4 %collective-permute-start.21 = (bf16[256,1024]{1,0:T(8,128)(2,1)S(1)}, bf16[256,1024]{1,0:T(8,128)(2,1)S(1)}, u32[]{:S(2)}, u32[]{:S(2)}) collective-permute-start(bf16[256,1024]{1,0:T(8,128)(2,1)S(1)} %slice.299), channel_id=1, source_target_pairs={{0,2},{1,3},{2,0},{3,1},{4,6},{5,7},{6,4},{7,5},{8,10},{9,11},{10,... | collective-permute-start | bytes 1572872 | tf_op jit(solution)/shard_map/ppermute | solution.py:669
  501.5 27.4 %collective-permute-start.47 = (bf16[272,896]{1,0:T(8,128)(2,1)}, bf16[272,896]{1,0:T(8,128)(2,1)}, u32[]{:S(2)}, u32[]{:S(2)}) collective-permute-start(bf16[272,896]{1,0:T(8,128)(2,1)} %fusion.19.refs_0_), channel_id=1, source_target_pairs={{0,24},{4,28},{8,0},{12,4},{16,8},{20,12},{24,16},{28,20},{1,25},{... | collective-permute-start | bytes 1462280 | tf_op jit(solution)/shard_map/ppermute | solution.py:734
  521.8 20.5 %collective-permute-start.52 = (bf16[32,1024]{1,0:T(8,128)(2,1)S(1)}, bf16[32,1024]{1,0:T(8,128)(2,1)S(1)}, u32[]{:S(2)}, u32[]{:S(2)}) collective-permute-start(bf16[32,1024]{1,0:T(8,128)(2,1)S(1)} %slice.302.refs_8_), channel_id=1, source_target_pairs={{0,8},{4,12},{8,16},{12,20},{16,24},{20,28},{24,0},{28,4},{1,9},{5... | collective-permute-start | bytes 196616 | tf_op jit(solution)/shard_map/ppermute | solution.py:734
  521.8 20.4 %collective-permute-start.51 = (bf16[32,1024]{1,0:T(8,128)(2,1)S(1)}, bf16[32,1024]{1,0:T(8,128)(2,1)S(1)}, u32[]{:S(2)}, u32[]{:S(2)}) collective-permute-start(bf16[32,1024]{1,0:T(8,128)(2,1)S(1)} %slice.302.refs_8_), channel_id=1, source_target_pairs={{0,4},{4,0},{8,12},{12,8},{16,20},{20,16},{24,28},{28,24},{1,5},{5... | collective-permute-start | bytes 196616 | tf_op jit(solution)/shard_map/ppermute | solution.py:734
  529.0 18.9 %collective-permute-start.49 = (bf16[272,896]{1,0:T(8,128)(2,1)}, bf16[272,896]{1,0:T(8,128)(2,1)}, u32[]{:S(2)}, u32[]{:S(2)}) collective-permute-start(bf16[272,896]{1,0:T(8,128)(2,1)} %collective-permute-done.45.refs_2_), channel_id=1, source_target_pairs={{0,8},{4,12},{8,16},{12,20},{16,24},{20,28},{24,0},{28,4},{1,9},{5... | collective-permute-start | bytes 1462280 | tf_op jit(solution)/shard_map/ppermute | solution.py:734
  529.9 17.9 %collective-permute-start.48 = (bf16[272,896]{1,0:T(8,128)(2,1)}, bf16[272,896]{1,0:T(8,128)(2,1)}, u32[]{:S(2)}, u32[]{:S(2)}) collective-permute-start(bf16[272,896]{1,0:T(8,128)(2,1)} %collective-permute-done.47.refs_4_), channel_id=1, source_target_pairs={{0,4},{4,0},{8,12},{12,8},{16,20},{20,16},{24,28},{28,24},{1,5},{5... | collective-permute-start | bytes 1462280 | tf_op jit(solution)/shard_map/ppermute | solution.py:734
  547.8 13.5 %collective-permute-start.50 = (bf16[272,896]{1,0:T(8,128)(2,1)}, bf16[272,896]{1,0:T(8,128)(2,1)S(1)}, u32[]{:S(2)}, u32[]{:S(2)}) collective-permute-start(bf16[272,896]{1,0:T(8,128)(2,1)} %collective-permute-done.49.refs_6_), channel_id=1, source_target_pairs={{0,4},{4,0},{8,12},{12,8},{16,20},{20,16},{24,28},{28,24},{1,5},{5... | collective-permute-start | bytes 1462280 | tf_op jit(solution)/shard_map/ppermute | solution.py:734
  (77 other events, 938.4 us)

commit v4 on v3

--- a/solution.py
+++ b/solution.py
@@ -8,6 +8,7 @@
 from jax.sharding import PartitionSpec as P
 
 SPAN = 64
+PER = 4
 ROWS = 128
 HEAD = 128
 EPSILON = 1e-06
@@ -29,16 +30,6 @@
 
 def mm(left, right, left_dim=1, right_dim=0):
     return contract(left.astype(LOW), right.astype(LOW), left_dim, right_dim)
-
-
-def mm3(left, right, left_dim=1, right_dim=0):
-    lh, ll = halves(left)
-    rh, rl = halves(right)
-    return (
-        contract(lh, rh, left_dim, right_dim)
-        + contract(lh, rl, left_dim, right_dim)
-        + contract(ll, rh, left_dim, right_dim)
-    )
 
 
 def stack(*parts):
@@ -104,13 +95,23 @@
     return beta, decay, strict, carry, leave, carry_all, tok ^ tok_c
 
 
+def in_turns(bodies):
+    bodies = list(bodies)
+    while bodies:
+        bodies = [body for body in bodies if next(body, "end") != "end"]
+
+
 def unit_lower_inverse(strict_part, apart):
     row = lax.broadcasted_iota(jnp.int32, (ROWS, ROWS), 0)
     col = lax.broadcasted_iota(jnp.int32, (ROWS, ROWS), 1)
     inverse = jnp.where(row == col, 1.0, 0.0) - jnp.where(apart == 0, strict_part, 0.0)
     for level in range(6):
         block = jnp.where((apart >> level) == 1, strict_part, 0.0)
-        inverse = inverse - mm(mm(inverse, block), inverse)
+        low = inverse.astype(LOW)
+        half = contract(low, block.astype(LOW), 1, 0).astype(LOW)
+        yield
+        inverse = inverse - contract(half, low, 1, 0)
+        yield
     return inverse
 
 
@@ -122,26 +123,29 @@
     span_count, doc_count, group,
     offs_ref, rate_ref, pre_ref, prior_ref, small_ref, gate_ref, edge_ref, taps_ref, gain_ref,
     state_ref,
-    conv_ref, t_ref, sc_ref, qh_ref, a_ref, gated_ref, mixed_ref, u_ref, s_ref, end_ref,
-    w_scr, u0_scr, b_scr, o0_scr, a_scr, qh_scr,
+    conv_ref, t_ref, sc_ref, qh_ref, ah_ref, al_ref, gated_ref, mixed_ref, u_ref, s_ref, end_ref,
+    w_scr, u0_scr, b_scr, o0_scr, ah_scr, al_scr, qh_scr,
 ):
     step = pl.program_id(0)
     base = offs_ref[0, doc_count]
     rate = rate_ref[0, 0]
     prior = jnp.where(step == 0, edge_ref[...].astype(WIDE), prior_ref[...].astype(WIDE))
 
-    for u in range(group):
+    def local(u):
         c = step * group + u
         here = pre_ref[u * SPAN : (u + 1) * SPAN, :].astype(WIDE)
         if u:
-            prior = pre_ref[u * SPAN - 16 : u * SPAN, :].astype(WIDE)
-        rows = stack(prior, here)
+            before = pre_ref[u * SPAN - 16 : u * SPAN, :].astype(WIDE)
+        else:
+            before = prior
+        rows = stack(before, here)
         pos = span_tokens(offs_ref, doc_count, base + c * SPAN)
         conv = taps_ref[0:1, :] * here
         for lag in range(1, 4):
             shifted = rows[16 - lag : 16 - lag + SPAN]
             conv = conv + jnp.where(pos >= lag, taps_ref[lag : lag + 1, :] * shifted, 0.0)
         conv_ref[u * SPAN : (u + 1) * SPAN, :] = conv
+        yield
         act = conv * jax.nn.sigmoid(conv)
         query, _ = unit(act[:, 0:128])
         key0, _ = unit(act[:, 128:256])
@@ -150,10 +154,15 @@
         values = stack(act[:, 384:512], act[:, 512:640])
         small = small_ref[u * SPAN : (u + 1) * SPAN, :]
         beta, decay, strict, carry, leave, carry_all, apart = span_factors(small, rate, pos)
+        yield
         inner = mm(keys, keys, 1, 1)
-        inverse = unit_lower_inverse(jnp.where(strict, beta * decay * inner, 0.0), apart)
+        yield
+        inverse = yield from unit_lower_inverse(
+            jnp.where(strict, beta * decay * inner, 0.0), apart
+        )
         t_ref[u] = inverse.astype(LOW)
         both = mm(inverse, jnp.concatenate([(beta * carry) * keys, beta * values], axis=1))
+        yield
         weight, fresh = both[:, :HEAD], both[:, HEAD:]
         w_scr[c] = weight.astype(LOW)
         u0_scr[c] = fresh
@@ -161,44 +170,66 @@
         row = lax.broadcasted_iota(jnp.int32, (HEAD, HEAD), 0)
         col = lax.broadcasted_iota(jnp.int32, (HEAD, HEAD), 1)
         step_map = jnp.where(row == col, carry_all, 0.0) - mm(leaving, weight, 0, 0)
-        a_ref[u] = step_map
-        a_scr[c] = step_map
+        map_high, map_rest = halves(step_map)
+        ah_ref[u], al_ref[u] = map_high, map_rest
+        ah_scr[c], al_scr[c] = map_high, map_rest
+        yield
         b_scr[c] = mm(fresh, leaving, 0, 0)
+        yield
         scores = mm(query, keys, 1, 1) * decay[SPAN:, :]
+        yield
         sc_ref[u] = scores.astype(LOW)
         mixed_both = mm(scores, both)
+        yield
         reach = (carry[SPAN:] * query - mixed_both[:, :HEAD]).astype(LOW)
         qh_ref[u] = reach
         qh_scr[c] = reach
         o0_scr[c] = mixed_both[:, HEAD:]
 
-    def chain(c, state):
-        s_ref[c] = state
-        low = state.astype(LOW)
+    in_turns(local(u) for u in range(group))
+
+    def chain(i, state):
+        for u in range(4):
+            c = i * 4 + u
+            s_ref[c] = state
+            high, rest = halves(state)
+            state = (
+                contract(high, ah_scr[c], 1, 1)
+                + contract(high, al_scr[c], 1, 1)
+                + contract(rest, ah_scr[c], 1, 1)
+                + b_scr[c]
+            )
+        return state
+
+    def mixing(c):
+        low = s_ref[c].astype(LOW)
         u_ref[c] = (u0_scr[c] - contract(w_scr[c], low, 1, 1)).astype(LOW)
+        yield
         mixed = o0_scr[c] + contract(qh_scr[c], low, 1, 1)
+        yield
         lo = pl.multiple_of(c * SPAN, SPAN)
         mixed_ref[pl.ds(lo, SPAN), :] = mixed
+        scale = lax.rsqrt(jnp.mean(mixed * mixed, axis=1, keepdims=True) + EPSILON)
+        yield
         gate = gate_ref[pl.ds(lo, SPAN), :]
-        scale = lax.rsqrt(jnp.mean(mixed * mixed, axis=1, keepdims=True) + EPSILON)
         gated_ref[pl.ds(lo, SPAN), :] = (
             mixed * scale * gain_ref[...] * (gate * jax.nn.sigmoid(gate))
         ).astype(LOW)
-        return mm3(state, a_scr[c], 1, 1) + b_scr[c]
-
-    def chain_step(i, state):
-        for u in range(4):
-            state = chain(i * 4 + u, state)
-        return state
+        yield
+
+    def mixing_step(i, none):
+        in_turns(mixing(i * 8 + u) for u in range(8))
+        return none
 
     @pl.when(step == pl.num_programs(0) - 1)
     def _():
-        end_ref[...] = lax.fori_loop(0, span_count // 4, chain_step, state_ref[...])
+        end_ref[...] = lax.fori_loop(0, span_count // 4, chain, state_ref[...])
+        lax.fori_loop(0, span_count // 8, mixing_step, 0)
 
 
 def gate_back_kernel(
     span_count,
-    gate_ref, gain_ref, mixed_ref, qh_ref, a_ref, dgated_ref, dend_ref,
+    gate_ref, gain_ref, mixed_ref, qh_ref, ah_ref, al_ref, dgated_ref, dend_ref,
     do_ref, ds_ref, dgate_ref, dgain_ref, dbegin_ref,
     f_scr,
 ):
@@ -210,6 +241,7 @@
         gate = gate_ref[pl.ds(lo, SPAN), :]
         scale = lax.rsqrt(jnp.mean(mixed * mixed, axis=1, keepdims=True) + EPSILON)
         normed = mixed * scale
+        yield
         sig = jax.nn.sigmoid(gate)
         grad = dgated_ref[pl.ds(lo, SPAN), :].astype(WIDE)
         by_gain = grad * normed
@@ -217,24 +249,31 @@
             by_gain * gain_ref[...] * (sig * (1.0 + gate * (1.0 - sig)))
         ).astype(LOW)
         dgain_ref[...] += jnp.sum(by_gain * (gate * sig), axis=0, keepdims=True)
+        yield
         dn = grad * (gate * sig) * gain_ref[...]
         dmixed = scale * (dn - normed * jnp.mean(dn * normed, axis=1, keepdims=True))
         do_low = dmixed.astype(LOW)
         do_ref[c] = do_low
+        yield
         f_scr[c] = contract(do_low, qh_ref[c], 0, 0)
 
     def gate_step(i, none):
-        for u in range(4):
-            gate_back(i * 4 + u)
+        in_turns(gate_back(i * 8 + u) for u in range(8))
         return none
 
-    lax.fori_loop(0, span_count // 4, gate_step, 0)
+    lax.fori_loop(0, span_count // 8, gate_step, 0)
 
     def chain_step(i, grad):
         for u in range(4):
             c = span_count - 1 - (i * 4 + u)
             ds_ref[c] = grad
-            grad = mm3(grad, a_ref[c]) + f_scr[c]
+            high, rest = halves(grad)
+            grad = (
+                contract(high, ah_ref[c], 1, 0)
+                + contract(high, al_ref[c], 1, 0)
+                + contract(rest, ah_ref[c], 1, 0)
+                + f_scr[c]
+            )
         return grad
 
     dbegin_ref[...] = lax.fori_loop(0, span_count // 4, chain_step, dend_ref[...])
@@ -258,35 +297,43 @@
         drate_ref[...] = drate_in[...]
 
     dy_ref[:, 640:768] = dgate_ref[...]
-    for n in (1, 0):
+
+    def local(n):
         lo, hi = n * SPAN, (n + 1) * SPAN
-        pos = span_tokens(offs_ref, doc_count, base + block * 2 * SPAN + lo)
+        pos = span_tokens(offs_ref, doc_count, base + block * PER * SPAN + lo)
         conv = conv_ref[lo:hi, :]
         sig = jax.nn.sigmoid(conv)
         act = conv * sig
         query, scale_q = unit(act[:, 0:128])
         key0, scale_0 = unit(act[:, 128:256])
         key1, scale_1 = unit(act[:, 256:384])
+        yield
         keys = stack(key0, key1)
         values = stack(act[:, 384:512], act[:, 512:640])
         small = small_ref[lo:hi, :]
         beta, decay, strict, carry, leave, carry_all, _ = span_factors(small, rate, pos)
+        yield
         state, dstate = s_ref[n], ds_ref[n]
         state_l, dstate_l = state.astype(LOW), dstate.astype(LOW)
         upd, out_grad, keys_l = u_ref[n], do_ref[n], keys.astype(LOW)
         dupd = contract(sc_ref[n], out_grad, 0, 0) + mm(keys * leave, dstate_l, 1, 1)
+        yield
         dtarget = mm(t_ref[n], dupd, 0, 0)
+        yield
         pair = stack(dtarget.astype(LOW), out_grad)
         by_upd = contract(pair, upd, 1, 1)
         by_state = contract(pair, state_l, 1, 0)
+        yield
         dinner = jnp.where(strict, -by_upd[:ROWS] * decay, 0.0)
         dscore = by_upd[ROWS:] * decay[SPAN:, :]
         both = stack(dinner, dscore).astype(LOW)
         reading = contract(both, keys_l, 1, 0)
+        yield
         read_key = reading[:ROWS] - carry * by_state[:ROWS]
         dquery = reading[ROWS:] + carry[SPAN:] * by_state[ROWS:]
         dleave = leave * contract(upd, dstate_l, 1, 0)
         write_key = contract(both, stack(beta * keys, query).astype(LOW), 0, 0) + dleave
+        yield
         key_read = jnp.sum(keys * read_key, axis=1, keepdims=True)
         dbeta = jnp.sum(dtarget * values, axis=1, keepdims=True) + key_read
         dcum = beta * key_read - jnp.sum(keys * write_key, axis=1, keepdims=True)
@@ -302,6 +349,7 @@
         upper = jnp.where(tok <= tok_c, 1.0, 0.0).astype(LOW)
         high, rest = halves(jnp.broadcast_to(dcum, (SPAN, 128)))
         dlog = contract(upper, high, 1, 0) + contract(upper, rest, 1, 0)
+        yield
         soft = softplus(small)
         sig_small = jax.nn.sigmoid(small)
         lane = lax.broadcasted_iota(jnp.int32, (SPAN, 128), 1)
@@ -309,6 +357,7 @@
         dsig = jnp.where(lane == 0, dbeta[:SPAN], dbeta[SPAN:]) * sig_small * (1.0 - sig_small)
         dsmall = jnp.where(lane < 2, dsig, jnp.where(lane == 2, -rate * dlog * sig_small, 0.0))
         dy_ref[lo:hi, 768:896] = dsmall.astype(LOW)
+        yield
         dkey = beta * read_key + write_key
         dvalue = beta * dtarget
 
@@ -326,6 +375,7 @@
             axis=1,
         )
         dconv = dact * (sig * (1.0 + conv * (1.0 - sig)))
+        yield
         here = pre_ref[lo:hi, :].astype(WIDE)
         if n:
             prior = pre_ref[lo - 16 : lo, :].astype(WIDE)
@@ -345,6 +395,8 @@
             next_ref[lag] = kept[0:8]
         dy_ref[lo:hi, 0:640] = dpre.astype(LOW)
 
+    in_turns(local(n) for n in reversed(range(PER)))
+
 
 def vmem_spec():
     return pl.BlockSpec(memory_space=pltpu.VMEM)
@@ -365,14 +417,15 @@
 def run_forward(offs, rate, pre, gs, edge, taps, gain, state):
     tokens = pre.shape[0]
     spans = tokens // SPAN
-    group = 4
+    group = 8
     shape = jax.ShapeDtypeStruct
     outs = (
         (shape((tokens, 640), WIDE), pl.BlockSpec((group * SPAN, 640), lambda i: (i, 0))),
         (shape((spans, ROWS, ROWS), LOW), pl.BlockSpec((group, ROWS, ROWS), lambda i: (i, 0, 0))),
         (shape((spans, SPAN, ROWS), LOW), pl.BlockSpec((group, SPAN, ROWS), lambda i: (i, 0, 0))),
         (shape((spans, SPAN, HEAD), LOW), pl.BlockSpec((group, SPAN, HEAD), lambda i: (i, 0, 0))),
-        (shape((spans, HEAD, HEAD), WIDE), pl.BlockSpec((group, HEAD, HEAD), lambda i: (i, 0, 0))),
+        (shape((spans, HEAD, HEAD), LOW), pl.BlockSpec((group, HEAD, HEAD), lambda i: (i, 0, 0))),
+        (shape((spans, HEAD, HEAD), LOW), pl.BlockSpec((group, HEAD, HEAD), lambda i: (i, 0, 0))),
         (shape((tokens, HEAD), LOW), fixed((tokens, HEAD))),
         (shape((tokens, HEAD), WIDE), fixed((tokens, HEAD))),
         (shape((spans, ROWS, HEAD), LOW), fixed((spans, ROWS, HEAD))),
@@ -401,7 +454,8 @@
             pltpu.VMEM((spans, ROWS, HEAD), WIDE),
             pltpu.VMEM((spans, HEAD, HEAD), WIDE),
             pltpu.VMEM((spans, SPAN, HEAD), WIDE),
-            pltpu.VMEM((spans, HEAD, HEAD), WIDE),
+            pltpu.VMEM((spans, HEAD, HEAD), LOW),
+            pltpu.VMEM((spans, HEAD, HEAD), LOW),
             pltpu.VMEM((spans, SPAN, HEAD), LOW),
         ],
         compiler_params=pltpu.CompilerParams(vmem_limit_bytes=VMEM_LIMIT),
@@ -410,7 +464,7 @@
     )(offs, rate, pre, pre, gs, gs, edge, taps, gain, state)
 
 
-def run_gate_back(gs, gain, mixed, qh, steps, dgated, dend):
+def run_gate_back(gs, gain, mixed, qh, high, rest, dgated, dend):
     tokens = mixed.shape[0]
     spans = tokens // SPAN
     shape = jax.ShapeDtypeStruct
@@ -430,6 +484,7 @@
             fixed((tokens, HEAD)),
             fixed((spans, SPAN, HEAD)),
             fixed((spans, HEAD, HEAD)),
+            fixed((spans, HEAD, HEAD)),
             fixed((tokens, HEAD)),
             fixed((HEAD, HEAD)),
         ],
@@ -444,7 +499,7 @@
         compiler_params=pltpu.CompilerParams(vmem_limit_bytes=VMEM_LIMIT),
         cost_estimate=estimate(15e9, 8),
         name="delta_gate_back",
-    )(gs, gain, mixed, qh, steps, dgated, dend)
+    )(gs, gain, mixed, qh, high, rest, dgated, dend)
 
 
 def run_backward(last, steps, offs, rate, pre, gs, edge, taps, saved, carried, dy):
@@ -455,10 +510,10 @@
         return last - i
 
     def rows(columns, lane=0):
-        return pl.BlockSpec((2 * SPAN, columns), lambda i: (at(i), lane))
+        return pl.BlockSpec((PER * SPAN, columns), lambda i: (at(i), lane))
 
     def spans(a, b):
-        return pl.BlockSpec((2, a, b), lambda i: (at(i), 0, 0))
+        return pl.BlockSpec((PER, a, b), lambda i: (at(i), 0, 0))
 
     shape = jax.ShapeDtypeStruct
     carried_specs = [fixed((4, 8, 640)), fixed((8, 640)), fixed((1, HEAD))]
@@ -468,7 +523,7 @@
         smem_spec(),
         smem_spec(),
         rows(640),
-        pl.BlockSpec((16, 640), lambda i: (jnp.maximum(at(i) * (2 * SPAN // 16) - 1, 0), 0)),
+        pl.BlockSpec((16, 640), lambda i: (jnp.maximum(at(i) * (PER * SPAN // 16) - 1, 0), 0)),
         rows(HEAD, 1),
         fixed((16, 640)),
         fixed((8, 640)),
@@ -500,7 +555,7 @@
         out_specs=(rows(896), *carried_specs),
         input_output_aliases=aliases,
         compiler_params=pltpu.CompilerParams(vmem_limit_bytes=VMEM_LIMIT),
-        cost_estimate=estimate(4e9 * steps, 1.3 * steps),
+        cost_estimate=estimate(4e9 * steps, 2.6 * steps),
         name="delta_backward",
     )(*operands)
     return dy, carried
@@ -538,6 +593,59 @@
     )(jnp.stack(places).astype(jnp.int32), dy, grad_out, weights)
 
 
+def weight_grads_kernel(
+    taps, at_ref, low_ref, dy_ref, w_ref, gain_ref, gff_ref, gh_ref, rate_ref, taps_ref, to_ref
+):
+    shard = w_ref.shape[0]
+    grads = contract(low_ref[...], dy_ref[...], 0, 0)
+    to_ref[:shard, :] = grads.astype(LOW)
+    sums = jnp.sum(grads * w_ref[...].astype(WIDE), axis=1, keepdims=True)
+    row = jnp.broadcast_to(sums, (shard, HEAD)).T[0:1] / gain_ref[...]
+
+    def wide(value):
+        return jnp.concatenate(
+            [value, jnp.zeros((value.shape[0], 896 - value.shape[1]), WIDE)], axis=1
+        )
+
+    to_ref[shard:, :] = stack(
+        wide(row),
+        wide(gff_ref[...]),
+        wide(gh_ref[0]),
+        wide(rate_ref[...]),
+        wide(taps_ref[:taps, :]),
+        jnp.zeros((12 - taps, 896), WIDE),
+    ).astype(LOW)
+
+
+def weight_grads(order, low, dy, weights, gain, gain_ffn, gain_head, rate, taps_grad, taps):
+    length, width = low.shape
+    members = order.shape[0]
+    shard = width // members
+    gh = jnp.pad(gain_head.reshape(members, 1, -1), ((0, 0), (0, 0), (0, HEAD)))[:, :, :HEAD]
+    return pl.pallas_call(
+        functools.partial(weight_grads_kernel, taps),
+        out_shape=jax.ShapeDtypeStruct((members * (shard + 16), 896), LOW),
+        grid_spec=pltpu.PrefetchScalarGridSpec(
+            num_scalar_prefetch=1,
+            grid=(members,),
+            in_specs=[
+                pl.BlockSpec((length, shard), lambda i, p: (0, p[i])),
+                fixed((length, 896)),
+                pl.BlockSpec((shard, 896), lambda i, p: (p[i], 0)),
+                pl.BlockSpec((1, shard), lambda i, p: (0, p[i])),
+                pl.BlockSpec((1, shard), lambda i, p: (0, p[i])),
+                pl.BlockSpec((1, 1, HEAD), lambda i, p: (p[i], 0, 0)),
+                fixed((1, HEAD)),
+                fixed((8, 640)),
+            ],
+            out_specs=pl.BlockSpec((shard + 16, 896), lambda i, p: (i, 0)),
+        ),
+        compiler_params=pltpu.CompilerParams(vmem_limit_bytes=VMEM_LIMIT),
+        cost_estimate=estimate(2 * length * width * 896, 12),
+        name="weight_grads",
+    )(order, low, dy, weights, gain, gain_ffn, gh, rate, taps_grad)
+
+
 def pack_kernel(
     heads, taps,
     place_ref, q_ref, k0_ref, k1_ref, v0_ref, v1_ref, g_ref, beta_ref, decay_ref, gin_ref,
@@ -602,42 +710,43 @@
     )(head.reshape(1), w_query, w_key, w_key, w_value, w_value, w_outgate, *small)
 
 
-def project_kernel(place_ref, tok_ref, other_ref, gain_ref, w_ref, *refs):
-    low_ref, pre_ref, gs_ref = refs[-3:]
-    values = jnp.where(pl.program_id(0) == 0, tok_ref[...], other_ref[...]).astype(WIDE)
-    scale = lax.rsqrt(jnp.mean(values * values, axis=1, keepdims=True) + EPSILON)
-    normed = (values * scale * gain_ref[...]).astype(LOW)
-    low_ref[...] = normed
+def project_kernel(count, place_ref, gain_ref, w_ref, *refs):
+    tok_refs, (low_ref, pre_ref, gs_ref) = refs[:count], refs[count:]
+    for n in range(count):
+
+        @pl.when(pl.program_id(0) == n)
+        def _():
+            values = tok_refs[n][...].astype(WIDE)
+            scale = lax.rsqrt(jnp.mean(values * values, axis=1, keepdims=True) + EPSILON)
+            low_ref[...] = (values * scale * gain_ref[...]).astype(LOW)
+
+    normed = low_ref[...]
     pre_ref[...] = contract(normed, w_ref[:, :640], 1, 0).astype(LOW)
     gs_ref[...] = contract(normed, w_ref[:, 640:], 1, 0)
 
 
-def project(places, rows, other, gain, weights, length, filled):
-    count, width = rows.shape
+def project(found, gain, weights):
+    blocks = [one for a, x, b, y in found for one in ((a, x), (b, y))]
+    places = jnp.stack([place for place, _ in blocks]).astype(jnp.int32)
+    count, (rows, width) = len(blocks), blocks[0][1].shape
     shape = jax.ShapeDtypeStruct
-    operands = [places, rows, other, gain, weights]
-    in_specs = [fixed(a.shape) for a in operands[1:]]
-    aliases = {}
-    if filled is not None:
-        aliases = {len(operands) + i: i for i in range(3)}
-        operands += filled
-        in_specs += [pl.BlockSpec(memory_space=pl.ANY)] * 3
     return pl.pallas_call(
-        project_kernel,
-        out_shape=[shape((length, n), t) for n, t in ((width, LOW), (640, LOW), (256, WIDE))],
+        functools.partial(project_kernel, count),
+        out_shape=[
+            shape((count * rows, n), t) for n, t in ((width, LOW), (640, LOW), (256, WIDE))
+        ],
         grid_spec=pltpu.PrefetchScalarGridSpec(
             num_scalar_prefetch=1,
-            grid=(2,),
-            in_specs=in_specs,
+            grid=(count,),
+            in_specs=[fixed(gain.shape), fixed(weights.shape)] + [fixed((rows, width))] * count,
             out_specs=[
-                pl.BlockSpec((count, n), lambda i, p: (p[i], 0)) for n in (width, 640, 256)
+                pl.BlockSpec((rows, n), lambda i, p: (p[i], 0)) for n in (width, 640, 256)
             ],
         ),
-        input_output_aliases=aliases,
         compiler_params=pltpu.CompilerParams(vmem_limit_bytes=VMEM_LIMIT),
-        cost_estimate=estimate(4 * count * width * 896, 6),
+        cost_estimate=estimate(2 * count * rows * width * 896, 13),
         name="project",
-    )(*operands)
+    )(places, gain, weights, *(value for _, value in blocks))
 
 
 def rms_parts(values):
@@ -694,6 +803,18 @@
         value = value[:half].astype(WIDE) + came
         bit *= 2
     return value
+
+
+def near_scatter_stages(value, axis, ties):
+    size, bit = lax.axis_size(axis), 1
+    while bit < size:
+        half = value.shape[0] // 2
+        value = after(value, *ties)
+        came = exchanged(value[half:].astype(LOW), axis, bit)
+        yield [came]
+        value = value[:half].astype(WIDE) + came.astype(WIDE)
+        bit *= 2
+    yield value
 
 
 def near_blocks(value, axis):
@@ -754,7 +875,7 @@
     if half > 1:
         turned[1] = turn(value, team, 1)
     if half > 2:
-        turned[half - 1] = turn(value, team, -1)
+        turned[half - 1] = turn(after(value, turned[1]), team, -1)
     for k in turns(team):
         across = cross(after(turned[k], *before, *ties), team)
         stage = [across]
@@ -796,6 +917,7 @@
             passing[to] = passing.get(to, []) + [moved]
         yield stage
         before = (came,)
+        keep = keep(came) if callable(keep) else keep
         pair = keep.astype(WIDE) + came.astype(WIDE)
         for moved in passing.pop(k, []):
             pair = pair + moved.astype(WIDE)
@@ -969,17 +1091,36 @@
     def gather_rows(value):
         return lax.all_gather(value, "fsdp", axis=0, tiled=True)
 
-    found = last_of(gather_stages(tokens[0], heads))
+    start_ties = []
+    spread = gather_stages(tokens[0], heads, start_ties)
+    came = next(spread)[:1]
     length = heads * own_rows
 
-    near = found[0][3]
+    def column_blocks(value):
+        return jnp.transpose(value.reshape(shard, fsdp, value.shape[1] // fsdp), (1, 0, 2))
+
     packed = pack_weights(
-        head, after(w_query, near), w_key, w_value, w_outgate, w_beta, w_decay, gain_in,
+        head, after(w_query, came[0]), w_key, w_value, w_outgate, w_beta, w_decay, gain_in,
         gain_ffn, gain_head, conv_query, conv_key, conv_value,
     )
     far_packed = far_exchange(packed, "fsdp")
-    far_packed = after(far_packed, *(rows for _, rows, _, _ in found[1:-1]))
+    start_ties[:] = [packed]
+    came += next(spread)[:1]
+    columns = jnp.stack(
+        [column_blocks(after(w_gate, came[1])), column_blocks(after(w_up, came[1]))], axis=1
+    )
+    others = near_order(fsdp)[1:]
+    column_sends = [lax.dynamic_index_in_dim(columns, member ^ o, 0, False) for o in others]
+    start_ties[:] = [far_packed]
+    came += next(spread)[:1]
+    far_out = far_exchange(after(w_out, far_packed), "fsdp")
     got = ordered_gather(packed, "fsdp", far_packed)
+    start_ties[:] = [got, far_out, *column_sends]
+    for stage in spread:
+        found = stage
+        came += stage[:1]
+    came = [one for one in came if not isinstance(one, tuple)]
+    came += [came[-1]] * 3
     full_packed = got[:, :shard].reshape(width, 896)
     vectors = got[:, shard:, :shard]
     full_gain_in = vectors[:, 0].reshape(width).astype(WIDE)
@@ -1002,22 +1143,12 @@
     def column_blocks(value):
         return jnp.transpose(value.reshape(shard, fsdp, value.shape[1] // fsdp), (1, 0, 2))
 
-    gate_blocks, up_blocks = column_blocks(after(w_gate, near)), column_blocks(after(w_up, near))
-    full_packed, gate_blocks, up_blocks = lax.optimization_barrier(
-        (full_packed, gate_blocks, up_blocks)
-    )
-    filled = None
-    for n, (at, rows, at_other, other) in enumerate(found):
-        places = jnp.stack([at, at_other]).astype(jnp.int32)
-        filled = project(places, rows, other, full_gain_in[None], full_packed, length, filled)
-        if n == 0:
-            w_out, gate_blocks, up_blocks, cot, *filled = lax.optimization_barrier(
-                (w_out, gate_blocks, up_blocks, cotangent[0], *filled)
-            )
-            cols_gate = lax.all_to_all(gate_blocks, "fsdp", 0, 0)
-            cols_up = lax.all_to_all(up_blocks, "fsdp", 0, 0)
-            far_out, far_cot = far_exchange(w_out, "fsdp"), far_exchange(cot, "fsdp")
-    normed_low, pre, gate_small = filled
+    cot = after(cotangent[0], came[2])
+    far_cot = far_exchange(cot, "fsdp")
+    column_got = [
+        exchanged(after(send, came[2]), "fsdp", o) for o, send in zip(others, column_sends)
+    ]
+    normed_low, pre, gate_small = project(found, full_gain_in[None], full_packed)
     offs = jnp.concatenate(
         [offsets, jnp.broadcast_to(team * length, (1, 1)).astype(jnp.int32)], axis=1
     )
@@ -1038,7 +1169,7 @@
     state_in = zero_state
     if teams > 1:
         trial = forward_from(zero_state)
-        steps, end = trial[4], trial[9]
+        steps, end = trial[4].astype(WIDE) + trial[5].astype(WIDE), trial[10]
 
         def along(c, total):
             return jnp.dot(total, steps[c].T, precision=lax.Precision.HIGHEST)
@@ -1047,13 +1178,21 @@
         for _ in range(teams - 1):
             out = jnp.dot(state_in, whole_map, precision=lax.Precision.HIGHEST) + end
             state_in = lax.ppermute(out.astype(LOW), "seq", forth).astype(WIDE)
-    conv, inverse, scores, reach, steps, gated, mixed, upd, states, _ = forward_from(state_in)
-    gated, far_out, cols_gate, cols_up, far_cot = lax.optimization_barrier(
-        (gated, far_out, cols_gate, cols_up, far_cot)
-    )
+    conv, inverse, scores, reach, high, rest, gated, mixed, upd, states, _ = forward_from(state_in)
+    gated, far_out, far_cot, *column_got = lax.optimization_barrier(
+        (gated, far_out, far_cot, *column_got)
+    )
+    own_columns = lax.dynamic_index_in_dim(columns, member, 0, False)
     full_out = ordered_gather(w_out, "fsdp", far_out).reshape(width, width)
     group_cot = near_gather(cot, "fsdp", far_cot)
-    cols_gate, cols_up = (a.reshape(width, a.shape[2]) for a in (cols_gate, cols_up))
+
+    def ordered_columns(which):
+        value = jnp.zeros((width, own_columns.shape[2]), LOW)
+        for o, rows in zip([0, *others], [own_columns, *column_got]):
+            value = lax.dynamic_update_slice(value, rows[which], ((member ^ o) * shard, 0))
+        return value
+
+    cols_gate, cols_up = ordered_columns(0), ordered_columns(1)
 
     gated_own = lax.all_to_all(
         gated, "seq", 0, 1, tiled=True, axis_index_groups=team_groups
@@ -1107,9 +1246,12 @@
             slabs_done = lax.all_gather(turned_columns(summed), "seq", axis=0)
             yield ff_outputs_plain(slabs_done, slab, shard, fsdp)
             return
+        def kept(at):
+            return lambda came: lax.dynamic_index_in_dim(after(slabs, came), at, 0, False)
+
         blocks = [
-            [lax.dynamic_index_in_dim(slabs, p, 0, False) for p in pair]
-            for pair in team_places(heads)
+            (lax.dynamic_index_in_dim(slabs, send, 0, False), kept(keep))
+            for send, keep in team_places(heads)
         ]
         for stage in scatter_stages(blocks, heads, ties):
             if isinstance(stage, list):
@@ -1134,20 +1276,20 @@
         stage = brought[-1]
         return value if isinstance(stage, tuple) else after(value, *stage)
 
-    beside(grad_gated)
     dgated = lax.all_to_all(
         grad_gated, "seq", 1, 0, tiled=True, axis_index_groups=team_groups
     )
-    dgated = settled(dgated)
+    grad_out = dot_left(after(gated_own, grad_gated), res_low, LOW).reshape(fsdp, shard, width)
+    late = near_blocks(grad_out, "fsdp")
+    dgated, late = lax.optimization_barrier((dgated, late))
     beside(dgated)
-    down_part = near_scatter(dot_plain(after(hidden, dgated), w_down), "fsdp")
-    layer_out = (mixer_res + down_part).astype(LOW)
-    grad_out = dot_left(after(gated_own, dgated), res_low, LOW).reshape(fsdp, shard, width)
-    grad_out = near_scatter(near_blocks(grad_out, "fsdp"), "fsdp").astype(LOW)
+    late_ties = []
+    late = near_scatter_stages(late, "fsdp", late_ties)
+    late_stage = []
 
     def gate_back_from(dend):
         return run_gate_back(
-            gate_small, full_gain_head, mixed, reach, steps, dgated, dend
+            gate_small, full_gain_head, mixed, reach, high, rest, dgated, dend
         )
 
     dend = zero_state
@@ -1162,12 +1304,17 @@
     carried = [
         jnp.zeros((4, 8, 640), WIDE), jnp.zeros((8, 640), WIDE), jnp.zeros((1, HEAD), WIDE)
     ]
-    dy, calls = None, 6
-    left = length // (2 * SPAN)
+    dy, calls = None, 2
+    left = length // (PER * SPAN)
     for call in range(calls, 0, -1):
         steps_here = -(-left // call)
-        carried[0] = settled(carried[0] if dy is not None else after(carried[0], do))
+        if dy is None:
+            carried[0] = after(carried[0], do)
+        carried[0] = settled(after(carried[0], *late_stage))
         beside(carried[0])
+        late_ties[:] = [carried[0]]
+        late_stage = next(late)
+        late_stage = late_stage if isinstance(late_stage, list) else [late_stage]
         dy, carried = run_backward(
             left - 1, steps_here, offs, rate, pre, gate_small, edge, head_taps,
             (conv, inverse, upd, scores, states, do, ds, dgate), carried, dy,
@@ -1175,6 +1322,10 @@
         carried = list(carried)
         left -= steps_here
     dy = settled(dy)
+    late_stage = late_stage[0]
+    for stage in late:
+        late_stage = stage
+    grad_out = late_stage.astype(LOW)
     following, dtaps, drate = carried
     if teams > 1:
         none = jnp.zeros((16, 640), WIDE)
@@ -1189,40 +1340,56 @@
         list(input_blocks(places, dy, grad_out, full_packed, own_rows, out_rows))
         for places in team_places(heads)
     ]
-    while not isinstance(brought[-1], tuple):
-        beside(dy)
+    turned_stage = []
+    if not isinstance(brought[-1], tuple):
+        beside(blocks[0][0])
+        turned_stage = brought[-1] if isinstance(brought[-1], list) else []
+    order = jnp.stack([member ^ o for o in near_order(fsdp)]).astype(jnp.int32)
+    combined = weight_grads(
+        order, normed_low, after(dy, blocks[0][0], *turned_stage), full_packed, full_gain_in[None],
+        grad_gain_ffn[None], dgain, drate, dtaps, taps,
+    )
+    blocks = [
+        (send if n == 0 else after(send, combined), keep)
+        for n, (send, keep) in enumerate(blocks)
+    ]
+    near = near_scatter_stages(combined, "fsdp", [])
+    near_stage = next(near)
+    tail_ties = []
+    sent = scatter_stages(blocks, heads, tail_ties)
+    queue = [next(sent)[0]]
+    joined = None
+    while joined is None or not isinstance(brought[-1], tuple):
+        if not isinstance(brought[-1], tuple):
+            beside(queue[-1])
+            if isinstance(brought[-1], list):
+                queue.append(brought[-1][0])
+        if joined is None:
+            tail_ties[:] = [queue[-1]]
+            if len(queue) == 2 and isinstance(near_stage, list):
+                tail_ties += near_stage
+            stage = next(sent)
+            if isinstance(stage, list):
+                queue.append(stage[0])
+            else:
+                joined = stage
+    for near_stage in near:
+        pass
+    combined = after(near_stage.astype(LOW), queue[-1])
     out_gate, out_up, out_down = brought[-1]
-    sent = scatter_stages(blocks, heads)
-    stage = next(sent)
-    grad_packed = dot_left(normed_low, after(dy, blocks[0][0]))
-    stage = next(sent)
-    stage = next(sent)
-    stage = next(sent)
-    ready = (stage[0],)
-    joined = next(sent)
+    down_part = near_scatter(dot_plain(after(hidden, queue[1]), w_down).astype(LOW), "fsdp")
+    layer_out = (mixer_res + down_part).astype(LOW)
     grad_normed, own_out = joined[:own_rows], joined[own_rows:].astype(LOW)
     input_grad = (grad_res + rms_back(grad_normed * full_gain_in, inputs)).astype(LOW)
     if teams > 1:
         own_out = lax.psum(own_out, "seq", axis_index_groups=head_groups)
     found_out = last_of(gather_stages(own_out, heads))
 
-    grad_gain_in = (
-        jnp.sum(grad_packed * full_packed.astype(WIDE), axis=1) / full_gain_in
-    )
-    extra = jnp.zeros((fsdp, 16, 896), WIDE)
-    extra = extra.at[:, 0, :shard].set(grad_gain_in.reshape(fsdp, shard))
-    extra = extra.at[:, 1, :shard].set(grad_gain_ffn.reshape(fsdp, shard))
-    gh = gain_head.shape[0]
-    extra = extra.at[:, 2, :gh].set(dgain.reshape(fsdp, gh))
-    extra = extra.at[:, 3, :HEAD].set(drate)
-    extra = extra.at[:, 4 : 4 + taps, :640].set(dtaps[None, :taps])
-    combined = jnp.concatenate([grad_packed.reshape(fsdp, shard, 896), extra], axis=1)
-    combined = near_scatter(near_blocks(combined.astype(LOW), "fsdp"), "fsdp").astype(LOW)
     if teams > 1:
         combined = lax.psum(combined, "seq", axis_index_groups=head_groups)
     (out_query, out_key, out_value, out_gatew, out_beta, out_decay, out_gain_in, out_gain_ffn,
      out_gain_head, out_rate, out_cq, out_ck, out_cv, out_out) = mixer_outputs(
-        last_of(gather_stages(after(combined, *ready), heads)), found_out, shard, gain_head.shape[0], taps, fsdp, member
+        last_of(gather_stages(combined, heads)), found_out, shard, gain_head.shape[0], taps, fsdp, member
     )
 
     return (

time: 579 us -> 523 us (0.903); the launches traced: 569 us -> 519 us
  Pallas kernels: 202 us -> 130 us
  waiting for transfers between devices: 150 us -> 189 us
  matrix products: 33.1 us -> 22 us
    pallas_call x1, Pallas kernels: 76.2 us -> 31.6 us  [run_forward(): pl.pallas_call(functools.partial(forward_kernel, spans, offs.shape[1] - 1...]
    pallas_call x6 -> x2, Pallas kernels: 57.6 us -> 29 us  [run_backward(): pl.pallas_call(functools.partial(backward_kernel, at, offs.shape[1] - 1),...]
    ppermute x42, waiting for transfers between devices: 120 us -> 137 us  [team_step(): return lax.ppermute(value, 'seq', pairs)]
    all_to_all x1, waiting for transfers between devices: 1.91 us -> 17.8 us  [per_device(): lax.all_to_all(grad_gated, 'seq', 1, 0, tiled=True, axis_index_groups=tea...]
    all_to_all x1, starting transfers between devices: 6.06 us -> 18.4 us  [per_device(): lax.all_to_all(gated, 'seq', 0, 1, tiled=True, axis_index_groups=team_gro...]
    dot_general x9 -> x8, matrix products: 25.2 us -> 14.2 us  [contract(): lax.dot_general(left, right, (((left_dim,), (right_dim,)), ((), ())), pre...]
    all_to_all x2 -> x0, starting transfers between devices: 8.01 us -> none  [the longest x1 4.46 us: per_device(): cols_gate = lax.all_to_all(gate_blocks, 'fsdp', 0, 0)]
    ppermute x16 -> x19, starting transfers between devices: 12.8 us -> 9.4 us  [exchanged(): return lax.ppermute(value, axis, [(i, i ^ bit) for i in range(size)])]
  transfers between devices with their start and end apart: 63 -> 64, of which waited for: 29 -> 25; matrix products, arithmetic and copies ran while one was open for 16% -> 16% of each run, Pallas kernels for 34% -> 23%
where the time goes in v4:
time: 523 us; the launch traced here: 519 us
  waiting for transfers between devices  189 us (36%)
  Pallas kernels  130 us (25%)
  starting transfers between devices  81.4 us (16%)
  other arithmetic  50.1 us (10%)
  local copies, waits for them, and re-layouts  45 us (9%)
  matrix products  22 us (4%)
    ppermute x42, waiting for transfers between devices, team_step(): return lax.ppermute(value, 'seq', pairs)  137 us
    ppermute x42, starting transfers between devices, team_step(): return lax.ppermute(value, 'seq', pairs)  45.3 us
    pallas_call x1, Pallas kernels, run_forward(): pl.pallas_call(functools.partial(forward_kernel, spans, offs.shape[1] - 1...  31.6 us
    pallas_call x2, Pallas kernels, run_backward(): pl.pallas_call(functools.partial(backward_kernel, at, offs.shape[1] - 1),...  29 us
    ppermute x19, waiting for transfers between devices, exchanged(): return lax.ppermute(value, axis, [(i, i ^ bit) for i in range(size)])  20.5 us
    pallas_call x4, Pallas kernels, input_blocks(): pl.pallas_call(input_blocks_kernel, out_shape=[jax.ShapeDtypeStruct((coun...  20.3 us
    all_to_all x1, starting transfers between devices, per_device(): lax.all_to_all(gated, 'seq', 0, 1, tiled=True, axis_index_groups=team_gro...  18.4 us
    all_to_all x1, waiting for transfers between devices, per_device(): lax.all_to_all(grad_gated, 'seq', 1, 0, tiled=True, axis_index_groups=tea...  17.8 us
  transfers between devices with their start and end apart: 64, of which 25 were waited for; matrix products, arithmetic and copies ran while one was open for 16% of the time, Pallas kernels for 23%

profile of v4, /device:TPU:0, one launch (start us, length us, event | category | flops | bytes accessed | tf_op | source)
XLA Modules:
  0.0 519.1 jit_solution(11012824728100637790)
XLA Ops:
  0.7 3.0 collective-permute-start
  8.9 6.9 %collective-permute-done.refs_1_ = bf16[256,1024]{1,0:T(8,128)(2,1)S(1)} collective-permute-done((bf16[256,1024]{1,0:T(8,128)(2,1)}, bf16[256,1024]{1,0:T(8,128)(2,1)S(1)}, u32[]{:S(2)}, u32[]{:S(2)}) %collective-permute-start) | collective-permute-done | bytes 524320 | tf_op jit(solution)/shard_map/ppermute | solution.py:855
  22.0 3.6 collective-permute-start.5
  25.6 6.4 %collective-permute-done.1 = bf16[288,896]{1,0:T(8,128)(2,1)S(1)} collective-permute-done((bf16[288,896]{1,0:T(8,128)(2,1)}, bf16[288,896]{1,0:T(8,128)(2,1)S(1)}, u32[]{:S(2)}, u32[]{:S(2)}) %collective-permute-start.1) | collective-permute-done | bytes 516128 | tf_op jit(solution)/shard_map/ppermute | solution.py:778
  32.0 2.4 maximum_select_fusion.5
  44.3 2.5 copy.51
  46.9 3.0 fusion.19
  64.6 6.7 %collective-permute-done.9.refs_7_ = bf16[256,1024]{1,0:T(8,128)(2,1)} collective-permute-done((bf16[256,1024]{1,0:T(8,128)(2,1)}, bf16[256,1024]{1,0:T(8,128)(2,1)}, u32[]{:S(2)}, u32[]{:S(2)}) %collective-permute-start.9) | collective-permute-done | bytes 524320 | tf_op jit(solution)/shard_map/ppermute | solution.py:855
  71.3 12.3 %project.1 = (bf16[2048,1024]{1,0:T(8,128)(2,1)}, bf16[2048,640]{1,0:T(8,128)(2,1)}, f32[2048,256]{1,0:T(8,128)}) custom-call(s32[8]{0:T(128)} %stack.168.place_ref, f32[1,1024]{1,0:T(1,128)} %bitcast.209, bf16[1024,896]{1,0:T(8,128)(2,1)} %bitcast.173, bf16[256,1024]{1,0:T(8,128)(2,1)} %bitcast.184, bf16[256,1024]{1,0:T(8,128)(2,1)} %copy-done.53, ...), custom_call_target="tpu_custom_call" | custom-call | flops 3758096384 | bytes 13631488 | tf_op jit(solution)/shard_map/project/pallas_call | solution.py:733
  84.8 31.6 %delta_forward.1 = (f32[2048,640]{1,0:T(8,128)}, bf16[32,128,128]{2,1,0:T(8,128)(2,1)}, bf16[32,64,128]{2,1,0:T(8,128)(2,1)}, bf16[32,64,128]{2,1,0:T(8,128)(2,1...) custom-call(s32[1,17]{1,0:T(1,128)} %pad_add_fusion.offs_ref, ...), custom_call_target="tpu_custom_call" | custom-call | flops 70000001024 | bytes 25165824 | tf_op jit(solution)/shard_map/delta_forward/pallas_call | solution.py:435
  116.5 2.7 maximum_select_fusion.3
  120.2 18.4 %all-to-all-start = ((bf16[8,256,128]{1,2,0:T(8,128)(2,1)}), bf16[8,256,128]{1,2,0:T(8,128)(2,1)S(1)}, u32[]{:S(2)}, u32[]{:S(2)}) async-start(bf16[8,256,128]{1,2,0:T(8,128)(2,1)} %copy.52), calls=%async_computation | async-start | bytes 1048576 | tf_op jit(solution)/shard_map/all_to_all | solution.py:1197
  142.0 11.8 %all-to-all-done = bf16[8,256,128]{1,2,0:T(8,128)(2,1)S(1)} async-done(((bf16[8,256,128]{1,2,0:T(8,128)(2,1)}), bf16[8,256,128]{1,2,0:T(8,128)(2,1)S(1)}, u32[]{:S(2)}, u32[]{:S(2)}) %all-to-all-start) | async-done | bytes 524320 | tf_op jit(solution)/shard_map/all_to_all | solution.py:1197
  153.8 2.6 multiply_reduce_fusion.2
  159.2 10.5 %collective-permute-done.15 = bf16[256,1024]{1,0:T(8,128)(2,1)S(1)} collective-permute-done((bf16[256,1024]{1,0:T(8,128)(2,1)S(1)}, bf16[256,1024]{1,0:T(8,128)(2,1)S(1)}, u32[]{:S(2)}, u32[]{:S(2)}) %collective-permute-start.15) | collective-permute-done | bytes 524320 | tf_op jit(solution)/shard_map/ppermute | solution.py:778
  179.1 2.9 multiply_convert_fusion
  200.1 9.0 %collective-permute-done.18 = bf16[264,1024]{1,0:T(8,128)(2,1)S(1)} collective-permute-done((bf16[264,1024]{1,0:T(8,128)(2,1)}, bf16[264,1024]{1,0:T(8,128)(2,1)S(1)}, u32[]{:S(2)}, u32[]{:S(2)}) %collective-permute-start.18) | collective-permute-done | bytes 540704 | tf_op jit(solution)/shard_map/ppermute | solution.py:855
  209.1 3.6 collective-permute-done.20
  212.8 2.4 multiply_reduce_fusion
  218.8 4.2 all-to-all-start.1
  223.0 2.3 fusion.9
  230.6 17.8 %all-to-all-done.1 = bf16[256,8,128]{2,0,1:T(8,128)(2,1)} async-done(((bf16[256,8,128]{2,0,1:T(8,128)(2,1)}), bf16[256,8,128]{2,0,1:T(8,128)(2,1)}, u32[]{:S(2)}, u32[]{:S(2)}) %all-to-all-start.1) | async-done | bytes 524320 | tf_op jit(solution)/shard_map/all_to_all | solution.py:1279
  249.8 11.8 %delta_gate_back.1 = (bf16[32,64,128]{2,1,0:T(8,128)(2,1)}, f32[32,128,128]{2,1,0:T(8,128)}, bf16[2048,128]{1,0:T(8,128)(2,1)}, f32[1,128]{1,0:T(1,128)}, f32[128,128]{1,0:T(8,128)}) custom-call(f32[2048,256]{1,0:T(8,128)} %get-tuple-element.138.small_ref.gate_ref, f32[1,128]{1,0:T(1,128)} %reshape.340.gain_ref, f32[2048,128]{1,0:T(8,128)} %get-tuple-element.156.mixed_ref, ...), custom_call_target="tpu_custom_call" | custom-call | flops 15000000512 | bytes 8388608 | tf_op jit(solution)/shard_map/delta_gate_back/pallas_call | solution.py:471
  266.1 14.5 %delta_backward.2 = (bf16[2048,896]{1,0:T(8,128)(2,1)}, f32[4,8,640]{2,1,0:T(8,128)}, f32[8,640]{1,0:T(8,128)}, f32[1,128]{1,0:T(1,128)}) custom-call(s32[1,17]{1,0:T(1,128)} %pad_add_fusion.offs_ref, f32[1,1]{1,0:T(1,128)} %bitcast.2.rate_ref, bf16[2048,640]{1,0:T(8,128)(2,1)} %get-tuple-element.137.pre_ref.prior_ref, ...), custom_call_target="tpu_custom_call" | custom-call | flops 16000000000 | bytes 10905190 | tf_op jit(solution)/shard_map/delta_backward/pallas_call | solution.py:545
  280.6 2.5 fusion.4
  289.2 14.5 %delta_backward.3 = (bf16[2048,896]{1,0:T(8,128)(2,1)}, f32[4,8,640]{2,1,0:T(8,128)}, f32[8,640]{1,0:T(8,128)}, f32[1,128]{1,0:T(1,128)}) custom-call(s32[1,17]{1,0:T(1,128)} %pad_add_fusion.offs_ref, f32[1,1]{1,0:T(1,128)} %bitcast.2.rate_ref, bf16[2048,640]{1,0:T(8,128)(2,1)} %get-tuple-element.137.pre_ref.prior_ref, ...), custom_call_target="tpu_custom_call", output_to_operand_aliasing={{0}: (18, {})} | custom-call | flops 16000000000 | bytes 10905190 | tf_op jit(solution)/shard_map/delta_backward/pallas_call | solution.py:545
  304.7 5.0 input_blocks.4
  313.0 4.1 all-to-all-start.2
  326.3 10.1 %weight_grads.1 = bf16[1088,896]{1,0:T(8,128)(2,1)} custom-call(s32[4]{0:T(128)} %pad_add_fusion.3.at_ref, bf16[2048,1024]{1,0:T(8,128)(2,1)} %get-tuple-element.193.low_ref, bf16[2048,896]{1,0:T(8,128)(2,1)} %get-tuple-element.194.dy_ref, bf16[1024,896]{1,0:T(8,128)(2,1)} %bitcast.175, f32[1,1024]{1,0:T(1,128)} %bitcast.210, f32[1,1024]{1,0:T(1,128)} %bitcast.216, ...), custom_call_target="tpu_custom_call" | custom-call | flops 3758096384 | bytes 12582912 | tf_op jit(solution)/shard_map/weight_grads/pallas_call | solution.py:625
  339.4 5.0 input_blocks.7
  344.4 8.0 %collective-permute-done.30.refs_1_ = bf16[264,1024]{1,0:T(8,128)(2,1)S(1)} collective-permute-done((bf16[264,1024]{1,0:T(8,128)(2,1)S(1)}, bf16[264,1024]{1,0:T(8,128)(2,1)S(1)}, u32[]{:S(2)}, u32[]{:S(2)}) %collective-permute-start.30) | collective-permute-done | bytes 540704 | tf_op jit(solution)/shard_map/ppermute | solution.py:855
  354.6 15.2 %collective-permute-done.35.refs_2_ = bf16[264,1024]{1,0:T(8,128)(2,1)} collective-permute-done((bf16[264,1024]{1,0:T(8,128)(2,1)S(1)}, bf16[264,1024]{1,0:T(8,128)(2,1)}, u32[]{:S(2)}, u32[]{:S(2)}) %collective-permute-start.35) | collective-permute-done | bytes 540704 | tf_op jit(solution)/shard_map/ppermute | solution.py:855
  371.3 5.2 input_blocks.6
  376.5 6.2 %collective-permute-done.36.refs_3_ = bf16[264,1024]{1,0:T(8,128)(2,1)} collective-permute-done((bf16[264,1024]{1,0:T(8,128)(2,1)}, bf16[264,1024]{1,0:T(8,128)(2,1)}, u32[]{:S(2)}, u32[]{:S(2)}) %collective-permute-start.36) | collective-permute-done | bytes 540704 | tf_op jit(solution)/shard_map/ppermute | solution.py:855
  384.6 10.5 %collective-permute-done.38.refs_4_ = bf16[264,1024]{1,0:T(8,128)(2,1)S(1)} collective-permute-done((bf16[264,1024]{1,0:T(8,128)(2,1)S(1)}, bf16[264,1024]{1,0:T(8,128)(2,1)S(1)}, u32[]{:S(2)}, u32[]{:S(2)}) %collective-permute-start.38) | collective-permute-done | bytes 540704 | tf_op jit(solution)/shard_map/ppermute | solution.py:855
  398.0 5.1 input_blocks.5
  403.6 5.3 %collective-permute-done.39.refs_5_ = bf16[264,1024]{1,0:T(8,128)(2,1)} collective-permute-done((bf16[264,1024]{1,0:T(8,128)(2,1)S(1)}, bf16[264,1024]{1,0:T(8,128)(2,1)}, u32[]{:S(2)}, u32[]{:S(2)}) %collective-permute-start.39) | collective-permute-done | bytes 540704 | tf_op jit(solution)/shard_map/ppermute | solution.py:855
  415.0 7.3 %collective-permute-done.40 = bf16[288,1024]{1,0:T(8,128)(2,1)S(1)} collective-permute-done((bf16[288,1024]{1,0:T(8,128)(2,1)S(1)}, bf16[288,1024]{1,0:T(8,128)(2,1)S(1)}, u32[]{:S(2)}, u32[]{:S(2)}) %collective-permute-start.40) | collective-permute-done | bytes 589856 | tf_op jit(solution)/shard_map/ppermute | solution.py:855
  425.8 8.9 %collective-permute-done.46.refs_7_ = bf16[264,1024]{1,0:T(8,128)(2,1)S(1)} collective-permute-done((bf16[264,1024]{1,0:T(8,128)(2,1)S(1)}, bf16[264,1024]{1,0:T(8,128)(2,1)S(1)}, u32[]{:S(2)}, u32[]{:S(2)}) %collective-permute-start.46) | collective-permute-done | bytes 540704 | tf_op jit(solution)/shard_map/ppermute | solution.py:855
  439.8 16.0 %collective-permute-done.48.refs_2_ = bf16[272,896]{1,0:T(8,128)(2,1)} collective-permute-done((bf16[272,896]{1,0:T(8,128)(2,1)}, bf16[272,896]{1,0:T(8,128)(2,1)}, u32[]{:S(2)}, u32[]{:S(2)}) %collective-permute-start.48) | collective-permute-done | bytes 487456 | tf_op jit(solution)/shard_map/ppermute | solution.py:855
  456.8 11.6 %collective-permute-done.43 = bf16[288,1024]{1,0:T(8,128)(2,1)} collective-permute-done((bf16[288,1024]{1,0:T(8,128)(2,1)}, bf16[288,1024]{1,0:T(8,128)(2,1)}, u32[]{:S(2)}, u32[]{:S(2)}) %collective-permute-start.43) | collective-permute-done | bytes 589856 | tf_op jit(solution)/shard_map/ppermute | solution.py:855
  471.3 7.4 %collective-permute-done.50.refs_4_ = bf16[272,896]{1,0:T(8,128)(2,1)S(1)} collective-permute-done((bf16[272,896]{1,0:T(8,128)(2,1)}, bf16[272,896]{1,0:T(8,128)(2,1)S(1)}, u32[]{:S(2)}, u32[]{:S(2)}) %collective-permute-start.50) | collective-permute-done | bytes 487456 | tf_op jit(solution)/shard_map/ppermute | solution.py:855
  481.2 3.4 collective-permute-start.57
  486.0 9.8 %collective-permute-done.57.refs_12_ = bf16[32,1024]{1,0:T(8,128)(2,1)S(1)} collective-permute-done((bf16[32,1024]{1,0:T(8,128)(2,1)S(1)}, bf16[32,1024]{1,0:T(8,128)(2,1)S(1)}, u32[]{:S(2)}, u32[]{:S(2)}) %collective-permute-start.57) | collective-permute-done | bytes 65568 | tf_op jit(solution)/shard_map/ppermute | solution.py:855
  498.0 2.8 collective-permute-done.58.refs_13_
  503.0 6.5 %ff_outputs.1 = (f32[256,2816]{1,0:T(8,128)}, f32[256,2816]{1,0:T(8,128)}, f32[704,1024]{1,0:T(8,128)}) custom-call(s32[8]{0:T(128)} %stack.168.place_ref, bf16[264,1024]{1,0:T(8,128)(2,1)} %copy-done.14, bf16[264,1024]{1,0:T(8,128)(2,1)} %copy-done.28, bf16[264,1024]{1,0:T(8,128)(2,1)} %collective-permute-done.35.refs_2_, ...), custom_call_target="tpu_custom_call" | custom-call | bytes 15728640 | tf_op jit(solution)/shard_map/ff_outputs/pallas_call | solution.py:1033
  509.6 2.2 collective-permute-done.60.refs_15_
  512.6 6.3 %mixer_outputs.1 = (f32[256,1024]{1,0:T(8,128)}, f32[256,2048]{1,0:T(8,128)}, f32[256,2048]{1,0:T(8,128)}, f32[256,1024]{1,0:T(8,128)}, f32[16,256]{1,0:T(8,128)...) custom-call(s32[1,9]{1,0:T(1,128)} %bitcast.217, ...), custom_call_target="tpu_custom_call" | custom-call | bytes 12582912 | tf_op jit(solution)/shard_map/mixer_outputs/pallas_call | solution.py:1000
  (327 shorter events, 145.4 us)
Async XLA Ops:
  0.7 15.1 %collective-permute-start = (bf16[256,1024]{1,0:T(8,128)(2,1)}, bf16[256,1024]{1,0:T(8,128)(2,1)S(1)}, u32[]{:S(2)}, u32[]{:S(2)}) collective-permute-start(bf16[256,1024]{1,0:T(8,128)(2,1)} %bitcast.182), channel_id=1, source_target_pairs={{0,4},{4,0},{8,12},{12,8},{16,20},{20,16},{24,28},{28,24},{1,5},{5... | collective-permute-start | bytes 1572872 | tf_op jit(solution)/shard_map/ppermute | solution.py:855
  3.7 16.8 %collective-permute-start.3 = (bf16[256,1024]{1,0:T(8,128)(2,1)}, bf16[256,1024]{1,0:T(8,128)(2,1)}, u32[]{:S(2)}, u32[]{:S(2)}) collective-permute-start(bf16[256,1024]{1,0:T(8,128)(2,1)} %bitcast.183), channel_id=1, source_target_pairs={{0,8},{4,12},{8,16},{12,20},{16,24},{20,28},{24,0},{28,4},{1,9},{5... | collective-permute-start | bytes 1572872 | tf_op jit(solution)/shard_map/ppermute | solution.py:855
  20.5 13.9 %collective-permute-start.4 = (bf16[256,1024]{1,0:T(8,128)(2,1)}, bf16[256,1024]{1,0:T(8,128)(2,1)S(1)}, u32[]{:S(2)}, u32[]{:S(2)}) collective-permute-start(bf16[256,1024]{1,0:T(8,128)(2,1)} %collective-permute-done.3.refs_2_), channel_id=1, source_target_pairs={{0,4},{4,0},{8,12},{12,8},{16,20},{20,16},{24,28},{28,24},{1,5},{5... | collective-permute-start | bytes 1572872 | tf_op jit(solution)/shard_map/ppermute | solution.py:855
  22.0 13.5 %collective-permute-start.5 = (bf16[256,1024]{1,0:T(8,128)(2,1)S(1)}, bf16[256,1024]{1,0:T(8,128)(2,1)S(1)}, u32[]{:S(2)}, u32[]{:S(2)}) collective-permute-start(bf16[256,1024]{1,0:T(8,128)(2,1)S(1)} %bitcast.185), channel_id=1, source_target_pairs={{0,24},{4,28},{8,0},{12,4},{16,8},{20,12},{24,16},{28,20},{1,25},{... | collective-permute-start | bytes 1572872 | tf_op jit(solution)/shard_map/ppermute | solution.py:855
  34.4 16.7 %collective-permute-start.2 = (bf16[2,288,896]{2,1,0:T(8,128)(2,1)}, bf16[2,288,896]{2,1,0:T(8,128)(2,1)}, u32[]{:S(2)}, u32[]{:S(2)}) collective-permute-start(bf16[2,288,896]{2,1,0:T(8,128)(2,1)} %maximum_select_fusion.5), channel_id=1, source_target_pairs={{0,1},{1,0},{2,3},{3,2},{4,5},{5,4},{6,7},{7,6},{8,9},{9,8},{10,11... | collective-permute-start | bytes 3096584 | tf_op jit(solution)/shard_map/ppermute | solution.py:778
  35.4 14.5 %collective-permute-start.6 = (bf16[256,1024]{1,0:T(8,128)(2,1)S(1)}, bf16[256,1024]{1,0:T(8,128)(2,1)}, u32[]{:S(2)}, u32[]{:S(2)}) collective-permute-start(bf16[256,1024]{1,0:T(8,128)(2,1)S(1)} %collective-permute-done.5.refs_4_), channel_id=1, source_target_pairs={{0,4},{4,0},{8,12},{12,8},{16,20},{20,16},{24,28},{28,24},{1,5},{5... | collective-permute-start | bytes 1572872 | tf_op jit(solution)/shard_map/ppermute | solution.py:855
  38.3 17.8 %collective-permute-start.7 = (bf16[256,1024]{1,0:T(8,128)(2,1)}, bf16[256,1024]{1,0:T(8,128)(2,1)}, u32[]{:S(2)}, u32[]{:S(2)}) collective-permute-start(bf16[256,1024]{1,0:T(8,128)(2,1)} %collective-permute-done.3.refs_2_), channel_id=1, source_target_pairs={{0,8},{4,12},{8,16},{12,20},{16,24},{20,28},{24,0},{28,4},{1,9},{5... | collective-permute-start | bytes 1572872 | tf_op jit(solution)/shard_map/ppermute | solution.py:855
  39.9 17.5 %collective-permute-start.8 = (bf16[256,1024]{1,0:T(8,128)(2,1)}, bf16[256,1024]{1,0:T(8,128)(2,1)}, u32[]{:S(2)}, u32[]{:S(2)}) collective-permute-start(bf16[256,1024]{1,0:T(8,128)(2,1)} %param.35), channel_id=1, source_target_pairs={{0,2},{1,3},{2,0},{3,1},{4,6},{5,7},{6,4},{7,5},{8,10},{9,11},{10,... | collective-permute-start | bytes 1572872 | tf_op jit(solution)/shard_map/ppermute | solution.py:778
  49.9 66.6 %collective-permute-start.11 = (bf16[2,256,704]{1,2,0:T(8,128)(2,1)}, bf16[2,256,704]{1,2,0:T(8,128)(2,1)}, u32[]{:S(2)}, u32[]{:S(2)}) collective-permute-start(bf16[2,256,704]{1,2,0:T(8,128)(2,1)} %get-tuple-element.141), channel_id=1, source_target_pairs={{0,2},{1,3},{2,0},{3,1},{4,6},{5,7},{6,4},{7,5},{8,10},{9,11},{10,... | collective-permute-start | bytes 2162696 | tf_op jit(solution)/shard_map/ppermute | solution.py:778
  51.0 65.4 %collective-permute-start.12 = (bf16[2,256,704]{1,2,0:T(8,128)(2,1)}, bf16[2,256,704]{1,2,0:T(8,128)(2,1)}, u32[]{:S(2)}, u32[]{:S(2)}) collective-permute-start(bf16[2,256,704]{1,2,0:T(8,128)(2,1)} %get-tuple-element.142), channel_id=1, source_target_pairs={{0,1},{1,0},{2,3},{3,2},{4,5},{5,4},{6,7},{7,6},{8,9},{9,8},{10,11... | collective-permute-start | bytes 2162696 | tf_op jit(solution)/shard_map/ppermute | solution.py:778
  51.1 65.4 %collective-permute-start.13 = (bf16[2,256,704]{1,2,0:T(8,128)(2,1)}, bf16[2,256,704]{1,2,0:T(8,128)(2,1)}, u32[]{:S(2)}, u32[]{:S(2)}) collective-permute-start(bf16[2,256,704]{1,2,0:T(8,128)(2,1)} %get-tuple-element.143), channel_id=1, source_target_pairs={{0,3},{1,2},{2,1},{3,0},{4,7},{5,6},{6,5},{7,4},{8,11},{9,10},{10,... | collective-permute-start | bytes 2162696 | tf_op jit(solution)/shard_map/ppermute | solution.py:778
  56.2 60.3 %collective-permute-start.10 = (bf16[256,1024]{1,0:T(8,128)(2,1)}, bf16[256,1024]{1,0:T(8,128)(2,1)}, u32[]{:S(2)}, u32[]{:S(2)}) collective-permute-start(bf16[256,1024]{1,0:T(8,128)(2,1)} %bitcast.36), channel_id=1, source_target_pairs={{0,2},{1,3},{2,0},{3,1},{4,6},{5,7},{6,4},{7,5},{8,10},{9,11},{10,... | collective-permute-start | bytes 1572872 | tf_op jit(solution)/shard_map/ppermute | solution.py:778
  57.4 13.9 %collective-permute-start.9 = (bf16[256,1024]{1,0:T(8,128)(2,1)}, bf16[256,1024]{1,0:T(8,128)(2,1)}, u32[]{:S(2)}, u32[]{:S(2)}) collective-permute-start(bf16[256,1024]{1,0:T(8,128)(2,1)} %collective-permute-done.7.refs_6_), channel_id=1, source_target_pairs={{0,4},{4,0},{8,12},{12,8},{16,20},{20,16},{24,28},{28,24},{1,5},{5... | collective-permute-start | bytes 1572872 | tf_op jit(solution)/shard_map/ppermute | solution.py:855
  119.2 21.1 %collective-permute-start.14 = (bf16[2,256,1024]{2,1,0:T(8,128)(2,1)}, bf16[2,256,1024]{2,1,0:T(8,128)(2,1)S(1)}, u32[]{:S(2)}, u32[]{:S(2)}) collective-permute-start(bf16[2,256,1024]{2,1,0:T(8,128)(2,1)} %maximum_select_fusion.3), channel_id=1, source_target_pairs={{0,1},{1,0},{2,3},{3,2},{4,5},{5,4},{6,7},{7,6},{8,9},{9,8},{10,11... | collective-permute-start | bytes 3145736 | tf_op jit(solution)/shard_map/ppermute | solution.py:778
  120.2 33.6 %all-to-all-start = ((bf16[8,256,128]{1,2,0:T(8,128)(2,1)}), bf16[8,256,128]{1,2,0:T(8,128)(2,1)S(1)}, u32[]{:S(2)}, u32[]{:S(2)}) async-start(bf16[8,256,128]{1,2,0:T(8,128)(2,1)} %copy.52), calls=%async_computation | async-start | bytes 1048576 | tf_op jit(solution)/shard_map/all_to_all | solution.py:1197
  159.1 16.4 %collective-permute-start.17 = (bf16[512,1024]{1,0:T(8,128)(2,1)S(1)}, bf16[512,1024]{1,0:T(8,128)(2,1)S(1)}, u32[]{:S(2)}, u32[]{:S(2)}) collective-permute-start(bf16[512,1024]{1,0:T(8,128)(2,1)S(1)} %pad_maximum_fusion.4), channel_id=1, source_target_pairs={{0,1},{1,0},{2,3},{3,2},{4,5},{5,4},{6,7},{7,6},{8,9},{9,8},{10,11... | collective-permute-start | bytes 3145736 | tf_op jit(solution)/shard_map/ppermute | solution.py:778
  194.7 14.4 %collective-permute-start.18 = (bf16[264,1024]{1,0:T(8,128)(2,1)}, bf16[264,1024]{1,0:T(8,128)(2,1)S(1)}, u32[]{:S(2)}, u32[]{:S(2)}) collective-permute-start(bf16[264,1024]{1,0:T(8,128)(2,1)} %get-tuple-element.245), channel_id=1, source_target_pairs={{0,4},{4,0},{8,12},{12,8},{16,20},{20,16},{24,28},{28,24},{1,5},{5... | collective-permute-start | bytes 1622024 | tf_op jit(solution)/shard_map/ppermute | solution.py:855
  199.0 13.8 %collective-permute-start.20 = (bf16[256,1024]{1,0:T(8,128)(2,1)}, bf16[256,1024]{1,0:T(8,128)(2,1)S(1)}, u32[]{:S(2)}, u32[]{:S(2)}) collective-permute-start(bf16[256,1024]{1,0:T(8,128)(2,1)} %slice.224), channel_id=1, source_target_pairs={{0,2},{1,3},{2,0},{3,1},{4,6},{5,7},{6,4},{7,5},{8,10},{9,11},{10,... | collective-permute-start | bytes 1572872 | tf_op jit(solution)/shard_map/ppermute | solution.py:778
  218.8 29.6 %all-to-all-start.1 = ((bf16[256,8,128]{2,0,1:T(8,128)(2,1)}), bf16[256,8,128]{2,0,1:T(8,128)(2,1)}, u32[]{:S(2)}, u32[]{:S(2)}) async-start(bf16[256,8,128]{2,0,1:T(8,128)(2,1)} %copy_bitcast_fusion), calls=%async_computation.1 | async-start | bytes 1048576 | tf_op jit(solution)/shard_map/all_to_all | solution.py:1279
  225.2 36.3 %collective-permute-start.22 = (bf16[264,1024]{1,0:T(8,128)(2,1)}, bf16[264,1024]{1,0:T(8,128)(2,1)}, u32[]{:S(2)}, u32[]{:S(2)}) collective-permute-start(bf16[264,1024]{1,0:T(8,128)(2,1)} %fusion.9), channel_id=1, source_target_pairs={{0,8},{4,12},{8,16},{12,20},{16,24},{20,28},{24,0},{28,4},{1,9},{5... | collective-permute-start | bytes 1622024 | tf_op jit(solution)/shard_map/ppermute | solution.py:855
  261.7 23.3 %collective-permute-start.24 = (bf16[512,1024]{1,0:T(8,128)(2,1)S(1)}, bf16[512,1024]{1,0:T(8,128)(2,1)S(1)}, u32[]{:S(2)}, u32[]{:S(2)}) collective-permute-start(bf16[512,1024]{1,0:T(8,128)(2,1)S(1)} %slice.130), channel_id=1, source_target_pairs={{0,1},{1,0},{2,3},{3,2},{4,5},{5,4},{6,7},{7,6},{8,9},{9,8},{10,11... | collective-permute-start | bytes 3145736 | tf_op jit(solution)/shard_map/ppermute | solution.py:778
  263.2 22.8 %collective-permute-start.25 = (bf16[264,1024]{1,0:T(8,128)(2,1)S(1)}, bf16[264,1024]{1,0:T(8,128)(2,1)}, u32[]{:S(2)}, u32[]{:S(2)}) collective-permute-start(bf16[264,1024]{1,0:T(8,128)(2,1)S(1)} %fusion.8), channel_id=1, source_target_pairs={{0,24},{4,28},{8,0},{12,4},{16,8},{20,12},{24,16},{28,20},{1,25},{... | collective-permute-start | bytes 1622024 | tf_op jit(solution)/shard_map/ppermute | solution.py:855
  263.2 17.3 %collective-permute-start.23 = (bf16[264,1024]{1,0:T(8,128)(2,1)}, bf16[264,1024]{1,0:T(8,128)(2,1)}, u32[]{:S(2)}, u32[]{:S(2)}) collective-permute-start(bf16[264,1024]{1,0:T(8,128)(2,1)} %get-tuple-element.164), channel_id=1, source_target_pairs={{0,4},{4,0},{8,12},{12,8},{16,20},{20,16},{24,28},{28,24},{1,5},{5... | collective-permute-start | bytes 1622024 | tf_op jit(solution)/shard_map/ppermute | solution.py:855
  283.0 21.7 %collective-permute-start.27 = (bf16[264,1024]{1,0:T(8,128)(2,1)}, bf16[264,1024]{1,0:T(8,128)(2,1)}, u32[]{:S(2)}, u32[]{:S(2)}) collective-permute-start(bf16[264,1024]{1,0:T(8,128)(2,1)} %fusion.4), channel_id=1, source_target_pairs={{0,8},{4,12},{8,16},{12,20},{16,24},{20,28},{24,0},{28,4},{1,9},{5... | collective-permute-start | bytes 1622024 | tf_op jit(solution)/shard_map/ppermute | solution.py:855
  287.7 16.1 %collective-permute-start.28 = (bf16[256,1024]{1,0:T(8,128)(2,1)S(1)}, bf16[256,1024]{1,0:T(8,128)(2,1)S(1)}, u32[]{:S(2)}, u32[]{:S(2)}) collective-permute-start(bf16[256,1024]{1,0:T(8,128)(2,1)S(1)} %slice.223), channel_id=1, source_target_pairs={{0,2},{1,3},{2,0},{3,1},{4,6},{5,7},{6,4},{7,5},{8,10},{9,11},{10,... | collective-permute-start | bytes 1572872 | tf_op jit(solution)/shard_map/ppermute | solution.py:778
  288.2 16.4 %collective-permute-start.26 = (bf16[264,1024]{1,0:T(8,128)(2,1)}, bf16[264,1024]{1,0:T(8,128)(2,1)S(1)}, u32[]{:S(2)}, u32[]{:S(2)}) collective-permute-start(bf16[264,1024]{1,0:T(8,128)(2,1)} %get-tuple-element.178), channel_id=1, source_target_pairs={{0,4},{4,0},{8,12},{12,8},{16,20},{20,16},{24,28},{28,24},{1,5},{5... | collective-permute-start | bytes 1622024 | tf_op jit(solution)/shard_map/ppermute | solution.py:855
  321.2 16.6 %collective-permute-start.29 = (bf16[288,1024]{1,0:T(8,128)(2,1)}, bf16[288,1024]{1,0:T(8,128)(2,1)}, u32[]{:S(2)}, u32[]{:S(2)}) collective-permute-start(bf16[288,1024]{1,0:T(8,128)(2,1)} %get-tuple-element.187), channel_id=1, source_target_pairs={{0,4},{4,0},{8,12},{12,8},{16,20},{20,16},{24,28},{28,24},{1,5},{5... | collective-permute-start | bytes 1769480 | tf_op jit(solution)/shard_map/ppermute | solution.py:855
  337.7 15.6 %collective-permute-start.33 = (bf16[544,896]{1,0:T(8,128)(2,1)S(1)}, bf16[544,896]{1,0:T(8,128)(2,1)S(1)}, u32[]{:S(2)}, u32[]{:S(2)}) collective-permute-start(bf16[544,896]{1,0:T(8,128)(2,1)S(1)} %slice.162), channel_id=1, source_target_pairs={{0,1},{1,0},{2,3},{3,2},{4,5},{5,4},{6,7},{7,6},{8,9},{9,8},{10,11... | collective-permute-start | bytes 2924552 | tf_op jit(solution)/shard_map/ppermute | solution.py:778
  337.8 14.7 %collective-permute-start.30 = (bf16[264,1024]{1,0:T(8,128)(2,1)S(1)}, bf16[264,1024]{1,0:T(8,128)(2,1)S(1)}, u32[]{:S(2)}, u32[]{:S(2)}) collective-permute-start(bf16[264,1024]{1,0:T(8,128)(2,1)S(1)} %pad_maximum_fusion.5.refs_0_), channel_id=1, source_target_pairs={{0,4},{4,0},{8,12},{12,8},{16,20},{20,16},{24,28},{28,24},{1,5},{5... | collective-permute-start | bytes 1622024 | tf_op jit(solution)/shard_map/ppermute | solution.py:855
  353.3 16.5 %collective-permute-start.34 = (bf16[288,1024]{1,0:T(8,128)(2,1)}, bf16[288,1024]{1,0:T(8,128)(2,1)S(1)}, u32[]{:S(2)}, u32[]{:S(2)}) collective-permute-start(bf16[288,1024]{1,0:T(8,128)(2,1)} %get-tuple-element.203), channel_id=1, source_target_pairs={{0,4},{4,0},{8,12},{12,8},{16,20},{20,16},{24,28},{28,24},{1,5},{5... | collective-permute-start | bytes 1769480 | tf_op jit(solution)/shard_map/ppermute | solution.py:855
  354.3 15.5 %collective-permute-start.35 = (bf16[264,1024]{1,0:T(8,128)(2,1)S(1)}, bf16[264,1024]{1,0:T(8,128)(2,1)}, u32[]{:S(2)}, u32[]{:S(2)}) collective-permute-start(bf16[264,1024]{1,0:T(8,128)(2,1)S(1)} %pad_maximum_fusion.5.refs_0_), channel_id=1, source_target_pairs={{0,8},{4,12},{8,16},{12,20},{16,24},{20,28},{24,0},{28,4},{1,9},{5... | collective-permute-start | bytes 1622024 | tf_op jit(solution)/shard_map/ppermute | solution.py:855
  382.7 13.7 %collective-permute-start.37 = (bf16[288,1024]{1,0:T(8,128)(2,1)}, bf16[288,1024]{1,0:T(8,128)(2,1)S(1)}, u32[]{:S(2)}, u32[]{:S(2)}) collective-permute-start(bf16[288,1024]{1,0:T(8,128)(2,1)} %get-tuple-element.205), channel_id=1, source_target_pairs={{0,4},{4,0},{8,12},{12,8},{16,20},{20,16},{24,28},{28,24},{1,5},{5... | collective-permute-start | bytes 1769480 | tf_op jit(solution)/shard_map/ppermute | solution.py:855
  403.5 19.8 %collective-permute-start.44 = (bf16[272,896]{1,0:T(8,128)(2,1)S(1)}, bf16[272,896]{1,0:T(8,128)(2,1)S(1)}, u32[]{:S(2)}, u32[]{:S(2)}) collective-permute-start(bf16[272,896]{1,0:T(8,128)(2,1)S(1)} %slice.225), channel_id=1, source_target_pairs={{0,2},{1,3},{2,0},{3,1},{4,6},{5,7},{6,4},{7,5},{8,10},{9,11},{10,... | collective-permute-start | bytes 1462280 | tf_op jit(solution)/shard_map/ppermute | solution.py:778
  408.8 13.5 %collective-permute-start.40 = (bf16[288,1024]{1,0:T(8,128)(2,1)S(1)}, bf16[288,1024]{1,0:T(8,128)(2,1)S(1)}, u32[]{:S(2)}, u32[]{:S(2)}) collective-permute-start(bf16[288,1024]{1,0:T(8,128)(2,1)S(1)} %copy-done.52), channel_id=1, source_target_pairs={{0,4},{4,0},{8,12},{12,8},{16,20},{20,16},{24,28},{28,24},{1,5},{5... | collective-permute-start | bytes 1769480 | tf_op jit(solution)/shard_map/ppermute | solution.py:855
  412.7 24.9 %collective-permute-start.31 = (bf16[512,1024]{1,0:T(8,128)(2,1)}, bf16[512,1024]{1,0:T(8,128)(2,1)}, u32[]{:S(2)}, u32[]{:S(2)}) collective-permute-start(bf16[512,1024]{1,0:T(8,128)(2,1)} %slice.159), channel_id=1, source_target_pairs={{0,1},{1,0},{2,3},{3,2},{4,5},{5,4},{6,7},{7,6},{8,9},{9,8},{10,11... | collective-permute-start | bytes 3145736 | tf_op jit(solution)/shard_map/ppermute | solution.py:778
  414.5 21.2 %collective-permute-start.42 = (bf16[288,1024]{1,0:T(8,128)(2,1)S(1)}, bf16[288,1024]{1,0:T(8,128)(2,1)S(1)}, u32[]{:S(2)}, u32[]{:S(2)}) collective-permute-start(bf16[288,1024]{1,0:T(8,128)(2,1)S(1)} %add_convert_fusion.1), channel_id=1, source_target_pairs={{0,8},{4,12},{8,16},{12,20},{16,24},{20,28},{24,0},{28,4},{1,9},{5... | collective-permute-start | bytes 1769480 | tf_op jit(solution)/shard_map/ppermute | solution.py:855
  425.3 31.6 %collective-permute-start.41 = (bf16[288,1024]{1,0:T(8,128)(2,1)}, bf16[288,1024]{1,0:T(8,128)(2,1)}, u32[]{:S(2)}, u32[]{:S(2)}) collective-permute-start(bf16[288,1024]{1,0:T(8,128)(2,1)} %add_convert_fusion.2), channel_id=1, source_target_pairs={{0,24},{4,28},{8,0},{12,4},{16,8},{20,12},{24,16},{28,20},{1,25},{... | collective-permute-start | bytes 1769480 | tf_op jit(solution)/shard_map/ppermute | solution.py:855
  434.7 21.1 %collective-permute-start.48 = (bf16[272,896]{1,0:T(8,128)(2,1)}, bf16[272,896]{1,0:T(8,128)(2,1)}, u32[]{:S(2)}, u32[]{:S(2)}) collective-permute-start(bf16[272,896]{1,0:T(8,128)(2,1)} %fusion.18.refs_0_), channel_id=1, source_target_pairs={{0,8},{4,12},{8,16},{12,20},{16,24},{20,28},{24,0},{28,4},{1,9},{5... | collective-permute-start | bytes 1462280 | tf_op jit(solution)/shard_map/ppermute | solution.py:855
  434.7 21.1 %collective-permute-start.47 = (bf16[272,896]{1,0:T(8,128)(2,1)}, bf16[272,896]{1,0:T(8,128)(2,1)}, u32[]{:S(2)}, u32[]{:S(2)}) collective-permute-start(bf16[272,896]{1,0:T(8,128)(2,1)} %fusion.18.refs_0_), channel_id=1, source_target_pairs={{0,4},{4,0},{8,12},{12,8},{16,20},{20,16},{24,28},{28,24},{1,5},{5... | collective-permute-start | bytes 1462280 | tf_op jit(solution)/shard_map/ppermute | solution.py:855
  436.8 31.7 %collective-permute-start.43 = (bf16[288,1024]{1,0:T(8,128)(2,1)}, bf16[288,1024]{1,0:T(8,128)(2,1)}, u32[]{:S(2)}, u32[]{:S(2)}) collective-permute-start(bf16[288,1024]{1,0:T(8,128)(2,1)} %add_convert_fusion), channel_id=1, source_target_pairs={{0,8},{4,12},{8,16},{12,20},{16,24},{20,28},{24,0},{28,4},{1,9},{5... | collective-permute-start | bytes 1769480 | tf_op jit(solution)/shard_map/ppermute | solution.py:855
  439.8 40.4 %collective-permute-start.32 = (bf16[256,1024]{1,0:T(8,128)(2,1)S(1)}, bf16[256,1024]{1,0:T(8,128)(2,1)S(1)}, u32[]{:S(2)}, u32[]{:S(2)}) collective-permute-start(bf16[256,1024]{1,0:T(8,128)(2,1)S(1)} %slice.222), channel_id=1, source_target_pairs={{0,2},{1,3},{2,0},{3,1},{4,6},{5,7},{6,4},{7,5},{8,10},{9,11},{10,... | collective-permute-start | bytes 1572872 | tf_op jit(solution)/shard_map/ppermute | solution.py:778
  455.8 22.9 %collective-permute-start.50 = (bf16[272,896]{1,0:T(8,128)(2,1)}, bf16[272,896]{1,0:T(8,128)(2,1)S(1)}, u32[]{:S(2)}, u32[]{:S(2)}) collective-permute-start(bf16[272,896]{1,0:T(8,128)(2,1)} %fusion.18.refs_0_), channel_id=1, source_target_pairs={{0,24},{4,28},{8,0},{12,4},{16,8},{20,12},{24,16},{28,20},{1,25},{... | collective-permute-start | bytes 1462280 | tf_op jit(solution)/shard_map/ppermute | solution.py:855
  455.8 23.3 %collective-permute-start.49 = (bf16[272,896]{1,0:T(8,128)(2,1)}, bf16[272,896]{1,0:T(8,128)(2,1)S(1)}, u32[]{:S(2)}, u32[]{:S(2)}) collective-permute-start(bf16[272,896]{1,0:T(8,128)(2,1)} %collective-permute-done.48.refs_2_), channel_id=1, source_target_pairs={{0,4},{4,0},{8,12},{12,8},{16,20},{20,16},{24,28},{28,24},{1,5},{5... | collective-permute-start | bytes 1462280 | tf_op jit(solution)/shard_map/ppermute | solution.py:855
  470.3 14.4 %collective-permute-start.54 = (bf16[32,1024]{1,0:T(8,128)(2,1)S(1)}, bf16[32,1024]{1,0:T(8,128)(2,1)S(1)}, u32[]{:S(2)}, u32[]{:S(2)}) collective-permute-start(bf16[32,1024]{1,0:T(8,128)(2,1)S(1)} %slice.226.refs_8_), channel_id=1, source_target_pairs={{0,4},{4,0},{8,12},{12,8},{16,20},{20,16},{24,28},{28,24},{1,5},{5... | collective-permute-start | bytes 196616 | tf_op jit(solution)/shard_map/ppermute | solution.py:855
  478.7 18.2 %collective-permute-start.52 = (bf16[272,896]{1,0:T(8,128)(2,1)}, bf16[272,896]{1,0:T(8,128)(2,1)S(1)}, u32[]{:S(2)}, u32[]{:S(2)}) collective-permute-start(bf16[272,896]{1,0:T(8,128)(2,1)} %collective-permute-done.48.refs_2_), channel_id=1, source_target_pairs={{0,8},{4,12},{8,16},{12,20},{16,24},{20,28},{24,0},{28,4},{1,9},{5... | collective-permute-start | bytes 1462280 | tf_op jit(solution)/shard_map/ppermute | solution.py:855
  479.1 17.8 %collective-permute-start.51 = (bf16[272,896]{1,0:T(8,128)(2,1)S(1)}, bf16[272,896]{1,0:T(8,128)(2,1)S(1)}, u32[]{:S(2)}, u32[]{:S(2)}) collective-permute-start(bf16[272,896]{1,0:T(8,128)(2,1)S(1)} %collective-permute-done.50.refs_4_), channel_id=1, source_target_pairs={{0,4},{4,0},{8,12},{12,8},{16,20},{20,16},{24,28},{28,24},{1,5},{5... | collective-permute-start | bytes 1462280 | tf_op jit(solution)/shard_map/ppermute | solution.py:855
  481.2 14.6 %collective-permute-start.57 = (bf16[32,1024]{1,0:T(8,128)(2,1)S(1)}, bf16[32,1024]{1,0:T(8,128)(2,1)S(1)}, u32[]{:S(2)}, u32[]{:S(2)}) collective-permute-start(bf16[32,1024]{1,0:T(8,128)(2,1)S(1)} %slice.226.refs_8_), channel_id=1, source_target_pairs={{0,24},{4,28},{8,0},{12,4},{16,8},{20,12},{24,16},{28,20},{1,25},{... | collective-permute-start | bytes 196616 | tf_op jit(solution)/shard_map/ppermute | solution.py:855
  496.9 14.9 %collective-permute-start.53 = (bf16[272,896]{1,0:T(8,128)(2,1)S(1)}, bf16[272,896]{1,0:T(8,128)(2,1)S(1)}, u32[]{:S(2)}, u32[]{:S(2)}) collective-permute-start(bf16[272,896]{1,0:T(8,128)(2,1)S(1)} %collective-permute-done.52.refs_6_), channel_id=1, source_target_pairs={{0,4},{4,0},{8,12},{12,8},{16,20},{20,16},{24,28},{28,24},{1,5},{5... | collective-permute-start | bytes 1462280 | tf_op jit(solution)/shard_map/ppermute | solution.py:855
  (77 other events, 1089.5 us)
